TPU v7x, 32 devices: a whole 2x2x4 slice. The times are simulated.
32 devices in a mesh: section: 8 (over y, x, core), tensor: 4 (over z).
Axes of the slice: x: 2, y: 2, z: 4, core: 2. Of those that a mesh axis runs over, the one named last changes fastest.
Arguments:
- frozen: bfloat16 [8, 14336, 2048], P('section', 'tensor'), may hold values from -1 to 1, as said below
- adapter_a: bfloat16 [8, 8, 14336], P('section', None, 'tensor'), may hold values from -0.119628906 to 0.119628906
- adapter_b: bfloat16 [8, 16, 2048], P('section'), may hold values from -0.22460938 to 0.22460938
- magnitude: float32 [8, 2048], P('section'), may hold values from 0.5 to 2
- hidden_fwd: bfloat16 [8, 128, 14336], P('section', None, 'tensor'), may hold values from -6 to 6
- carried: bfloat16 [8, 256, 2048], P('section', 'tensor'), may hold values from -6 to 6
- embedded: bfloat16 [256, 4096], P('tensor'), may hold values from -6 to 6
- hidden_bwd: bfloat16 [8, 128, 14336], P('section', None, 'tensor'), may hold values from -6 to 6
- returned: bfloat16 [8, 256, 2048], P('section', 'tensor'), may hold values from -1.5 to 1.5
- head_grad: bfloat16 [256, 4096], P('tensor'), may hold values from -1.5 to 1.5
Outputs:
- section_out: bfloat16 [8, 256, 2048], P('section', 'tensor')
- grad_magnitude: float32 [8, 2048], P('section')
- grad_a: float32 [8, 8, 14336], P('section', None, 'tensor')
- grad_b: float32 [8, 16, 2048], P('section')
- hidden_grad: bfloat16 [8, 128, 14336], P('section', None, 'tensor')
Inputs may be any that keep to these rules, and one draw needn't show every extreme that they name: frozen projection weights.
All inputs are finite; a program needn't handle non-finite values.
Results may differ from a plain program's by a relative error of at most 0.0057.
Values may be sent and summed in bfloat16 or wider, within the bound.
No kernel may reach another device: no remote copies, remote signals or barrier semaphores. Data moves between devices by JAX's collectives and lax.ppermute only.
A program may use at most 128 MiB of HBM per device.

v0:
```python
import jax
import jax.numpy as jnp
from jax import lax
from jax.sharding import PartitionSpec as P

epsilon = 1e-06


def swapped(array, axis, apart):
    return lax.ppermute(array, axis, [(i, i ^ 1 << apart) for i in range(lax.axis_size(axis))])


def from_behind(array, axis, by):
    count = lax.axis_size(axis)
    pairs = [(i, i + by) for i in range(count) if 0 <= i + by < count]
    return lax.ppermute(array, axis, pairs)


def column_norms(squares):
    return jnp.sqrt(lax.psum(squares, "tensor") + epsilon)


def forward_rows(term_fn, own_rows):
    return lax.psum_scatter(
        term_fn(jnp.int32(0), own_rows * lax.axis_size("tensor")),
        "tensor",
        scatter_dimension=0,
        tiled=True,
    )


def local(
    frozen,
    adapter_a,
    adapter_b,
    magnitude,
    hidden_fwd,
    carried,
    embedded,
    hidden_bwd,
    returned,
    head_grad,
):
    base_w = frozen[0]
    fac_half = adapter_a[0]
    fac_b = adapter_b[0]
    mag = magnitude[0]
    own_rows = carried.shape[1]
    slot_id = lax.axis_index("section")
    slot_count = lax.axis_size("section")
    half = slot_id % 2
    first_half = half == 0
    fwd_other, bwd_other, fac_other = swapped(
        (hidden_fwd[0], hidden_bwd[0], fac_half), "section", 0
    )

    def in_order(own, other):
        return jnp.concatenate(
            [jnp.where(first_half, own, other), jnp.where(first_half, other, own)], axis=0
        )

    hid_fwd = in_order(hidden_fwd[0], fwd_other)
    hid_bwd = in_order(hidden_bwd[0], bwd_other)
    fac_a = in_order(fac_half, fac_other)
    width = base_w.shape[1]
    arriving = from_behind(carried[0], "section", 2)
    embed_cols = lax.dynamic_slice_in_dim(embedded, half * width, width, 1)
    inflow = jnp.where(slot_id < 2, embed_cols, arriving)
    coming = from_behind(returned[0], "section", -2)
    head_cols = lax.dynamic_slice_in_dim(head_grad, half * width, width, 1)
    cotangent = jnp.where(slot_id >= slot_count - 2, head_cols, coming)
    merged = (
        base_w.astype(jnp.float32)
        + jnp.einsum("rf,rd->fd", fac_a, fac_b, preferred_element_type=jnp.float32)
    ).astype(jnp.bfloat16)
    merged_f = merged.astype(jnp.float32)
    squares = jnp.sum(merged_f * merged_f, axis=0)
    low_part = jnp.einsum("tf,rf->tr", hid_bwd, fac_a, preferred_element_type=jnp.float32)
    low = lax.psum(low_part, "tensor").astype(jnp.bfloat16)
    col_norms = column_norms(squares)
    col_scale = mag / col_norms

    def scaled_term(offset, amount):
        return jnp.dot(hid_fwd, merged, preferred_element_type=jnp.float32) * col_scale

    projected = forward_rows(scaled_term, own_rows)
    section_out = (inflow.astype(jnp.float32) + projected).astype(jnp.bfloat16)
    all_rows = hid_bwd.shape[0]
    cot_block = lax.all_gather(cotangent, "tensor", axis=0, tiled=True)
    scaled_cot = (cot_block.astype(jnp.float32) * col_scale).astype(jnp.bfloat16)
    hid_part = jnp.einsum("td,fd->tf", scaled_cot, merged, preferred_element_type=jnp.float32)
    hid_acc = hid_part
    adapt_part = jnp.einsum("td,rd->tr", scaled_cot, fac_b, preferred_element_type=jnp.float32)
    adapt_acc = adapt_part
    grad_b_acc = jnp.einsum("tr,td->rd", low, scaled_cot, preferred_element_type=jnp.float32)
    recomputed = jnp.dot(hid_bwd, merged, preferred_element_type=jnp.float32)
    mag_acc = jnp.sum(cot_block.astype(jnp.float32) * recomputed, axis=0)
    hid_acc, adapt_acc, grad_b_acc, mag_acc = (hid_acc, adapt_acc, grad_b_acc, mag_acc)
    half_rows = all_rows // 2
    send_hid = lax.dynamic_slice_in_dim(hid_acc, (1 - half) * half_rows, half_rows, 0)
    got_hid, got_adapt = swapped((send_hid, adapt_acc), "section", 0)
    own_hid = lax.dynamic_slice_in_dim(hid_acc, half * half_rows, half_rows, 0)
    hidden_grad = (own_hid + got_hid).astype(jnp.bfloat16)
    adapter_cot = (adapt_acc + got_adapt).astype(jnp.bfloat16)
    rank_half = fac_half.shape[0]
    own_cot = lax.dynamic_slice_in_dim(adapter_cot, half * rank_half, rank_half, 1)
    grad_a = jnp.einsum("tr,tf->rf", own_cot, hid_bwd, preferred_element_type=jnp.float32)
    grad_mag = lax.psum(mag_acc, "tensor") / col_norms
    return (section_out[None], grad_mag[None], grad_a[None], grad_b_acc[None], hidden_grad[None])


def solution(mesh):
    placed = (
        P("section", "tensor", None),
        P("section", None, "tensor"),
        P("section", None, None),
        P("section", None),
        P("section", None, "tensor"),
        P("section", "tensor", None),
        P("tensor", None),
        P("section", None, "tensor"),
        P("section", "tensor", None),
        P("tensor", None),
    )
    return jax.shard_map(
        local,
        mesh=mesh,
        in_specs=placed,
        out_specs=(
            P("section", "tensor", None),
            P("section", None),
            P("section", None, "tensor"),
            P("section", None, None),
            P("section", None, "tensor"),
        ),
        check_vma=False,
    )
```

profile of v0, /device:TPU:0, one launch (start us, length us, event | category | flops | bytes accessed | tf_op | source)
XLA Modules:
  0.0 143.7 jit_solution(12849420476507222453)
XLA Ops:
  7.2 0.0 copy-start
  7.2 0.0 all-gather.2.cloned.1.call-start
  7.2 0.6 collective-permute-start.2
  7.8 0.1 collective-permute-start.1
  7.9 1.3 collective-permute-start.3
  9.2 0.5 collective-permute-start.4
  9.6 0.0 collective-permute-done.2
  9.7 0.8 broadcast_select_fusion.5
  10.5 0.0 copy-done
  10.5 0.0 copy-start.10
  10.5 0.0 copy-start.4
  10.5 11.0 %multiply_reduce_fusion = (f32[2048]{0:T(1024)S(1)}, bf16[3584,2048]{1,0:T(8,128)(2,1)}) fusion(bf16[1,16,2048]{2,1,0:T(8,128)(2,1)S(1)} %copy-done, bf16[8,3584]{1,0:T(8,128)(2,1)S(1)} %get-tuple-element.13, bf16[8,3584]{1,0:T(8,128)(2,1)S(1)} %get-tuple-element.12, bf16[1,3584,2048]{2,1,0:T(8,128)(2,1)} %param.10), kind=kOutput, calls=%fused_computation.2 | convolution fusion | flops 279148544 | bytes 29548544 | tf_op jit(solution)/shard_map/rf,rd->fd/dot_general | solution.py:74
  21.5 0.0 collective-permute-done.3
  21.5 0.0 copy-done.10
  21.5 0.8 dynamic-slice_select_fusion
  22.3 0.0 all-gather.2.cloned.1.call-update
  22.3 0.0 reduce-scatter.2.cloned.1.call-start
  22.3 0.0 collective-permute-done.4
  22.3 0.0 copy-done.4
  22.4 1.3 broadcast_select_fusion.1
  23.7 0.0 copy-start.8
  23.7 0.0 copy-start.6
  23.7 0.0 copy-start.5
  23.7 0.6 fusion.12
  24.3 0.0 collective-permute-done.1
  24.3 0.3 copy-done.8
  24.6 0.9 copy-done.5
  25.5 1.0 broadcast_select_fusion.3
  26.6 27.4 %all-gather.2.cloned.1.call-done = bf16[256,2048]{1,0:T(8,128)(2,1)} async-done(((bf16[64,2048]{1,0:T(8,128)(2,1)}), bf16[256,2048]{1,0:T(8,128)(2,1)}) %all-gather.2.cloned.1.call-update) | async-done | bytes 1048592 | tf_op jit(solution)/shard_map/all_gather | solution.py:89
  54.0 0.0 copy-done.6
  54.0 0.0 copy-start.12
  54.0 0.0 copy-start.9
  54.0 9.7 %fusion.5 = f32[2048]{0:T(1024)S(1)} fusion(bf16[3584,2048]{1,0:T(8,128)(2,1)} %get-tuple-element.17, bf16[256,2048]{1,0:T(8,128)(2,1)} %all-gather.2.cloned.1.call-done, bf16[128,3584]{1,0:T(8,128)(2,1)} %copy-done.8, bf16[128,3584]{1,0:T(8,128)(2,1)S(1)} %get-tuple-element.8), kind=kOutput, calls=%fused_computation.14 | convolution fusion | flops 3763337216 | bytes 17571840 | tf_op jit(solution)/shard_map/dot_general | solution.py:96
  63.7 19.6 %all-reduce = (f32[2048]{0:T(1024)S(1)}, f32[2048]{0:T(1024)S(1)}, bf16[256,16]{1,0:T(8,128)(2,1)S(1)}) all-reduce(f32[2048]{0:T(1024)S(1)} %get-tuple-element.16, f32[2048]{0:T(1024)S(1)} %fusion.5, f32[256,16]{1,0:T(8,128)S(1)} %fusion.12), channel_id=1, replica_groups=mesh['section'=8,'tensor'=4] {'tensor'}, use_global_device_ids=true, to_apply=%region_1.2 | all-reduce | flops 8192 | bytes 57344 | tf_op jit(solution)/shard_map/psum | solution.py:20
  83.3 0.0 copy-done.12
  83.3 0.6 fusion.18
  83.9 0.0 copy-done.9
  83.9 8.9 %convolution_multiply_fusion.1 = f32[256,2048]{1,0:T(8,128)} fusion(bf16[3584,2048]{1,0:T(8,128)(2,1)} %get-tuple-element.17, bf16[128,3584]{1,0:T(8,128)(2,1)S(1)} %copy-done.9, bf16[128,3584]{1,0:T(8,128)(2,1)S(1)} %get-tuple-element.10, f32[2048]{0:T(1024)S(1)} %get-tuple-element.15), kind=kOutput, calls=%fused_computation.5 | convolution fusion | flops 3762290688 | bytes 18620416 | tf_op jit(solution)/shard_map/dot_general | solution.py:84
  92.9 0.0 copy-start.3
  92.9 0.0 reduce-scatter.2.cloned.1.call-update
  92.9 1.2 copy-done.3
  94.1 7.7 %fusion.7 = f32[256,3584]{1,0:T(8,128)S(1)} fusion(bf16[3584,2048]{1,0:T(8,128)(2,1)} %get-tuple-element.17, bf16[256,2048]{1,0:T(8,128)(2,1)S(1)} %copy-done.3, f32[2048]{0:T(1024)S(1)} %get-tuple-element.15), kind=kOutput, calls=%fused_computation.20 | convolution fusion | flops 3759669248 | bytes 19406848 | tf_op jit(solution)/shard_map/td,fd->tf/dot_general | solution.py:91
  101.8 0.0 copy-start.1
  101.8 1.8 %copy-done.1 = f32[256,3584]{1,0:T(8,128)} copy-done((f32[256,3584]{1,0:T(8,128)}, f32[256,3584]{1,0:T(8,128)S(1)}, u32[]{:S(2)}) %copy-start.1) | copy-done | bytes 3670040
  103.6 0.0 copy-start.13
  103.6 1.4 constant_dynamic-slice_fusion
  104.9 0.0 collective-permute-start.6
  105.0 0.0 copy-done.13
  105.0 3.4 %collective-permute-start = (bf16[64,2048]{1,0:T(8,128)(2,1)S(1)}, bf16[64,2048]{1,0:T(8,128)(2,1)S(1)}, u32[]{:S(2)}, u32[]{:S(2)}) collective-permute-start(bf16[64,2048]{1,0:T(8,128)(2,1)S(1)} %bitcast.41), channel_id=1, source_target_pairs={{0,8},{4,12},{8,16},{12,20},{16,24},{20,28},{1,9},{5,13},{9,17},{1... | collective-permute-start | bytes 786440 | tf_op jit(solution)/shard_map/ppermute | solution.py:16
  108.4 0.0 copy-start.7
  108.4 0.4 fusion.10
  108.7 0.0 copy-start.2
  108.7 0.2 collective-permute-start.5
  109.0 0.9 convolution_bitcast_fusion.1
  109.9 0.0 collective-permute-done.5
  109.9 0.0 copy-done.7
  109.9 2.2 %convolution_bitcast_fusion = f32[1,8,3584]{2,1,0:T(8,128)} fusion(bf16[128,3584]{1,0:T(8,128)(2,1)} %copy-done.8, bf16[128,3584]{1,0:T(8,128)(2,1)S(1)} %copy-done.7, f32[256,16]{0,1:T(8,128)S(1)} %collective-permute-done.5, s32[]{:T(128)S(6)} %select_n.80, f32[256,16]{0,1:T(8,128)S(1)} %fusion.10), kind=kOutput, calls=%fused_computation.3 | convolution fusion | flops 18354176 | bytes 1966084 | tf_op jit(solution)/shard_map/tr,tf->rf/dot_general | solution.py:107
  112.1 0.0 collective-permute-done.6
  112.2 0.0 copy-done.2
  112.2 1.2 fusion.6
  113.3 1.2 collective-permute-done
  114.5 20.4 %reduce-scatter.2.cloned.1.call-done = f32[64,2048]{1,0:T(8,128)} async-done(((f32[256,2048]{1,0:T(8,128)}), f32[64,2048]{1,0:T(8,128)}) %reduce-scatter.2.cloned.1.call-update) | async-done | bytes 524304 | tf_op jit(solution)/shard_map/reduce_scatter | solution.py:24
  135.0 0.0 copy-done.11
  135.0 1.8 %fusion.13 = bf16[1,64,2048]{2,1,0:T(8,128)(2,1)} fusion(f32[64,2048]{1,0:T(8,128)} %reduce-scatter.2.cloned.1.call-done, bf16[64,2048]{1,0:T(8,128)(2,1)S(1)} %collective-permute-done, bf16[64,4096]{1,0:T(8,128)(2,1)S(1)} %copy-done.11, s32[]{:T(128)S(6)} %select_n.68, pred[]{:T(512)S(6)} %lt.22), kind=kLoop, calls=%fused_computation.24 | loop fusion | flops 524288 | bytes 1310725 | tf_op jit(solution)/shard_map/broadcast_in_dim | solution.py:109
  (1 shorter events, 0.0 us)
Async XLA Ops:
  7.2 3.3 %copy-start = (bf16[1,16,2048]{2,1,0:T(8,128)(2,1)S(1)}, bf16[1,16,2048]{2,1,0:T(8,128)(2,1)}, u32[]{:S(2)}) copy-start(bf16[1,16,2048]{2,1,0:T(8,128)(2,1)} %param.12) | copy-start | bytes 196612
  7.2 46.8 %all-gather.2.cloned.1.call-start = ((), (), s32[]{:S(2)}) async-start(), calls=%async_computation.2 | async-start | bytes 1310720 | tf_op jit(solution)/shard_map/all_gather | solution.py:89
  7.2 2.4 %collective-permute-start.2 = (bf16[8,3584]{1,0:T(8,128)(2,1)}, bf16[8,3584]{1,0:T(8,128)(2,1)S(1)}, u32[]{:S(2)}, u32[]{:S(2)}) collective-permute-start(bf16[8,3584]{1,0:T(8,128)(2,1)} %bitcast.37), channel_id=1, source_target_pairs={{0,4},{4,0},{8,12},{12,8},{16,20},{20,16},{24,28},{28,24},{1,5},{5... | collective-permute-start | bytes 172040 | tf_op jit(solution)/shard_map/ppermute | solution.py:10
  7.8 16.5 %collective-permute-start.1 = (bf16[128,3584]{1,0:T(8,128)(2,1)}, bf16[128,3584]{1,0:T(8,128)(2,1)S(1)}, u32[]{:S(2)}, u32[]{:S(2)}) collective-permute-start(bf16[128,3584]{1,0:T(8,128)(2,1)} %bitcast.36), channel_id=1, source_target_pairs={{0,4},{4,0},{8,12},{12,8},{16,20},{20,16},{24,28},{28,24},{1,5},{5... | collective-permute-start | bytes 2752520 | tf_op jit(solution)/shard_map/ppermute | solution.py:10
  7.9 13.6 %collective-permute-start.3 = (bf16[64,2048]{1,0:T(8,128)(2,1)}, bf16[64,2048]{1,0:T(8,128)(2,1)S(1)}, u32[]{:S(2)}, u32[]{:S(2)}) collective-permute-start(bf16[64,2048]{1,0:T(8,128)(2,1)} %bitcast.40), channel_id=1, source_target_pairs={{8,0},{12,4},{16,8},{20,12},{24,16},{28,20},{9,1},{13,5},{17,9},{2... | collective-permute-start | bytes 786440 | tf_op jit(solution)/shard_map/ppermute | solution.py:16
  9.2 13.2 %collective-permute-start.4 = (bf16[128,3584]{1,0:T(8,128)(2,1)}, bf16[128,3584]{1,0:T(8,128)(2,1)}, u32[]{:S(2)}, u32[]{:S(2)}) collective-permute-start(bf16[128,3584]{1,0:T(8,128)(2,1)} %bitcast.35), channel_id=1, source_target_pairs={{0,4},{4,0},{8,12},{12,8},{16,20},{20,16},{24,28},{28,24},{1,5},{5... | collective-permute-start | bytes 2752520 | tf_op jit(solution)/shard_map/ppermute | solution.py:10
  10.5 11.0 %copy-start.10 = (bf16[64,4096]{1,0:T(8,128)(2,1)S(1)}, bf16[64,4096]{1,0:T(8,128)(2,1)}, u32[]{:S(2)}) copy-start(bf16[64,4096]{1,0:T(8,128)(2,1)} %param.19) | copy-start | bytes 1572868
  10.5 11.8 %copy-start.4 = (bf16[1,128,3584]{2,1,0:T(8,128)(2,1)S(1)}, bf16[1,128,3584]{2,1,0:T(8,128)(2,1)}, u32[]{:S(2)}) copy-start(bf16[1,128,3584]{2,1,0:T(8,128)(2,1)} %param.17) | copy-start | bytes 2752516
  22.3 112.7 %reduce-scatter.2.cloned.1.call-start = ((), (), s32[]{:S(2)}) async-start(), calls=%async_computation.1 | async-start | bytes 2621440 | tf_op jit(solution)/shard_map/reduce_scatter | solution.py:24
  23.7 0.9 copy-start.8
  23.7 30.3 %copy-start.6 = (bf16[128,3584]{1,0:T(8,128)(2,1)}, bf16[128,3584]{1,0:T(8,128)(2,1)S(1)}, u32[]{:S(2)}) copy-start(bf16[128,3584]{1,0:T(8,128)(2,1)S(1)} %get-tuple-element.8) | copy-start | bytes 2752516
  23.7 1.8 %copy-start.5 = (bf16[1,128,3584]{2,1,0:T(8,128)(2,1)S(1)}, bf16[1,128,3584]{2,1,0:T(8,128)(2,1)}, u32[]{:S(2)}) copy-start(bf16[1,128,3584]{2,1,0:T(8,128)(2,1)} %param.14) | copy-start | bytes 2752516
  54.0 29.3 %copy-start.12 = (f32[1,2048]{1,0:T(1,128)S(1)}, f32[1,2048]{1,0:T(1,128)}, u32[]{:S(2)}) copy-start(f32[1,2048]{1,0:T(1,128)} %param.13) | copy-start | bytes 24580
  54.0 30.0 %copy-start.9 = (bf16[128,3584]{1,0:T(8,128)(2,1)S(1)}, bf16[128,3584]{1,0:T(8,128)(2,1)}, u32[]{:S(2)}) copy-start(bf16[128,3584]{1,0:T(8,128)(2,1)} %get-tuple-element.11) | copy-start | bytes 2752516
  92.9 1.2 copy-start.3
  101.8 1.8 %copy-start.1 = (f32[256,3584]{1,0:T(8,128)}, f32[256,3584]{1,0:T(8,128)S(1)}, u32[]{:S(2)}) copy-start(f32[256,3584]{1,0:T(8,128)S(1)} %fusion.7) | copy-start | bytes 11010052
  103.6 1.4 copy-start.13
  104.9 7.2 %collective-permute-start.6 = (f32[128,3584]{1,0:T(8,128)}, f32[128,3584]{1,0:T(8,128)S(1)}, u32[]{:S(2)}, u32[]{:S(2)}) collective-permute-start(f32[128,3584]{1,0:T(8,128)} %constant_dynamic-slice_fusion), channel_id=1, source_target_pairs={{0,4},{4,0},{8,12},{12,8},{16,20},{20,16},{24,28},{28,24},{1,5},{5... | collective-permute-start | bytes 5505032 | tf_op jit(solution)/shard_map/ppermute | solution.py:10
  105.0 9.6 %collective-permute-start = (bf16[64,2048]{1,0:T(8,128)(2,1)S(1)}, bf16[64,2048]{1,0:T(8,128)(2,1)S(1)}, u32[]{:S(2)}, u32[]{:S(2)}) collective-permute-start(bf16[64,2048]{1,0:T(8,128)(2,1)S(1)} %bitcast.41), channel_id=1, source_target_pairs={{0,8},{4,12},{8,16},{12,20},{16,24},{20,28},{1,9},{5,13},{9,17},{1... | collective-permute-start | bytes 786440 | tf_op jit(solution)/shard_map/ppermute | solution.py:16
  108.4 1.6 %copy-start.7 = (bf16[128,3584]{1,0:T(8,128)(2,1)S(1)}, bf16[128,3584]{1,0:T(8,128)(2,1)}, u32[]{:S(2)}) copy-start(bf16[128,3584]{1,0:T(8,128)(2,1)} %copy-done.6) | copy-start | bytes 2752516
  108.7 3.4 %copy-start.2 = (f32[256,3584]{1,0:T(8,128)S(1)}, f32[256,3584]{1,0:T(8,128)}, u32[]{:S(2)}) copy-start(f32[256,3584]{1,0:T(8,128)} %copy-done.1) | copy-start | bytes 11010052
  108.7 1.2 collective-permute-start.5
  112.1 22.8 %copy-start.11 = (bf16[64,4096]{1,0:T(8,128)(2,1)S(1)}, bf16[64,4096]{1,0:T(8,128)(2,1)}, u32[]{:S(2)}) copy-start(bf16[64,4096]{1,0:T(8,128)(2,1)} %param.16) | copy-start | bytes 1572868
Sparse Core Ops, SparseCore 0:
  22.4 31.5 all-gather.1
  93.0 41.9 reduce-scatter.1
where the time goes:
time: 144 us
  waiting for transfers between devices  49.1 us (34%)
  matrix products  41.4 us (29%)
  blocking collectives  19.6 us (14%)
  between operations  14.2 us (10%)
  other arithmetic  7.57 us (5%)
  starting transfers between devices  6.09 us (4%)
  local copies, waits for them, and re-layouts  5.62 us (4%)
    all_gather x1, waiting for transfers between devices, local(): cot_block = lax.all_gather(cotangent, 'tensor', axis=0, tiled=True)  27.4 us
    reduce_scatter x1, waiting for transfers between devices, forward_rows(): lax.psum_scatter(term_fn(jnp.int32(0), own_rows * lax.axis_size('tensor')...  20.4 us
    psum x1, blocking collectives, column_norms(): return jnp.sqrt(lax.psum(squares, 'tensor') + epsilon)  19.6 us
    dot_general x1, matrix products, local(): jnp.einsum('rf,rd->fd', fac_a, fac_b, preferred_element_type=jnp.float32)  11 us
    dot_general x1, matrix products, local(): recomputed = jnp.dot(hid_bwd, merged, preferred_element_type=jnp.float32)  9.7 us
    dot_general x1, matrix products, scaled_term(): jnp.dot(hid_fwd, merged, preferred_element_type=jnp.float32) * col_scale  8.91 us
    dot_general x1, matrix products, local(): jnp.einsum('td,fd->tf', scaled_cot, merged, preferred_element_type=jnp.fl...  7.7 us
    ppermute x2, starting transfers between devices, from_behind(): return lax.ppermute(array, axis, pairs)  4.65 us
  transfers between devices with their start and end apart: 9, of which 3 were waited for; matrix products, arithmetic and copies ran while one was open for 20% of the time, Pallas kernels for 0%

commit v1 on v0

v1 whole, which is shorter than its diff:
```python
import functools

import jax
import jax.numpy as jnp
from jax import lax
from jax.experimental import pallas as pl
from jax.experimental.pallas import tpu as pltpu
from jax.sharding import PartitionSpec as P

epsilon = 1e-06
f32 = jnp.float32
bf16 = jnp.bfloat16
NT = (((1,), (1,)), ((), ()))
TN = (((0,), (0,)), ((), ()))


def block_of(size, most):
    return max(b for b in range(128, most + 1, 128) if size % b == 0)


def dot(a, b, dims=(((1,), (0,)), ((), ()))):
    return lax.dot_general(a, b, dims, preferred_element_type=f32)


def two_parts(value):
    high = value.astype(bf16)
    low = (value - high.astype(f32)).astype(bf16)
    return jnp.concatenate([high, low], axis=1)


def halves(own, other, half):
    own, other = own.astype(f32), other.astype(f32)
    first = jnp.where(half == 0, own, other)
    second = jnp.where(half == 0, other, own)
    return jnp.concatenate([first, second], axis=0).astype(bf16)


def place_of(shard, half, count):
    return jnp.bitwise_xor(shard, half * (count // 2))


def forward_kernel(
    count, rows, xo, xt, yo, yt, ao, at, b, w, *refs
):
    outs, pack = refs[:count], refs[count]
    xs, lx, gram, res = refs[count + 1 :]
    half = lax.axis_index("section") % 2
    me = lax.axis_index("tensor")
    step = pl.program_id(0)
    tokens = 2 * xo.shape[0]
    rank = b.shape[0]
    lines = pack.shape[0] - rank

    @pl.when(step == 0)
    def _():
        fac = halves(ao[...], at[...], half)
        xs[: tokens // 2, :] = xo[...]
        xs[tokens // 2 : tokens, :] = xt[...]
        xs[tokens:, :] = fac
        lx[...] = two_parts(dot(xs[:tokens, :], fac, NT))
        gram[...] = two_parts(dot(fac, fac, NT))
        low = jnp.concatenate([dot(yo[...], fac, NT), dot(yt[...], fac, NT)], axis=0)
        pack[lines:, :] = low.T

    wv = w[...]
    both_b = jnp.concatenate([b[...], b[...]], axis=0)
    total = dot(xs[...], wv)
    res[...] = total[:tokens] + dot(lx[...], both_b)
    wf = wv.astype(f32)
    squares = jnp.sum((wf * wf).reshape(wf.shape[0] // 8, 8, wf.shape[1]), axis=0)
    cross = 2.0 * total[tokens:] + dot(gram[...], both_b)
    cross = b[...].astype(f32) * cross
    for r in range(0, rank, 8):
        squares = squares + cross[r : r + 8]
    squares = jnp.sum(squares, axis=0, keepdims=True)
    across = pack.shape[1]
    many = wv.shape[1] // across
    for i in range(many):
        pack[pl.ds(step * many + i, 1), :] = squares[:, i * across : (i + 1) * across]
    for k in range(count):
        at_row = place_of(jnp.bitwise_xor(me, k), half, count) * rows
        piece = res[pl.ds(pl.multiple_of(at_row, rows), rows), :]
        outs[k][...] = piece.astype(outs[k].dtype)


def forward(count, rows, xo, xt, yo, yt, ao, at, b, w):
    ff, width = w.shape
    tokens = 2 * xo.shape[0]
    rank = b.shape[0]
    nb = block_of(width, 512)
    whole = lambda a: pl.BlockSpec(a.shape, lambda j: (0, 0))
    lines = width // tokens
    shapes = [jax.ShapeDtypeStruct((rows, width), f32 if k == 0 else bf16) for k in range(count)]
    return pl.pallas_call(
        functools.partial(forward_kernel, count, rows),
        grid=(width // nb,),
        in_specs=[whole(a) for a in (xo, xt, yo, yt, ao, at)]
        + [pl.BlockSpec((rank, nb), lambda j: (0, j)), pl.BlockSpec((ff, nb), lambda j: (0, j))],
        out_specs=[pl.BlockSpec((rows, nb), lambda j: (0, j)) for _ in range(count)]
        + [pl.BlockSpec((lines + rank, tokens), lambda j: (0, 0))],
        out_shape=shapes + [jax.ShapeDtypeStruct((lines + rank, tokens), f32)],
        scratch_shapes=[
            pltpu.VMEM((tokens + rank, ff), bf16),
            pltpu.VMEM((tokens, 2 * rank), bf16),
            pltpu.VMEM((rank, 2 * rank), bf16),
            pltpu.VMEM((tokens, nb), f32),
        ],
        name="forward",
        cost_estimate=pl.CostEstimate(
            flops=2 * tokens * ff * width, bytes_accessed=2 * ff * width, transcendentals=0
        ),
    )(xo, xt, yo, yt, ao, at, b, w)


def again_kernel(yo, yt, pack, b, w, out, ys, ly):
    half_tokens = yo.shape[0]
    rank = b.shape[0]

    @pl.when(pl.program_id(0) == 0)
    def _():
        ys[:half_tokens, :] = yo[...]
        ys[half_tokens:, :] = yt[...]
        ly[...] = two_parts(pack[pack.shape[0] - rank :, :].T)

    both_b = jnp.concatenate([b[...], b[...]], axis=0)
    out[...] = dot(ys[...], w[...]) + dot(ly[...], both_b)


def again(yo, yt, pack, b, w):
    ff, width = w.shape
    tokens = 2 * yo.shape[0]
    rank = b.shape[0]
    nb = block_of(width, 512)
    whole = lambda a: pl.BlockSpec(a.shape, lambda j: (0, 0))
    return pl.pallas_call(
        again_kernel,
        grid=(width // nb,),
        in_specs=[whole(a) for a in (yo, yt, pack)]
        + [pl.BlockSpec((rank, nb), lambda j: (0, j)), pl.BlockSpec((ff, nb), lambda j: (0, j))],
        out_specs=pl.BlockSpec((tokens, nb), lambda j: (0, j)),
        out_shape=jax.ShapeDtypeStruct((tokens, width), f32),
        scratch_shapes=[pltpu.VMEM((tokens, ff), bf16), pltpu.VMEM((tokens, 2 * rank), bf16)],
        name="again",
        cost_estimate=pl.CostEstimate(
            flops=2 * tokens * ff * width, bytes_accessed=2 * ff * width, transcendentals=0
        ),
    )(yo, yt, pack, b, w)


def backward_kernel(count, rows, *refs):
    cots, packs = refs[:count], refs[count : 2 * count]
    mag, r, b, ao, at, w = refs[2 * count : 2 * count + 6]
    own, send, adapt, gb, magpack, norms = refs[2 * count + 6 : 2 * count + 12]
    sc, ad = refs[2 * count + 12 :]
    half = lax.axis_index("section") % 2
    me = lax.axis_index("tensor")
    rank = b.shape[0]
    tokens, width = sc.shape

    @pl.when(pl.program_id(0) == 0)
    def _():
        total = packs[0][...]
        for k in range(1, count):
            total = total + packs[k][...]
        lines = total.shape[0] - rank
        across = total.shape[1]
        sqr = jnp.sqrt(jnp.maximum(total[:lines], 0.0) + epsilon)
        for i in range(lines):
            norms[0:1, i * across : (i + 1) * across] = sqr[i : i + 1, :]
        scale = mag[...] / norms[0:1, :]
        norms[1:2, :] = scale
        mags = jnp.zeros((8, width), f32)
        for k in range(count):
            at_row = place_of(jnp.bitwise_xor(me, k), half, count) * rows
            spot = pl.ds(pl.multiple_of(at_row, rows), rows)
            cot = cots[k][...].astype(f32)
            sc[spot, :] = (cot * scale).astype(bf16)
            mags = mags + jnp.sum((cot * r[spot, :]).reshape(rows // 8, 8, width), axis=0)
        mags = jnp.sum(mags, axis=0, keepdims=True)
        for i in range(lines):
            magpack[i : i + 1, :] = mags[:, i * across : (i + 1) * across]
        part = dot(sc[...], b[...], NT)
        adapt[...] = part
        ad[...] = two_parts(part)
        low = total[lines:].astype(bf16)
        gb[...] = dot(low, sc[...])

    fac = halves(ao[...], at[...], half)
    both_a = jnp.concatenate([fac, fac], axis=0)
    out = dot(sc[...], w[...], NT) + dot(ad[...], both_a)
    own[...] = out[: tokens // 2]
    send[...] = out[tokens // 2 :].astype(bf16)


def backward(count, rows, cots, packs, mag, r, b, ao, at, w):
    ff, width = w.shape
    tokens = rows * count
    rank = b.shape[0]
    rb = block_of(ff, 512)
    lines = packs[0].shape[0] - rank
    whole = lambda a: pl.BlockSpec(a.shape, lambda j: (0, 0))
    fixed = lambda shape: pl.BlockSpec(shape, lambda j: (0, 0))
    cols = lambda m: pl.BlockSpec((m, rb), lambda j: (0, j))
    return pl.pallas_call(
        functools.partial(backward_kernel, count, rows),
        grid=(ff // rb,),
        in_specs=[whole(a) for a in (*cots, *packs, mag, r, b)]
        + [cols(rank // 2), cols(rank // 2), pl.BlockSpec((rb, width), lambda j: (j, 0))],
        out_specs=[
            cols(tokens // 2),
            cols(tokens // 2),
            fixed((tokens, rank)),
            fixed((rank, width)),
            fixed((lines, tokens)),
            fixed((2, width)),
        ],
        out_shape=[
            jax.ShapeDtypeStruct((tokens // 2, ff), f32),
            jax.ShapeDtypeStruct((tokens // 2, ff), bf16),
            jax.ShapeDtypeStruct((tokens, rank), f32),
            jax.ShapeDtypeStruct((rank, width), f32),
            jax.ShapeDtypeStruct((lines, tokens), f32),
            jax.ShapeDtypeStruct((2, width), f32),
        ],
        scratch_shapes=[pltpu.VMEM((tokens, width), bf16), pltpu.VMEM((tokens, 2 * rank), bf16)],
        name="backward",
        cost_estimate=pl.CostEstimate(
            flops=2 * tokens * ff * width, bytes_accessed=2 * ff * width, transcendentals=0
        ),
    )(*cots, *packs, mag, r, b, ao, at, w)


def emit_kernel(count, *refs):
    parts = refs[:count]
    carried, embedded, norms, out = refs[count:]
    slot = lax.axis_index("section")
    half = slot % 2
    width = out.shape[1]
    here = embedded[:, pl.ds(pl.multiple_of(half * width, width), width)].astype(f32)
    inflow = jnp.where(slot < 2, here, carried[...].astype(f32))
    total = parts[0][...]
    for k in range(1, count):
        total = total + parts[k][...].astype(f32)
    out[...] = (inflow + total * norms[1:2, :]).astype(bf16)


def emit(count, parts, carried, embedded, norms):
    return pl.pallas_call(
        functools.partial(emit_kernel, count),
        out_shape=jax.ShapeDtypeStruct(carried.shape, bf16),
        name="emit",
    )(*parts, carried, embedded, norms)


def finish_kernel(count, *refs):
    own, got, adapt, got_adapt, yo, yt = refs[:6]
    mags = refs[6 : 6 + count]
    norms = refs[6 + count]
    hidden, ga, gm = refs[7 + count :]
    half = lax.axis_index("section") % 2
    hidden[...] = (own[...] + got[...].astype(f32)).astype(bf16)
    tokens, rank = adapt.shape
    ht, hr = tokens // 2, rank // 2
    first = adapt[:ht, :] + got_adapt[ht:, :]
    second = adapt[ht:, :] + got_adapt[:ht, :]
    pick = lambda v: jnp.where(half == 0, v[:, :hr], v[:, hr:]).astype(bf16)
    ga[...] = dot(pick(first), yo[...], TN) + dot(pick(second), yt[...], TN)

    @pl.when(pl.program_id(0) == 0)
    def _():
        total = mags[0][...]
        for k in range(1, count):
            total = total + mags[k][...]
        across = total.shape[1]
        for i in range(total.shape[0]):
            cut = slice(i * across, (i + 1) * across)
            gm[:, cut] = total[i : i + 1, :] / norms[0:1, cut]


def finish(count, own, got, adapt, got_adapt, yo, yt, mags, norms):
    ht, ff = own.shape
    rank = adapt.shape[1]
    rb = block_of(ff, 1792)
    whole = lambda a: pl.BlockSpec(a.shape, lambda j: (0, 0))
    cols = lambda m: pl.BlockSpec((m, rb), lambda j: (0, j))
    return pl.pallas_call(
        functools.partial(finish_kernel, count),
        grid=(ff // rb,),
        in_specs=[cols(ht), cols(ht), whole(adapt), whole(got_adapt), cols(ht), cols(ht)]
        + [whole(a) for a in (*mags, norms)],
        out_specs=[
            cols(ht),
            cols(rank // 2),
            pl.BlockSpec((1, norms.shape[1]), lambda j: (0, 0)),
        ],
        out_shape=[
            jax.ShapeDtypeStruct((ht, ff), bf16),
            jax.ShapeDtypeStruct((rank // 2, ff), f32),
            jax.ShapeDtypeStruct((1, norms.shape[1]), f32),
        ],
        name="finish",
    )(own, got, adapt, got_adapt, yo, yt, *mags, norms)


def local(
    frozen,
    adapter_a,
    adapter_b,
    magnitude,
    hidden_fwd,
    carried,
    embedded,
    hidden_bwd,
    returned,
    head_grad,
):
    w, ao, b, xo, yo = frozen[0], adapter_a[0], adapter_b[0], hidden_fwd[0], hidden_bwd[0]
    slots = lax.axis_size("section")
    count = lax.axis_size("tensor")
    slot = lax.axis_index("section")
    half = slot % 2
    rows, width = carried.shape[1:]

    def swap(array):
        return lax.ppermute(array, "section", [(i, i ^ 1) for i in range(slots)])

    def across(array, k):
        return lax.ppermute(array, "tensor", [(i, i ^ k) for i in range(count)])

    def shift(array, k):
        pairs = [
            (((s + 2) % slots) * count + t, s * count + (t ^ k))
            for s in range(slots)
            for t in range(count)
        ]
        return lax.ppermute(array, ("section", "tensor"), pairs)

    head = lax.dynamic_slice_in_dim(head_grad, half * width, width, 1)
    leaving = jnp.where(slot < 2, head, returned[0])
    xt, at, yt = swap(xo), swap(ao), swap(yo)
    cots = [None] * count
    for k in range(0, count, 2):
        cots[k] = shift(leaving, k)
        cots[k + 1] = across(cots[k], 1)
    arriving = lax.ppermute(carried[0], "section", [(i, i + 2) for i in range(slots - 2)])

    *parts, pack = forward(count, rows, xo, xt, yo, yt, ao, at, b, w)
    packs = [pack] + [across(pack, k) for k in range(1, count)]
    parts = [parts[0]] + [across(parts[k], k) for k in range(1, count)]
    r = again(yo, yt, pack, b, w)
    own, send, adapt, gb, magpack, norms = backward(
        count, rows, cots, packs, magnitude, r, b, ao, at, w
    )
    got, got_adapt = swap(send), swap(adapt)
    mags = [magpack] + [across(magpack, k) for k in range(1, count)]
    out = emit(count, parts, arriving, embedded, norms)
    hidden, ga, gm = finish(count, own, got, adapt, got_adapt, yo, yt, mags, norms)
    return (out[None], gm, ga[None], gb[None], hidden[None])


def solution(mesh):
    placed = (
        P("section", "tensor", None),
        P("section", None, "tensor"),
        P("section", None, None),
        P("section", None),
        P("section", None, "tensor"),
        P("section", "tensor", None),
        P("tensor", None),
        P("section", None, "tensor"),
        P("section", "tensor", None),
        P("tensor", None),
    )
    return jax.shard_map(
        local,
        mesh=mesh,
        in_specs=placed,
        out_specs=(
            P("section", "tensor", None),
            P("section", None),
            P("section", None, "tensor"),
            P("section", None, None),
            P("section", None, "tensor"),
        ),
        check_vma=False,
    )
```

time: 144 us -> 102 us (0.71)
  matrix products: 41.4 us -> 0 us
  Pallas kernels: 0 us -> 40.2 us
  blocking collectives: 19.6 us -> 0 us
  waiting for transfers between devices: 49.1 us -> 29.8 us
  starting transfers between devices: 6.09 us -> 24.9 us
  between operations: 14.2 us -> 0.83 us
  other arithmetic: 7.57 us -> 1.09 us
  local copies, waits for them, and re-layouts: 5.62 us -> 3.58 us
    dot_general x8 -> x0, matrix products: 41.4 us -> none  [the longest x1 11 us: local(): jnp.einsum('rf,rd->fd', fac_a, fac_b, preferred_element_type=jnp.float32)]
    pallas_call x0 -> x5, Pallas kernels: none -> 40.2 us  [the longest x1 12.9 us: backward(): pl.pallas_call(functools.partial(backward_kernel, count, rows), grid=(ff...]
    ppermute x7 -> x19, waiting for transfers between devices: 1.23 us -> 29.8 us  [the longest x11 17.3 us: across(): return lax.ppermute(array, 'tensor', [(i, i ^ k) for i in range(count)])]
    all_gather x1 -> x0, waiting for transfers between devices: 27.4 us -> none  [local(): cot_block = lax.all_gather(cotangent, 'tensor', axis=0, tiled=True)]
    reduce_scatter x1 -> x0, waiting for transfers between devices: 20.4 us -> none  [forward_rows(): lax.psum_scatter(term_fn(jnp.int32(0), own_rows * lax.axis_size('tensor')...]
    psum x1 -> x0, blocking collectives: 19.6 us -> none  [column_norms(): return jnp.sqrt(lax.psum(squares, 'tensor') + epsilon)]
    ppermute x7 -> x19, starting transfers between devices: 6.02 us -> 24.9 us  [the longest x11 13.5 us: across(): return lax.ppermute(array, 'tensor', [(i, i ^ k) for i in range(count)])]
    broadcast_in_dim x2 -> x0, other arithmetic: 3 us -> none  [the longest x1 1.83 us: local(): section_out[None]]
  transfers between devices with their start and end apart: 9 -> 19, of which waited for: 3 -> 6; matrix products, arithmetic and copies ran while one was open for 20% -> 1% of each run, Pallas kernels for 0% -> 23%
where the time goes in v1:
time: 102 us; the launch traced here: 100 us
  Pallas kernels  40.2 us (39%)
  waiting for transfers between devices  29.8 us (29%)
  starting transfers between devices  24.9 us (24%)
  local copies, waits for them, and re-layouts  3.58 us (4%)
  other arithmetic  1.09 us (1%)
    ppermute x11, waiting for transfers between devices, across(): return lax.ppermute(array, 'tensor', [(i, i ^ k) for i in range(count)])  17.3 us
    ppermute x11, starting transfers between devices, across(): return lax.ppermute(array, 'tensor', [(i, i ^ k) for i in range(count)])  13.5 us
    pallas_call x1, Pallas kernels, backward(): pl.pallas_call(functools.partial(backward_kernel, count, rows), grid=(ff...  12.9 us
    pallas_call x1, Pallas kernels, forward(): pl.pallas_call(functools.partial(forward_kernel, count, rows), grid=(widt...  11.4 us
    ppermute x2, waiting for transfers between devices, shift(): return lax.ppermute(array, ('section', 'tensor'), pairs)  10.8 us
    pallas_call x1, Pallas kernels, again(): pl.pallas_call(again_kernel, grid=(width // nb,), in_specs=[whole(a) for...  9.75 us
    ppermute x2, starting transfers between devices, shift(): return lax.ppermute(array, ('section', 'tensor'), pairs)  6.47 us
    ppermute x1, starting transfers between devices, local(): lax.ppermute(carried[0], 'section', [(i, i + 2) for i in range(slots - 2)])  4.22 us
  transfers between devices with their start and end apart: 19, of which 6 were waited for; matrix products, arithmetic and copies ran while one was open for 1% of the time, Pallas kernels for 23%

profile of v1, /device:TPU:0, one launch (start us, length us, event | category | flops | bytes accessed | tf_op | source)
XLA Modules:
  0.0 100.4 jit_solution(1795406453620868313)
XLA Ops:
  0.6 0.6 collective-permute-start.1
  1.2 0.1 collective-permute-start
  1.3 1.1 %bitcast_select_fusion = bf16[64,2048]{1,0:T(8,128)(2,1)S(1)} fusion(bf16[1,64,2048]{2,1,0:T(8,128)(2,1)} %param.18, bf16[64,4096]{1,0:T(8,128)(2,1)} %param.19, s32[]{:T(128)S(6)} %select_n.20, pred[]{:T(512)S(6)} %lt.12), kind=kLoop, calls=%fused_computation | loop fusion | flops 131072 | bytes 786437 | tf_op jit(solution)/shard_map/jit(_where)/select_n | solution.py:339
  2.4 5.9 %collective-permute-start.9 = (bf16[64,2048]{1,0:T(8,128)(2,1)S(1)}, bf16[64,2048]{1,0:T(8,128)(2,1)S(1)}, u32[]{:S(2)}, u32[]{:S(2)}) collective-permute-start(bf16[64,2048]{1,0:T(8,128)(2,1)S(1)} %bitcast_select_fusion), channel_id=1, source_target_pairs={{8,2},{9,3},{10,0},{11,1},{12,6},{13,7},{14,4},{15,5},{16,10},{17,... | collective-permute-start | bytes 786440 | tf_op jit(solution)/shard_map/ppermute | solution.py:336
  8.3 0.5 collective-permute-start.7
  8.8 0.0 collective-permute-start.2
  8.8 10.8 %collective-permute-done.9.refs_2_ = bf16[64,2048]{1,0:T(8,128)(2,1)S(1)} collective-permute-done((bf16[64,2048]{1,0:T(8,128)(2,1)S(1)}, bf16[64,2048]{1,0:T(8,128)(2,1)S(1)}, u32[]{:S(2)}, u32[]{:S(2)}) %collective-permute-start.9) | collective-permute-done | bytes 262176 | tf_op jit(solution)/shard_map/ppermute | solution.py:336
  19.6 1.6 %collective-permute-start.10 = (bf16[64,2048]{1,0:T(8,128)(2,1)S(1)}, bf16[64,2048]{1,0:T(8,128)(2,1)S(1)}, u32[]{:S(2)}, u32[]{:S(2)}) collective-permute-start(bf16[64,2048]{1,0:T(8,128)(2,1)S(1)} %collective-permute-done.9.refs_2_), channel_id=1, source_target_pairs={{0,1},{1,0},{2,3},{3,2},{4,5},{5,4},{6,7},{7,6},{8,9},{9,8},{10,11... | collective-permute-start | bytes 786440 | tf_op jit(solution)/shard_map/ppermute | solution.py:328
  21.2 0.0 collective-permute-done.7.refs_0_
  21.2 0.5 collective-permute-start.8
  21.7 0.0 collective-permute-done.2.at.refs_12_
  21.7 0.0 collective-permute-done.1.yt.refs_5_
  21.7 0.0 copy-start
  21.7 0.0 collective-permute-done.xt
  21.7 0.0 copy-start.2
  21.7 0.6 copy-done.11
  22.3 0.3 copy-done
  22.6 0.3 copy-done.2
  22.9 11.4 %forward.1 = (f32[64,2048]{1,0:T(8,128)}, bf16[64,2048]{1,0:T(8,128)(2,1)}, bf16[64,2048]{1,0:T(8,128)(2,1)}, bf16[64,2048]{1,0:T(8,128)(2,1)}, f32[24,256]{1,0:T(8,128)}) custom-call(bf16[128,3584]{1,0:T(8,128)(2,1)} %bitcast.20, bf16[128,3584]{1,0:T(8,128)(2,1)} %copy-done.2, bf16[128,3584]{1,0:T(8,128)(2,1)} %bitcast.16, bf16[128,3584]{1,0:T(8,128)(2,1)} %copy-done, ...), custom_call_target="tpu_custom_call" | custom-call | flops 3758096384 | bytes 14680064 | tf_op jit(solution)/shard_map/forward/pallas_call | solution.py:94
  34.3 0.0 copy-done.3
  34.3 1.6 %collective-permute-start.11 = (f32[24,256]{1,0:T(8,128)}, f32[24,256]{1,0:T(8,128)S(1)}, u32[]{:S(2)}, u32[]{:S(2)}) collective-permute-start(f32[24,256]{1,0:T(8,128)} %get-tuple-element.23.pack.refs_4_), channel_id=1, source_target_pairs={{0,1},{1,0},{2,3},{3,2},{4,5},{5,4},{6,7},{7,6},{8,9},{9,8},{10,11... | collective-permute-start | bytes 73736 | tf_op jit(solution)/shard_map/ppermute | solution.py:328
  36.0 2.5 %collective-permute-start.12 = (f32[24,256]{1,0:T(8,128)}, f32[24,256]{1,0:T(8,128)S(1)}, u32[]{:S(2)}, u32[]{:S(2)}) collective-permute-start(f32[24,256]{1,0:T(8,128)} %get-tuple-element.23.pack.refs_4_), channel_id=1, source_target_pairs={{0,2},{1,3},{2,0},{3,1},{4,6},{5,7},{6,4},{7,5},{8,10},{9,11},{10,... | collective-permute-start | bytes 73736 | tf_op jit(solution)/shard_map/ppermute | solution.py:328
  38.5 0.3 collective-permute-start.13
  38.8 9.7 %again.1.refs_9_ = f32[256,2048]{1,0:T(8,128)} custom-call(bf16[128,3584]{1,0:T(8,128)(2,1)} %bitcast.17, bf16[128,3584]{1,0:T(8,128)(2,1)} %copy-done, f32[24,256]{1,0:T(8,128)} %get-tuple-element.23.pack.refs_4_, bf16[16,2048]{1,0:T(8,128)(2,1)} %bitcast.22, bf16[3584,2048]{1,0:T(8,128)(2,1)} %bitcast.13), custom_call_target="tpu_custom_call" | custom-call | flops 3758096384 | bytes 14680064 | tf_op jit(solution)/shard_map/again/pallas_call | solution.py:135
  48.6 0.0 collective-permute-done.10.refs_3_
  48.6 0.0 collective-permute-done.8.refs_1_
  48.6 0.0 collective-permute-done.11.refs_5_
  48.6 0.0 copy-start.13
  48.6 0.0 collective-permute-done.12.refs_6_
  48.6 0.0 collective-permute-done.13.refs_7_
  48.6 0.6 copy-done.5
  49.3 0.1 copy-done.6
  49.4 0.0 copy-done.13
  49.4 0.0 copy-done.14
  49.4 0.6 copy-done.15
  50.0 12.9 %backward.1 = (f32[128,3584]{1,0:T(8,128)}, bf16[128,3584]{1,0:T(8,128)(2,1)}, f32[256,16]{1,0:T(8,128)}, f32[16,2048]{1,0:T(8,128)}, f32[8,256]{1,0:T(8,128)}, /*index=5*/f32[2,2048]{1,0:T(2,128)}) custom-call(bf16[64,2048]{1,0:T(8,128)(2,1)} %copy-done.4, bf16[64,2048]{1,0:T(8,128)(2,1)} %copy-done.6, bf16[64,2048]{1,0:T(8,128)(2,1)} %copy-done.3, ...), custom_call_target="tpu_custom_call" | custom-call | flops 3758096384 | bytes 14680064 | tf_op jit(solution)/shard_map/backward/pallas_call | solution.py:204
  62.9 0.1 collective-permute-start.14
  63.0 4.2 %collective-permute-start.6 = (bf16[64,2048]{1,0:T(8,128)(2,1)S(1)}, bf16[64,2048]{1,0:T(8,128)(2,1)S(1)}, u32[]{:S(2)}, u32[]{:S(2)}) collective-permute-start(bf16[64,2048]{1,0:T(8,128)(2,1)S(1)} %bitcast.29), channel_id=1, source_target_pairs={{0,8},{4,12},{8,16},{12,20},{16,24},{20,28},{1,9},{5,13},{9,17},{1... | collective-permute-start | bytes 786440 | tf_op jit(solution)/shard_map/ppermute | solution.py:345
  67.2 0.3 collective-permute-start.3
  67.5 3.8 %collective-permute-start.4 = (bf16[64,2048]{1,0:T(8,128)(2,1)}, bf16[64,2048]{1,0:T(8,128)(2,1)S(1)}, u32[]{:S(2)}, u32[]{:S(2)}) collective-permute-start(bf16[64,2048]{1,0:T(8,128)(2,1)} %get-tuple-element.21), channel_id=1, source_target_pairs={{0,2},{1,3},{2,0},{3,1},{4,6},{5,7},{6,4},{7,5},{8,10},{9,11},{10,... | collective-permute-start | bytes 786440 | tf_op jit(solution)/shard_map/ppermute | solution.py:328
  71.3 0.0 copy-done.20
  71.3 0.3 collective-permute-start.5
  71.7 1.7 %collective-permute-done.6.refs_4_ = bf16[64,2048]{1,0:T(8,128)(2,1)S(1)} collective-permute-done((bf16[64,2048]{1,0:T(8,128)(2,1)S(1)}, bf16[64,2048]{1,0:T(8,128)(2,1)S(1)}, u32[]{:S(2)}, u32[]{:S(2)}) %collective-permute-start.6) | collective-permute-done | bytes 262176 | tf_op jit(solution)/shard_map/ppermute | solution.py:345
  73.4 0.0 collective-permute-start.15
  73.4 7.6 %collective-permute-done.3.refs_1_ = bf16[64,2048]{1,0:T(8,128)(2,1)S(1)} collective-permute-done((bf16[64,2048]{1,0:T(8,128)(2,1)}, bf16[64,2048]{1,0:T(8,128)(2,1)S(1)}, u32[]{:S(2)}, u32[]{:S(2)}) %collective-permute-start.3) | collective-permute-done | bytes 262176 | tf_op jit(solution)/shard_map/ppermute | solution.py:328
  81.0 0.0 collective-permute-start.16
  81.0 9.0 %collective-permute-done.4.refs_2_ = bf16[64,2048]{1,0:T(8,128)(2,1)S(1)} collective-permute-done((bf16[64,2048]{1,0:T(8,128)(2,1)}, bf16[64,2048]{1,0:T(8,128)(2,1)S(1)}, u32[]{:S(2)}, u32[]{:S(2)}) %collective-permute-start.4) | collective-permute-done | bytes 262176 | tf_op jit(solution)/shard_map/ppermute | solution.py:328
  90.0 0.0 collective-permute-start.17
  90.0 0.0 collective-permute-done.5.refs_3_
  90.0 2.6 %collective-permute-start.18 = (f32[8,256]{1,0:T(8,128)}, f32[8,256]{1,0:T(8,128)S(1)}, u32[]{:S(2)}, u32[]{:S(2)}) collective-permute-start(f32[8,256]{1,0:T(8,128)} %get-tuple-element.28.refs_6_), channel_id=1, source_target_pairs={{0,3},{1,2},{2,1},{3,0},{4,7},{5,6},{6,5},{7,4},{8,11},{9,10},{10,... | collective-permute-start | bytes 24584 | tf_op jit(solution)/shard_map/ppermute | solution.py:328
  92.6 0.0 copy-done.10
  92.6 2.4 %emit.1 = bf16[64,2048]{1,0:T(8,128)(2,1)} custom-call(f32[64,2048]{1,0:T(8,128)} %get-tuple-element.19.refs_0_, bf16[64,2048]{1,0:T(8,128)(2,1)} %copy-done.8, bf16[64,2048]{1,0:T(8,128)(2,1)} %copy-done.9, bf16[64,2048]{1,0:T(8,128)(2,1)} %copy-done.10, bf16[64,2048]{1,0:T(8,128)(2,1)} %copy-done.7, bf16[64,4096]{1,0:T(8,128)(2,1)} %refs_5_.1, ...), custom_call_target="tpu_custom_call" | custom-call | tf_op jit(solution)/shard_map/emit/pallas_call | solution.py:248
  95.1 0.0 collective-permute-done.16.refs_7_
  95.1 0.2 collective-permute-done.17.refs_8_
  95.3 0.5 collective-permute-done.18.refs_9_
  95.8 0.0 collective-permute-done.15.refs_3_
  95.8 0.0 collective-permute-done.14.refs_1_
  95.8 0.0 copy-start.1
  95.8 0.0 copy-done.16
  95.8 0.1 copy-done.17
  95.9 0.5 copy-done.18
  96.3 0.1 copy-done.12
  96.4 0.3 copy-done.1
  96.7 3.7 %finish.1 = (bf16[128,3584]{1,0:T(8,128)(2,1)}, f32[8,3584]{1,0:T(8,128)}, f32[1,2048]{1,0:T(1,128)}) custom-call(f32[128,3584]{1,0:T(8,128)} %get-tuple-element.25.refs_0_, bf16[128,3584]{1,0:T(8,128)(2,1)} %copy-done.1, f32[256,16]{1,0:T(8,128)} %get-tuple-element.27.refs_2_, f32[256,16]{1,0:T(8,128)} %copy-done.12, bf16[128,3584]{1,0:T(8,128)(2,1)} %bitcast.18, ...), custom_call_target="tpu_custom_call" | custom-call | tf_op jit(solution)/shard_map/finish/pallas_call | solution.py:286
  (22 shorter events, 0.0 us)
Async XLA Ops:
  0.6 21.0 %collective-permute-start.1 = (bf16[128,3584]{1,0:T(8,128)(2,1)}, bf16[128,3584]{1,0:T(8,128)(2,1)S(1)}, u32[]{:S(2)}, u32[]{:S(2)}) collective-permute-start(bf16[128,3584]{1,0:T(8,128)(2,1)} %bitcast.15), channel_id=1, source_target_pairs={{0,4},{4,0},{8,12},{12,8},{16,20},{20,16},{24,28},{28,24},{1,5},{5... | collective-permute-start | bytes 2752520 | tf_op jit(solution)/shard_map/ppermute | solution.py:325
  1.2 20.5 %collective-permute-start = (bf16[128,3584]{1,0:T(8,128)(2,1)}, bf16[128,3584]{1,0:T(8,128)(2,1)S(1)}, u32[]{:S(2)}, u32[]{:S(2)}) collective-permute-start(bf16[128,3584]{1,0:T(8,128)(2,1)} %bitcast.19), channel_id=1, source_target_pairs={{0,4},{4,0},{8,12},{12,8},{16,20},{20,16},{24,28},{28,24},{1,5},{5... | collective-permute-start | bytes 2752520 | tf_op jit(solution)/shard_map/ppermute | solution.py:325
  2.4 17.3 %collective-permute-start.9 = (bf16[64,2048]{1,0:T(8,128)(2,1)S(1)}, bf16[64,2048]{1,0:T(8,128)(2,1)S(1)}, u32[]{:S(2)}, u32[]{:S(2)}) collective-permute-start(bf16[64,2048]{1,0:T(8,128)(2,1)S(1)} %bitcast_select_fusion), channel_id=1, source_target_pairs={{8,2},{9,3},{10,0},{11,1},{12,6},{13,7},{14,4},{15,5},{16,10},{17,... | collective-permute-start | bytes 786440 | tf_op jit(solution)/shard_map/ppermute | solution.py:336
  8.3 12.9 %collective-permute-start.7 = (bf16[64,2048]{1,0:T(8,128)(2,1)S(1)}, bf16[64,2048]{1,0:T(8,128)(2,1)S(1)}, u32[]{:S(2)}, u32[]{:S(2)}) collective-permute-start(bf16[64,2048]{1,0:T(8,128)(2,1)S(1)} %bitcast_select_fusion), channel_id=1, source_target_pairs={{8,0},{9,1},{10,2},{11,3},{12,4},{13,5},{14,6},{15,7},{16,8},{17,9... | collective-permute-start | bytes 786440 | tf_op jit(solution)/shard_map/ppermute | solution.py:336
  8.8 12.8 %collective-permute-start.2 = (bf16[8,3584]{1,0:T(8,128)(2,1)}, bf16[8,3584]{1,0:T(8,128)(2,1)S(1)}, u32[]{:S(2)}, u32[]{:S(2)}) collective-permute-start(bf16[8,3584]{1,0:T(8,128)(2,1)} %bitcast.25), channel_id=1, source_target_pairs={{0,4},{4,0},{8,12},{12,8},{16,20},{20,16},{24,28},{28,24},{1,5},{5... | collective-permute-start | bytes 172040 | tf_op jit(solution)/shard_map/ppermute | solution.py:325
  19.6 14.7 %copy-start.3 = (bf16[64,2048]{1,0:T(8,128)(2,1)}, bf16[64,2048]{1,0:T(8,128)(2,1)S(1)}, u32[]{:S(2)}) copy-start(bf16[64,2048]{1,0:T(8,128)(2,1)S(1)} %collective-permute-done.9.refs_2_) | copy-start | bytes 786436
  19.6 28.9 %collective-permute-start.10 = (bf16[64,2048]{1,0:T(8,128)(2,1)S(1)}, bf16[64,2048]{1,0:T(8,128)(2,1)S(1)}, u32[]{:S(2)}, u32[]{:S(2)}) collective-permute-start(bf16[64,2048]{1,0:T(8,128)(2,1)S(1)} %collective-permute-done.9.refs_2_), channel_id=1, source_target_pairs={{0,1},{1,0},{2,3},{3,2},{4,5},{5,4},{6,7},{7,6},{8,9},{9,8},{10,11... | collective-permute-start | bytes 786440 | tf_op jit(solution)/shard_map/ppermute | solution.py:328
  21.2 13.1 %copy-start.4 = (bf16[64,2048]{1,0:T(8,128)(2,1)}, bf16[64,2048]{1,0:T(8,128)(2,1)S(1)}, u32[]{:S(2)}) copy-start(bf16[64,2048]{1,0:T(8,128)(2,1)S(1)} %collective-permute-done.7.refs_0_) | copy-start | bytes 786436
  21.2 27.4 %collective-permute-start.8 = (bf16[64,2048]{1,0:T(8,128)(2,1)S(1)}, bf16[64,2048]{1,0:T(8,128)(2,1)S(1)}, u32[]{:S(2)}, u32[]{:S(2)}) collective-permute-start(bf16[64,2048]{1,0:T(8,128)(2,1)S(1)} %collective-permute-done.7.refs_0_), channel_id=1, source_target_pairs={{0,1},{1,0},{2,3},{3,2},{4,5},{5,4},{6,7},{7,6},{8,9},{9,8},{10,11... | collective-permute-start | bytes 786440 | tf_op jit(solution)/shard_map/ppermute | solution.py:328
  21.7 0.6 copy-start.11
  21.7 1.0 copy-start
  21.7 1.2 %copy-start.2 = (bf16[128,3584]{1,0:T(8,128)(2,1)}, bf16[128,3584]{1,0:T(8,128)(2,1)S(1)}, u32[]{:S(2)}) copy-start(bf16[128,3584]{1,0:T(8,128)(2,1)S(1)} %collective-permute-done.xt) | copy-start | bytes 2752516
  34.3 14.2 %collective-permute-start.11 = (f32[24,256]{1,0:T(8,128)}, f32[24,256]{1,0:T(8,128)S(1)}, u32[]{:S(2)}, u32[]{:S(2)}) collective-permute-start(f32[24,256]{1,0:T(8,128)} %get-tuple-element.23.pack.refs_4_), channel_id=1, source_target_pairs={{0,1},{1,0},{2,3},{3,2},{4,5},{5,4},{6,7},{7,6},{8,9},{9,8},{10,11... | collective-permute-start | bytes 73736 | tf_op jit(solution)/shard_map/ppermute | solution.py:328
  36.0 12.6 %collective-permute-start.12 = (f32[24,256]{1,0:T(8,128)}, f32[24,256]{1,0:T(8,128)S(1)}, u32[]{:S(2)}, u32[]{:S(2)}) collective-permute-start(f32[24,256]{1,0:T(8,128)} %get-tuple-element.23.pack.refs_4_), channel_id=1, source_target_pairs={{0,2},{1,3},{2,0},{3,1},{4,6},{5,7},{6,4},{7,5},{8,10},{9,11},{10,... | collective-permute-start | bytes 73736 | tf_op jit(solution)/shard_map/ppermute | solution.py:328
  38.5 10.2 %collective-permute-start.13 = (f32[24,256]{1,0:T(8,128)}, f32[24,256]{1,0:T(8,128)S(1)}, u32[]{:S(2)}, u32[]{:S(2)}) collective-permute-start(f32[24,256]{1,0:T(8,128)} %get-tuple-element.23.pack.refs_4_), channel_id=1, source_target_pairs={{0,3},{1,2},{2,1},{3,0},{4,7},{5,6},{6,5},{7,4},{8,11},{9,10},{10,... | collective-permute-start | bytes 73736 | tf_op jit(solution)/shard_map/ppermute | solution.py:328
  48.5 14.4 %copy-start.19 = (bf16[1,64,2048]{2,1,0:T(8,128)(2,1)S(1)}, bf16[1,64,2048]{2,1,0:T(8,128)(2,1)}, u32[]{:S(2)}) copy-start(bf16[1,64,2048]{2,1,0:T(8,128)(2,1)} %param.15) | copy-start | bytes 786436
  48.5 22.8 %copy-start.20 = (bf16[64,2048]{1,0:T(8,128)(2,1)S(1)}, bf16[64,2048]{1,0:T(8,128)(2,1)}, u32[]{:S(2)}) copy-start(bf16[64,2048]{1,0:T(8,128)(2,1)} %get-tuple-element.22) | copy-start | bytes 786436
  48.6 0.7 copy-start.5
  48.6 0.8 copy-start.6
  48.6 0.8 copy-start.13
  48.6 0.8 copy-start.14
  49.4 0.6 copy-start.15
  62.9 32.9 %collective-permute-start.14 = (bf16[128,3584]{1,0:T(8,128)(2,1)}, bf16[128,3584]{1,0:T(8,128)(2,1)S(1)}, u32[]{:S(2)}, u32[]{:S(2)}) collective-permute-start(bf16[128,3584]{1,0:T(8,128)(2,1)} %get-tuple-element.26), channel_id=1, source_target_pairs={{0,4},{4,0},{8,12},{12,8},{16,20},{20,16},{24,28},{28,24},{1,5},{5... | collective-permute-start | bytes 2752520 | tf_op jit(solution)/shard_map/ppermute | solution.py:325
  63.0 10.4 %collective-permute-start.6 = (bf16[64,2048]{1,0:T(8,128)(2,1)S(1)}, bf16[64,2048]{1,0:T(8,128)(2,1)S(1)}, u32[]{:S(2)}, u32[]{:S(2)}) collective-permute-start(bf16[64,2048]{1,0:T(8,128)(2,1)S(1)} %bitcast.29), channel_id=1, source_target_pairs={{0,8},{4,12},{8,16},{12,20},{16,24},{20,28},{1,9},{5,13},{9,17},{1... | collective-permute-start | bytes 786440 | tf_op jit(solution)/shard_map/ppermute | solution.py:345
  67.2 13.8 %collective-permute-start.3 = (bf16[64,2048]{1,0:T(8,128)(2,1)}, bf16[64,2048]{1,0:T(8,128)(2,1)S(1)}, u32[]{:S(2)}, u32[]{:S(2)}) collective-permute-start(bf16[64,2048]{1,0:T(8,128)(2,1)} %get-tuple-element.20), channel_id=1, source_target_pairs={{0,1},{1,0},{2,3},{3,2},{4,5},{5,4},{6,7},{7,6},{8,9},{9,8},{10,11... | collective-permute-start | bytes 786440 | tf_op jit(solution)/shard_map/ppermute | solution.py:328
  67.5 22.5 %collective-permute-start.4 = (bf16[64,2048]{1,0:T(8,128)(2,1)}, bf16[64,2048]{1,0:T(8,128)(2,1)S(1)}, u32[]{:S(2)}, u32[]{:S(2)}) collective-permute-start(bf16[64,2048]{1,0:T(8,128)(2,1)} %get-tuple-element.21), channel_id=1, source_target_pairs={{0,2},{1,3},{2,0},{3,1},{4,6},{5,7},{6,4},{7,5},{8,10},{9,11},{10,... | collective-permute-start | bytes 786440 | tf_op jit(solution)/shard_map/ppermute | solution.py:328
  71.3 18.7 %collective-permute-start.5 = (bf16[64,2048]{1,0:T(8,128)(2,1)S(1)}, bf16[64,2048]{1,0:T(8,128)(2,1)S(1)}, u32[]{:S(2)}, u32[]{:S(2)}) collective-permute-start(bf16[64,2048]{1,0:T(8,128)(2,1)S(1)} %copy-done.20), channel_id=1, source_target_pairs={{0,3},{1,2},{2,1},{3,0},{4,7},{5,6},{6,5},{7,4},{8,11},{9,10},{10,... | collective-permute-start | bytes 786440 | tf_op jit(solution)/shard_map/ppermute | solution.py:328
  73.4 19.2 %copy-start.7 = (bf16[64,2048]{1,0:T(8,128)(2,1)}, bf16[64,2048]{1,0:T(8,128)(2,1)S(1)}, u32[]{:S(2)}) copy-start(bf16[64,2048]{1,0:T(8,128)(2,1)S(1)} %collective-permute-done.6.refs_4_) | copy-start | bytes 786436
  73.4 22.4 %collective-permute-start.15 = (f32[256,16]{1,0:T(8,128)}, f32[256,16]{1,0:T(8,128)S(1)}, u32[]{:S(2)}, u32[]{:S(2)}) collective-permute-start(f32[256,16]{1,0:T(8,128)} %get-tuple-element.27.refs_2_), channel_id=1, source_target_pairs={{0,4},{4,0},{8,12},{12,8},{16,20},{20,16},{24,28},{28,24},{1,5},{5... | collective-permute-start | bytes 49160 | tf_op jit(solution)/shard_map/ppermute | solution.py:325
  81.0 11.6 %copy-start.8 = (bf16[64,2048]{1,0:T(8,128)(2,1)}, bf16[64,2048]{1,0:T(8,128)(2,1)S(1)}, u32[]{:S(2)}) copy-start(bf16[64,2048]{1,0:T(8,128)(2,1)S(1)} %collective-permute-done.3.refs_1_) | copy-start | bytes 786436
  81.0 14.0 %collective-permute-start.16 = (f32[8,256]{1,0:T(8,128)}, f32[8,256]{1,0:T(8,128)S(1)}, u32[]{:S(2)}, u32[]{:S(2)}) collective-permute-start(f32[8,256]{1,0:T(8,128)} %get-tuple-element.28.refs_6_), channel_id=1, source_target_pairs={{0,1},{1,0},{2,3},{3,2},{4,5},{5,4},{6,7},{7,6},{8,9},{9,8},{10,11... | collective-permute-start | bytes 24584 | tf_op jit(solution)/shard_map/ppermute | solution.py:328
  90.0 2.6 %copy-start.9 = (bf16[64,2048]{1,0:T(8,128)(2,1)}, bf16[64,2048]{1,0:T(8,128)(2,1)S(1)}, u32[]{:S(2)}) copy-start(bf16[64,2048]{1,0:T(8,128)(2,1)S(1)} %collective-permute-done.4.refs_2_) | copy-start | bytes 786436
  90.0 5.3 %collective-permute-start.17 = (f32[8,256]{1,0:T(8,128)}, f32[8,256]{1,0:T(8,128)S(1)}, u32[]{:S(2)}, u32[]{:S(2)}) collective-permute-start(f32[8,256]{1,0:T(8,128)} %get-tuple-element.28.refs_6_), channel_id=1, source_target_pairs={{0,2},{1,3},{2,0},{3,1},{4,6},{5,7},{6,4},{7,5},{8,10},{9,11},{10,... | collective-permute-start | bytes 24584 | tf_op jit(solution)/shard_map/ppermute | solution.py:328
  90.0 2.6 %copy-start.10 = (bf16[64,2048]{1,0:T(8,128)(2,1)}, bf16[64,2048]{1,0:T(8,128)(2,1)S(1)}, u32[]{:S(2)}) copy-start(bf16[64,2048]{1,0:T(8,128)(2,1)S(1)} %collective-permute-done.5.refs_3_) | copy-start | bytes 786436
  90.0 5.7 %collective-permute-start.18 = (f32[8,256]{1,0:T(8,128)}, f32[8,256]{1,0:T(8,128)S(1)}, u32[]{:S(2)}, u32[]{:S(2)}) collective-permute-start(f32[8,256]{1,0:T(8,128)} %get-tuple-element.28.refs_6_), channel_id=1, source_target_pairs={{0,3},{1,2},{2,1},{3,0},{4,7},{5,6},{6,5},{7,4},{8,11},{9,10},{10,... | collective-permute-start | bytes 24584 | tf_op jit(solution)/shard_map/ppermute | solution.py:328
  95.1 0.7 copy-start.16
  95.3 0.6 copy-start.17
  95.8 0.6 copy-start.18
  95.8 0.7 copy-start.12
  95.8 1.0 copy-start.1

commit v2 on v0

v2 whole, which is shorter than its diff:
```python
import functools

import jax
import jax.numpy as jnp
from jax import lax
from jax.experimental import pallas as pl
from jax.experimental.pallas import tpu as pltpu
from jax.sharding import PartitionSpec as P

epsilon = 1e-06
f32 = jnp.float32
bf16 = jnp.bfloat16
NT = (((1,), (1,)), ((), ()))
TN = (((0,), (0,)), ((), ()))


def block_of(size, most):
    return max(b for b in range(128, most + 1, 128) if size % b == 0)


def dot(a, b, dims=(((1,), (0,)), ((), ()))):
    return lax.dot_general(a, b, dims, preferred_element_type=f32)


def two_parts(value):
    high = value.astype(bf16)
    low = (value - high.astype(f32)).astype(bf16)
    return jnp.concatenate([high, low], axis=1)


def halves(own, other, half):
    own, other = own.astype(f32), other.astype(f32)
    first = jnp.where(half == 0, own, other)
    second = jnp.where(half == 0, other, own)
    return jnp.concatenate([first, second], axis=0).astype(bf16)


def place_of(shard, half, count):
    return jnp.bitwise_xor(shard, half * (count // 2))


def whole_call(body, args, shapes, scratch=(), flops=0, moved=0, limit=12 << 20):
    one = pl.BlockSpec(memory_space=pltpu.VMEM)
    return pl.pallas_call(
        body,
        in_specs=[one] * len(args),
        out_specs=[one] * len(shapes),
        out_shape=shapes,
        scratch_shapes=scratch,
        compiler_params=pltpu.CompilerParams(vmem_limit_bytes=limit),
        cost_estimate=pl.CostEstimate(flops=flops, bytes_accessed=moved, transcendentals=0),
    )(*args)


def in_hbm(array):
    return pltpu.with_memory_space_constraint(array, pltpu.HBM)


def shaped(shape, dtype):
    return jax.ShapeDtypeStruct(shape, dtype)


def choose_kernel(returned, head, out):
    slot = lax.axis_index("section")
    width = out.shape[1]
    spot = pl.ds(pl.multiple_of((slot % 2) * width, width), width)

    @pl.when(slot < 2)
    def _():
        pltpu.sync_copy(head.at[:, spot], out)

    @pl.when(slot >= 2)
    def _():
        pltpu.sync_copy(returned, out)


def choose(returned, head):
    return pl.pallas_call(
        choose_kernel,
        in_specs=[pl.BlockSpec(memory_space=pltpu.HBM)] * 2,
        out_specs=pl.BlockSpec(memory_space=pltpu.VMEM),
        out_shape=shaped(returned.shape, bf16),
        name="choose",
        compiler_params=pltpu.CompilerParams(vmem_limit_bytes=4 << 20),
    )(in_hbm(returned), in_hbm(head))


def forward_kernel(count, rows, nb, xo, xt, yo, yt, ao, at, b_in, w_in, *refs):
    outs, (pack, w, ys, fac, b) = refs[:count], refs[count : count + 5]
    xs, res, a_first, a_second, sems = refs[count + 5 :]
    half = lax.axis_index("section") % 2
    me = lax.axis_index("tensor")
    ht = xo.shape[0]
    tokens = 2 * ht
    rank, width = b.shape
    lines, across = pack.shape[0] - rank, pack.shape[1]
    cuts = [pl.ds(j, nb) for j in range(0, width, nb)]
    moves = [
        (ao, a_first),
        (at, a_second),
        (b_in, b),
        (xo, xs.at[:ht, :]),
        (xt, xs.at[ht:tokens, :]),
        (w_in.at[:, cuts[0]], w.at[:, cuts[0]]),
        (yo, ys.at[:ht, :]),
        (yt, ys.at[ht:, :]),
    ] + [(w_in.at[:, c], w.at[:, c]) for c in cuts[1:]]
    copies = [pltpu.make_async_copy(m[0], m[1], sems.at[i]) for i, m in enumerate(moves)]
    for copy in copies:
        copy.start()
    for copy in copies[:5]:
        copy.wait()
    fac[...] = halves(a_first[...], a_second[...], half)
    xs[tokens:, :] = fac[...]
    lx = two_parts(dot(xs[:tokens, :], fac[...], NT))
    gram = two_parts(dot(fac[...], fac[...], NT))
    for n, j in enumerate(range(0, width, nb)):
        copies[5 if n == 0 else 7 + n].wait()
        cut = slice(j, j + nb)
        wv, bv = w[:, cut], b[:, cut]
        both_b = jnp.concatenate([bv, bv], axis=0)
        total = dot(xs[...], wv)
        res[...] = total[:tokens] + dot(lx, both_b)
        wf = wv.astype(f32)
        squares = jnp.sum((wf * wf).reshape(wf.shape[0] // 8, 8, nb), axis=0)
        cross = 2.0 * total[tokens:] + dot(gram, both_b)
        cross = bv.astype(f32) * cross
        for r in range(0, rank, 8):
            squares = squares + cross[r : r + 8]
        squares = jnp.sum(squares, axis=0, keepdims=True)
        for i in range(0, nb, across):
            at_line = (j + i) // across
            pack[at_line : at_line + 1, :] = squares[:, i : i + across]
        for k in range(count):
            at_row = place_of(jnp.bitwise_xor(me, k), half, count) * rows
            piece = res[pl.ds(pl.multiple_of(at_row, rows), rows), :]
            outs[k][:, cut] = piece.astype(outs[k].dtype)
        if n == 0:
            copies[6].wait()
            copies[7].wait()
            pack[lines:, :] = dot(ys[...], fac[...], NT).T


def forward(count, rows, xo, xt, yo, yt, ao, at, b, w):
    ff, width = w.shape
    ht = xo.shape[0]
    tokens = 2 * ht
    rank = b.shape[0]
    nb = block_of(width, 512)
    args = (in_hbm(xo), xt, in_hbm(yo), yt, in_hbm(ao), at, in_hbm(b), in_hbm(w))
    shapes = [shaped((rows, width), f32 if k == 0 else bf16) for k in range(count)] + [
        shaped((width // tokens + rank, tokens), f32),
        shaped(w.shape, bf16),
        shaped((tokens, ff), bf16),
        shaped((rank, ff), bf16),
        shaped(b.shape, bf16),
    ]
    return pl.pallas_call(
        functools.partial(forward_kernel, count, rows, nb),
        in_specs=[pl.BlockSpec(memory_space=m) for m in (pltpu.HBM, pl.ANY) * 3 + (pltpu.HBM,) * 2],
        out_specs=[pl.BlockSpec(memory_space=pltpu.VMEM)] * len(shapes),
        out_shape=shapes,
        scratch_shapes=[
            pltpu.VMEM((tokens + rank, ff), bf16),
            pltpu.VMEM((tokens, nb), f32),
            pltpu.VMEM((rank // 2, ff), bf16),
            pltpu.VMEM((rank // 2, ff), bf16),
            pltpu.SemaphoreType.DMA((7 + width // nb,)),
        ],
        name="forward",
        compiler_params=pltpu.CompilerParams(vmem_limit_bytes=12 << 20),
        cost_estimate=pl.CostEstimate(
            flops=2 * tokens * ff * width, bytes_accessed=2 * ff * width, transcendentals=0
        ),
    )(*args)


def again_kernel(nb, ys, pack, b, w, out):
    rank, width = b.shape
    ly = two_parts(pack[pack.shape[0] - rank :, :].T)
    for j in range(0, width, nb):
        cut = slice(j, j + nb)
        both_b = jnp.concatenate([b[:, cut], b[:, cut]], axis=0)
        out[:, cut] = dot(ys[...], w[:, cut]) + dot(ly, both_b)


def again(ys, pack, b, w):
    ff, width = w.shape
    tokens = ys.shape[0]
    return whole_call(
        functools.partial(again_kernel, block_of(width, 512)),
        (ys, pack, b, w),
        [shaped((tokens, width), f32)],
        (),
        2 * tokens * ff * width,
        2 * ff * width,
    )[0]


def backward_kernel(count, rows, rb, *refs):
    cots, packs = refs[:count], refs[count : 2 * count]
    mag, r, b, fac, w = refs[2 * count : 2 * count + 5]
    own, send, adapt, gb, magpack, norms = refs[2 * count + 5 : 2 * count + 11]
    (sc,) = refs[2 * count + 11 :]
    half = lax.axis_index("section") % 2
    me = lax.axis_index("tensor")
    rank = b.shape[0]
    tokens, width = sc.shape
    total = packs[0][...]
    for k in range(1, count):
        total = total + packs[k][...]
    lines = total.shape[0] - rank
    across = total.shape[1]
    sqr = jnp.sqrt(jnp.maximum(total[:lines], 0.0) + epsilon)
    for i in range(lines):
        norms[0:1, i * across : (i + 1) * across] = sqr[i : i + 1, :]
    scale = mag[...] / norms[0:1, :]
    norms[1:2, :] = scale
    mags = jnp.zeros((8, width), f32)
    for k in range(count):
        at_row = place_of(jnp.bitwise_xor(me, k), half, count) * rows
        spot = pl.ds(pl.multiple_of(at_row, rows), rows)
        cot = cots[k][...].astype(f32)
        sc[spot, :] = (cot * scale).astype(bf16)
        mags = mags + jnp.sum((cot * r[spot, :]).reshape(rows // 8, 8, width), axis=0)
    mags = jnp.sum(mags, axis=0, keepdims=True)
    for i in range(lines):
        magpack[i : i + 1, :] = mags[:, i * across : (i + 1) * across]
    part = dot(sc[...], b[...], NT)
    adapt[...] = part
    ad = two_parts(part)
    gb[...] = dot(total[lines:].astype(bf16), sc[...])
    for j in range(0, w.shape[0], rb):
        cut = slice(j, j + rb)
        both_a = jnp.concatenate([fac[:, cut], fac[:, cut]], axis=0)
        out = dot(sc[...], w[cut, :], NT) + dot(ad, both_a)
        own[:, cut] = out[: tokens // 2]
        send[:, cut] = out[tokens // 2 :].astype(bf16)


def backward(count, rows, cots, packs, mag, r, b, fac, w):
    ff, width = w.shape
    tokens = rows * count
    rank = b.shape[0]
    return whole_call(
        functools.partial(backward_kernel, count, rows, block_of(ff, 512)),
        (*cots, *packs, mag, r, b, fac, w),
        [
            shaped((tokens // 2, ff), f32),
            shaped((tokens // 2, ff), bf16),
            shaped((tokens, rank), f32),
            shaped((rank, width), f32),
            shaped((width // tokens, tokens), f32),
            shaped((2, width), f32),
        ],
        [pltpu.VMEM((tokens, width), bf16)],
        2 * tokens * ff * width,
        2 * ff * width,
    )


def emit_kernel(count, *refs):
    parts = refs[:count]
    carried, embedded, norms, out = refs[count:]
    slot = lax.axis_index("section")
    half = slot % 2
    width = out.shape[1]
    here = embedded[:, pl.ds(pl.multiple_of(half * width, width), width)].astype(f32)
    inflow = jnp.where(slot < 2, here, carried[...].astype(f32))
    total = parts[0][...]
    for k in range(1, count):
        total = total + parts[k][...].astype(f32)
    out[...] = (inflow + total * norms[1:2, :]).astype(bf16)


def emit(count, parts, carried, embedded, norms):
    return whole_call(
        functools.partial(emit_kernel, count),
        (*parts, carried, embedded, norms),
        [shaped(carried.shape, bf16)],
        moved=8 * carried.size * 2,
    )[0]


def finish_kernel(count, *refs):
    own, got, adapt, got_adapt, ys = refs[:5]
    mags = refs[5 : 5 + count]
    norms = refs[5 + count]
    hidden, ga, gm = refs[6 + count :]
    half = lax.axis_index("section") % 2
    hidden[...] = (own[...] + got[...].astype(f32)).astype(bf16)
    tokens, rank = adapt.shape
    ht, hr = tokens // 2, rank // 2
    first = adapt[:ht, :] + got_adapt[ht:, :]
    second = adapt[ht:, :] + got_adapt[:ht, :]
    pick = lambda v: jnp.where(half == 0, v[:, :hr], v[:, hr:]).astype(bf16)
    ga[...] = dot(pick(jnp.concatenate([first, second], axis=0)), ys[...], TN)
    total = mags[0][...]
    for k in range(1, count):
        total = total + mags[k][...]
    across = total.shape[1]
    for i in range(total.shape[0]):
        cut = slice(i * across, (i + 1) * across)
        gm[:, cut] = total[i : i + 1, :] / norms[0:1, cut]


def finish(count, own, got, adapt, got_adapt, ys, mags, norms):
    ht, ff = own.shape
    rank = adapt.shape[1]
    return whole_call(
        functools.partial(finish_kernel, count),
        (own, got, adapt, got_adapt, ys, *mags, norms),
        [shaped((ht, ff), bf16), shaped((rank // 2, ff), f32), shaped((1, norms.shape[1]), f32)],
        moved=12 * ht * ff,
    )


def local(
    frozen,
    adapter_a,
    adapter_b,
    magnitude,
    hidden_fwd,
    carried,
    embedded,
    hidden_bwd,
    returned,
    head_grad,
):
    w, ao, b, xo, yo = frozen[0], adapter_a[0], adapter_b[0], hidden_fwd[0], hidden_bwd[0]
    slots = lax.axis_size("section")
    count = lax.axis_size("tensor")
    rows = carried.shape[1]

    def swap(array):
        return lax.ppermute(array, "section", [(i, i ^ 1) for i in range(slots)])

    def across(array, k):
        return lax.ppermute(array, "tensor", [(i, i ^ k) for i in range(count)])

    def shift(array, k):
        pairs = [
            (((s + 2) % slots) * count + t, s * count + (t ^ k))
            for s in range(slots)
            for t in range(count)
        ]
        return lax.ppermute(array, ("section", "tensor"), pairs)

    leaving = choose(returned[0], head_grad)
    xt, at, yt = swap(xo), swap(ao), swap(yo)
    cots = [None] * count
    for k in range(0, count, 2):
        cots[k] = shift(leaving, k)
        cots[k + 1] = across(cots[k], 1)
    arriving = lax.ppermute(carried[0], "section", [(i, i + 2) for i in range(slots - 2)])
    *parts, pack, w, ys, fac, b = forward(count, rows, xo, xt, yo, yt, ao, at, b, w)
    packs = [pack]
    for k in range(1, count):
        parts[k] = across(parts[k], k)
    for k in range(1, count):
        packs.append(across(pack, k))
    r = again(ys, pack, b, w)
    own, send, adapt, gb, magpack, norms = backward(
        count, rows, cots, packs, magnitude, r, b, fac, w
    )
    got, got_adapt = swap(send), swap(adapt)
    mags = [magpack]
    for k in range(1, count):
        mags.append(across(magpack, k))
    out = emit(count, parts, arriving, embedded, norms)
    hidden, ga, gm = finish(count, own, got, adapt, got_adapt, ys, mags, norms)
    return (out[None], gm, ga[None], gb[None], hidden[None])


def solution(mesh):
    placed = (
        P("section", "tensor", None),
        P("section", None, "tensor"),
        P("section", None, None),
        P("section", None),
        P("section", None, "tensor"),
        P("section", "tensor", None),
        P("tensor", None),
        P("section", None, "tensor"),
        P("section", "tensor", None),
        P("tensor", None),
    )

    return jax.shard_map(
        local,
        mesh=mesh,
        in_specs=placed,
        out_specs=(
            P("section", "tensor", None),
            P("section", None),
            P("section", None, "tensor"),
            P("section", None, None),
            P("section", None, "tensor"),
        ),
        check_vma=False,
    )
```

time: 144 us -> 80.9 us (0.56)
  matrix products: 41.4 us -> 0 us
  Pallas kernels: 0 us -> 23.3 us
  blocking collectives: 19.6 us -> 0 us
  starting transfers between devices: 6.09 us -> 24.7 us
  waiting for transfers between devices: 49.1 us -> 31 us
  between operations: 14.2 us -> 0.72 us
  other arithmetic: 7.57 us -> 0 us
  local copies, waits for them, and re-layouts: 5.62 us -> 0.01 us
    dot_general x8 -> x0, matrix products: 41.4 us -> none  [the longest x1 11 us: local(): jnp.einsum('rf,rd->fd', fac_a, fac_b, preferred_element_type=jnp.float32)]
    ppermute x7 -> x19, waiting for transfers between devices: 1.23 us -> 31 us  [the longest x11 18.5 us: across(): return lax.ppermute(array, 'tensor', [(i, i ^ k) for i in range(count)])]
    all_gather x1 -> x0, waiting for transfers between devices: 27.4 us -> none  [local(): cot_block = lax.all_gather(cotangent, 'tensor', axis=0, tiled=True)]
    pallas_call x0 -> x6, Pallas kernels: none -> 23.3 us  [the longest x4 13.4 us: whole_call(): pl.pallas_call(body, in_specs=[one] * len(args), out_specs=[one] * len(sh...]
    reduce_scatter x1 -> x0, waiting for transfers between devices: 20.4 us -> none  [forward_rows(): lax.psum_scatter(term_fn(jnp.int32(0), own_rows * lax.axis_size('tensor')...]
    psum x1 -> x0, blocking collectives: 19.6 us -> none  [column_norms(): return jnp.sqrt(lax.psum(squares, 'tensor') + epsilon)]
    ppermute x7 -> x19, starting transfers between devices: 6.02 us -> 24.7 us  [the longest x11 13.5 us: across(): return lax.ppermute(array, 'tensor', [(i, i ^ k) for i in range(count)])]
    unnamed x28 -> x6, local copies, waits for them, and re-layouts: 4.24 us -> 0.01 us
  transfers between devices with their start and end apart: 9 -> 19, of which waited for: 3 -> 7; matrix products, arithmetic and copies ran while one was open for 20% -> 0% of each run, Pallas kernels for 0% -> 19%
where the time goes in v2:
time: 80.9 us; the launch traced here: 79.8 us
  waiting for transfers between devices  31 us (38%)
  starting transfers between devices  24.7 us (31%)
  Pallas kernels  23.3 us (29%)
    ppermute x11, waiting for transfers between devices, across(): return lax.ppermute(array, 'tensor', [(i, i ^ k) for i in range(count)])  18.5 us
    ppermute x11, starting transfers between devices, across(): return lax.ppermute(array, 'tensor', [(i, i ^ k) for i in range(count)])  13.5 us
    pallas_call x4, Pallas kernels, whole_call(): pl.pallas_call(body, in_specs=[one] * len(args), out_specs=[one] * len(sh...  13.4 us
    ppermute x2, waiting for transfers between devices, shift(): return lax.ppermute(array, ('section', 'tensor'), pairs)  10.8 us
    pallas_call x1, Pallas kernels, forward(): pl.pallas_call(functools.partial(forward_kernel, count, rows, nb), in_spe...  8.98 us
    ppermute x2, starting transfers between devices, shift(): return lax.ppermute(array, ('section', 'tensor'), pairs)  6.42 us
    ppermute x1, starting transfers between devices, local(): lax.ppermute(carried[0], 'section', [(i, i + 2) for i in range(slots - 2)])  4.2 us
    ppermute x1, waiting for transfers between devices, local(): lax.ppermute(carried[0], 'section', [(i, i + 2) for i in range(slots - 2)])  1.75 us
  transfers between devices with their start and end apart: 19, of which 7 were waited for; matrix products, arithmetic and copies ran while one was open for 0% of the time, Pallas kernels for 19%

profile of v2, /device:TPU:0, one launch (start us, length us, event | category | flops | bytes accessed | tf_op | source)
XLA Modules:
  0.0 79.8 jit_solution(8585039022751164771)
XLA Ops:
  0.6 0.6 collective-permute-start
  1.2 0.1 collective-permute-start.1
  1.3 0.9 %choose.1 = bf16[64,2048]{1,0:T(8,128)(2,1)S(1)} custom-call(bf16[64,2048]{1,0:T(8,128)(2,1)} %bitcast.17, bf16[64,4096]{1,0:T(8,128)(2,1)} %head.1), custom_call_target="tpu_custom_call" | custom-call | tf_op jit(solution)/shard_map/choose/pallas_call | solution.py:78
  2.2 5.9 %collective-permute-start.9 = (bf16[64,2048]{1,0:T(8,128)(2,1)S(1)}, bf16[64,2048]{1,0:T(8,128)(2,1)S(1)}, u32[]{:S(2)}, u32[]{:S(2)}) collective-permute-start(bf16[64,2048]{1,0:T(8,128)(2,1)S(1)} %choose.1), channel_id=1, source_target_pairs={{8,2},{9,3},{10,0},{11,1},{12,6},{13,7},{14,4},{15,5},{16,10},{17,... | collective-permute-start | bytes 786440 | tf_op jit(solution)/shard_map/ppermute | solution.py:347
  8.1 0.5 collective-permute-start.7
  8.6 0.0 collective-permute-start.2
  8.6 10.8 %collective-permute-done.9.refs_2_ = bf16[64,2048]{1,0:T(8,128)(2,1)S(1)} collective-permute-done((bf16[64,2048]{1,0:T(8,128)(2,1)S(1)}, bf16[64,2048]{1,0:T(8,128)(2,1)S(1)}, u32[]{:S(2)}, u32[]{:S(2)}) %collective-permute-start.9) | collective-permute-done | bytes 262176 | tf_op jit(solution)/shard_map/ppermute | solution.py:347
  19.4 1.6 %collective-permute-start.10 = (bf16[64,2048]{1,0:T(8,128)(2,1)S(1)}, bf16[64,2048]{1,0:T(8,128)(2,1)S(1)}, u32[]{:S(2)}, u32[]{:S(2)}) collective-permute-start(bf16[64,2048]{1,0:T(8,128)(2,1)S(1)} %collective-permute-done.9.refs_2_), channel_id=1, source_target_pairs={{0,1},{1,0},{2,3},{3,2},{4,5},{5,4},{6,7},{7,6},{8,9},{9,8},{10,11... | collective-permute-start | bytes 786440 | tf_op jit(solution)/shard_map/ppermute | solution.py:339
  21.0 0.0 collective-permute-done.7.refs_0_
  21.0 0.4 collective-permute-start.8
  21.4 0.0 collective-permute-done.2.at
  21.4 0.0 collective-permute-done.xt
  21.5 0.0 collective-permute-done.1.yt
  21.5 9.0 %forward.1 = (f32[64,2048]{1,0:T(8,128)S(1)}, bf16[64,2048]{1,0:T(8,128)(2,1)S(1)}, bf16[64,2048]{1,0:T(8,128)(2,1)S(1)}, bf16[64,2048]{1,0:T(8,128)(2,1)S(1)}, ...) custom-call(bf16[128,3584]{1,0:T(8,128)(2,1)} %bitcast.13, ...), custom_call_target="tpu_custom_call" | custom-call | flops 3758096384 | bytes 14680064 | tf_op jit(solution)/shard_map/forward/pallas_call | solution.py:158
  30.4 1.6 %collective-permute-start.11 = (f32[24,256]{1,0:T(8,128)S(1)}, f32[24,256]{1,0:T(8,128)S(1)}, u32[]{:S(2)}, u32[]{:S(2)}) collective-permute-start(f32[24,256]{1,0:T(8,128)S(1)} %get-tuple-element.27.pack.refs_4_), channel_id=1, source_target_pairs={{0,1},{1,0},{2,3},{3,2},{4,5},{5,4},{6,7},{7,6},{8,9},{9,8},{10,11... | collective-permute-start | bytes 73736 | tf_op jit(solution)/shard_map/ppermute | solution.py:339
  32.1 2.5 %collective-permute-start.12 = (f32[24,256]{1,0:T(8,128)S(1)}, f32[24,256]{1,0:T(8,128)S(1)}, u32[]{:S(2)}, u32[]{:S(2)}) collective-permute-start(f32[24,256]{1,0:T(8,128)S(1)} %get-tuple-element.27.pack.refs_4_), channel_id=1, source_target_pairs={{0,2},{1,3},{2,0},{3,1},{4,6},{5,7},{6,4},{7,5},{8,10},{9,11},{10,... | collective-permute-start | bytes 73736 | tf_op jit(solution)/shard_map/ppermute | solution.py:339
  34.6 0.3 collective-permute-start.13
  34.9 0.0 copy-start.1
  34.9 4.4 %shard_map.137.refs_9_ = f32[256,2048]{1,0:T(8,128)S(1)} custom-call(bf16[256,3584]{1,0:T(8,128)(2,1)S(1)} %get-tuple-element.28.ys.refs_4_, f32[24,256]{1,0:T(8,128)S(1)} %get-tuple-element.27.pack.refs_4_, bf16[16,2048]{1,0:T(8,128)(2,1)S(1)} %get-tuple-element.29.b.refs_10_, bf16[3584,2048]{1,0:T(8,128)(2,1)S(1)} %get-tuple-element.30.w.refs_12_), custom_call_target="tpu_custom_call" | custom-call | flops 3758096384 | bytes 14680064 | tf_op jit(solution)/shard_map/pallas_call | solution.py:44
  39.3 0.0 collective-permute-done.10.refs_3_
  39.3 0.0 collective-permute-done.8.refs_1_
  39.3 0.0 collective-permute-done.11.refs_5_
  39.3 0.0 collective-permute-done.12.refs_6_
  39.3 0.9 %collective-permute-done.13.refs_7_ = f32[24,256]{1,0:T(8,128)S(1)} collective-permute-done((f32[24,256]{1,0:T(8,128)S(1)}, f32[24,256]{1,0:T(8,128)S(1)}, u32[]{:S(2)}, u32[]{:S(2)}) %collective-permute-start.13) | collective-permute-done | bytes 24608 | tf_op jit(solution)/shard_map/ppermute | solution.py:339
  40.2 0.0 copy-done.1
  40.2 0.0 copy-start.2
  40.2 0.0 copy-start
  40.2 6.5 %shard_map.138 = (f32[128,3584]{1,0:T(8,128)S(1)}, bf16[128,3584]{1,0:T(8,128)(2,1)S(1)}, f32[256,16]{1,0:T(8,128)S(1)}, f32[16,2048]{1,0:T(8,128)}, f32[8,256]{1,0:T(8,128)S(1)}, /*index=5*/f32[2,2048]{1,0:T(2,128)S(1)}) custom-call(bf16[64,2048]{1,0:T(8,128)(2,1)S(1)} %collective-permute-done.7.refs_0_, ...), custom_call_target="tpu_custom_call" | custom-call | flops 3758096384 | bytes 14680064 | tf_op jit(solution)/shard_map/pallas_call | solution.py:44
  46.7 0.0 collective-permute-start.14
  46.7 0.0 copy-done.2
  46.7 4.2 %collective-permute-start.6 = (bf16[64,2048]{1,0:T(8,128)(2,1)S(1)}, bf16[64,2048]{1,0:T(8,128)(2,1)S(1)}, u32[]{:S(2)}, u32[]{:S(2)}) collective-permute-start(bf16[64,2048]{1,0:T(8,128)(2,1)S(1)} %bitcast.22), channel_id=1, source_target_pairs={{0,8},{4,12},{8,16},{12,20},{16,24},{20,28},{1,9},{5,13},{9,17},{1... | collective-permute-start | bytes 786440 | tf_op jit(solution)/shard_map/ppermute | solution.py:355
  50.9 0.1 collective-permute-start.3
  51.0 3.2 %collective-permute-start.4 = (bf16[64,2048]{1,0:T(8,128)(2,1)S(1)}, bf16[64,2048]{1,0:T(8,128)(2,1)S(1)}, u32[]{:S(2)}, u32[]{:S(2)}) collective-permute-start(bf16[64,2048]{1,0:T(8,128)(2,1)S(1)} %get-tuple-element.25), channel_id=1, source_target_pairs={{0,2},{1,3},{2,0},{3,1},{4,6},{5,7},{6,4},{7,5},{8,10},{9,11},{10,... | collective-permute-start | bytes 786440 | tf_op jit(solution)/shard_map/ppermute | solution.py:339
  54.2 1.2 %collective-permute-start.5 = (bf16[64,2048]{1,0:T(8,128)(2,1)S(1)}, bf16[64,2048]{1,0:T(8,128)(2,1)S(1)}, u32[]{:S(2)}, u32[]{:S(2)}) collective-permute-start(bf16[64,2048]{1,0:T(8,128)(2,1)S(1)} %get-tuple-element.26), channel_id=1, source_target_pairs={{0,3},{1,2},{2,1},{3,0},{4,7},{5,6},{6,5},{7,4},{8,11},{9,10},{10,... | collective-permute-start | bytes 786440 | tf_op jit(solution)/shard_map/ppermute | solution.py:339
  55.4 1.7 %collective-permute-done.6.refs_4_ = bf16[64,2048]{1,0:T(8,128)(2,1)S(1)} collective-permute-done((bf16[64,2048]{1,0:T(8,128)(2,1)S(1)}, bf16[64,2048]{1,0:T(8,128)(2,1)S(1)}, u32[]{:S(2)}, u32[]{:S(2)}) %collective-permute-start.6) | collective-permute-done | bytes 262176 | tf_op jit(solution)/shard_map/ppermute | solution.py:355
  57.1 0.0 collective-permute-start.15
  57.1 7.4 %collective-permute-done.3.refs_1_ = bf16[64,2048]{1,0:T(8,128)(2,1)S(1)} collective-permute-done((bf16[64,2048]{1,0:T(8,128)(2,1)S(1)}, bf16[64,2048]{1,0:T(8,128)(2,1)S(1)}, u32[]{:S(2)}, u32[]{:S(2)}) %collective-permute-start.3) | collective-permute-done | bytes 262176 | tf_op jit(solution)/shard_map/ppermute | solution.py:339
  64.5 0.0 collective-permute-start.16
  64.6 8.1 %collective-permute-done.4.refs_2_ = bf16[64,2048]{1,0:T(8,128)(2,1)S(1)} collective-permute-done((bf16[64,2048]{1,0:T(8,128)(2,1)S(1)}, bf16[64,2048]{1,0:T(8,128)(2,1)S(1)}, u32[]{:S(2)}, u32[]{:S(2)}) %collective-permute-start.4) | collective-permute-done | bytes 262176 | tf_op jit(solution)/shard_map/ppermute | solution.py:339
  72.7 0.0 collective-permute-start.17
  72.7 0.0 collective-permute-done.5.refs_3_
  72.7 2.5 %collective-permute-start.18 = (f32[8,256]{1,0:T(8,128)S(1)}, f32[8,256]{1,0:T(8,128)S(1)}, u32[]{:S(2)}, u32[]{:S(2)}) collective-permute-start(f32[8,256]{1,0:T(8,128)S(1)} %get-tuple-element.36.refs_5_), channel_id=1, source_target_pairs={{0,3},{1,2},{2,1},{3,0},{4,7},{5,6},{6,5},{7,4},{8,11},{9,10},{10,... | collective-permute-start | bytes 24584 | tf_op jit(solution)/shard_map/ppermute | solution.py:339
  75.2 0.0 copy-done
  75.2 0.9 %shard_map.139 = bf16[64,2048]{1,0:T(8,128)(2,1)} custom-call(f32[64,2048]{1,0:T(8,128)S(1)} %get-tuple-element.23.refs_0_, bf16[64,2048]{1,0:T(8,128)(2,1)S(1)} %collective-permute-done.3.refs_1_, bf16[64,2048]{1,0:T(8,128)(2,1)S(1)} %collective-permute-done.4.refs_2_, bf16[64,2048]{1,0:T(8,128)(2,1)S(1)} %collective-permute-done.5.refs_3_, ...), custom_call_target="tpu_custom_call" | custom-call | bytes 2097152 | tf_op jit(solution)/shard_map/pallas_call | solution.py:44
  76.1 0.0 collective-permute-done.16.refs_6_
  76.1 1.9 %collective-permute-done.17.refs_7_ = f32[8,256]{1,0:T(8,128)S(1)} collective-permute-done((f32[8,256]{1,0:T(8,128)S(1)}, f32[8,256]{1,0:T(8,128)S(1)}, u32[]{:S(2)}, u32[]{:S(2)}) %collective-permute-start.17) | collective-permute-done | bytes 8224 | tf_op jit(solution)/shard_map/ppermute | solution.py:339
  78.0 0.1 collective-permute-done.18.refs_8_
  78.1 0.0 collective-permute-done.15.refs_3_
  78.1 0.0 collective-permute-done.14.refs_1_
  78.2 1.6 %shard_map.140 = (bf16[128,3584]{1,0:T(8,128)(2,1)}, f32[8,3584]{1,0:T(8,128)}, f32[1,2048]{1,0:T(1,128)}) custom-call(f32[128,3584]{1,0:T(8,128)S(1)} %get-tuple-element.33.refs_0_, bf16[128,3584]{1,0:T(8,128)(2,1)S(1)} %collective-permute-done.14.refs_1_, f32[256,16]{1,0:T(8,128)S(1)} %get-tuple-element.35.refs_2_, ...), custom_call_target="tpu_custom_call" | custom-call | bytes 5505024 | tf_op jit(solution)/shard_map/pallas_call | solution.py:44
Async XLA Ops:
  0.6 20.8 %collective-permute-start = (bf16[128,3584]{1,0:T(8,128)(2,1)}, bf16[128,3584]{1,0:T(8,128)(2,1)S(1)}, u32[]{:S(2)}, u32[]{:S(2)}) collective-permute-start(bf16[128,3584]{1,0:T(8,128)(2,1)} %bitcast.12), channel_id=1, source_target_pairs={{0,4},{4,0},{8,12},{12,8},{16,20},{20,16},{24,28},{28,24},{1,5},{5... | collective-permute-start | bytes 2752520 | tf_op jit(solution)/shard_map/ppermute | solution.py:336
  1.2 20.3 %collective-permute-start.1 = (bf16[128,3584]{1,0:T(8,128)(2,1)}, bf16[128,3584]{1,0:T(8,128)(2,1)S(1)}, u32[]{:S(2)}, u32[]{:S(2)}) collective-permute-start(bf16[128,3584]{1,0:T(8,128)(2,1)} %bitcast.14), channel_id=1, source_target_pairs={{0,4},{4,0},{8,12},{12,8},{16,20},{20,16},{24,28},{28,24},{1,5},{5... | collective-permute-start | bytes 2752520 | tf_op jit(solution)/shard_map/ppermute | solution.py:336
  2.2 17.2 %collective-permute-start.9 = (bf16[64,2048]{1,0:T(8,128)(2,1)S(1)}, bf16[64,2048]{1,0:T(8,128)(2,1)S(1)}, u32[]{:S(2)}, u32[]{:S(2)}) collective-permute-start(bf16[64,2048]{1,0:T(8,128)(2,1)S(1)} %choose.1), channel_id=1, source_target_pairs={{8,2},{9,3},{10,0},{11,1},{12,6},{13,7},{14,4},{15,5},{16,10},{17,... | collective-permute-start | bytes 786440 | tf_op jit(solution)/shard_map/ppermute | solution.py:347
  8.1 12.9 %collective-permute-start.7 = (bf16[64,2048]{1,0:T(8,128)(2,1)S(1)}, bf16[64,2048]{1,0:T(8,128)(2,1)S(1)}, u32[]{:S(2)}, u32[]{:S(2)}) collective-permute-start(bf16[64,2048]{1,0:T(8,128)(2,1)S(1)} %choose.1), channel_id=1, source_target_pairs={{8,0},{9,1},{10,2},{11,3},{12,4},{13,5},{14,6},{15,7},{16,8},{17,9... | collective-permute-start | bytes 786440 | tf_op jit(solution)/shard_map/ppermute | solution.py:347
  8.6 12.8 %collective-permute-start.2 = (bf16[8,3584]{1,0:T(8,128)(2,1)}, bf16[8,3584]{1,0:T(8,128)(2,1)S(1)}, u32[]{:S(2)}, u32[]{:S(2)}) collective-permute-start(bf16[8,3584]{1,0:T(8,128)(2,1)} %bitcast.19), channel_id=1, source_target_pairs={{0,4},{4,0},{8,12},{12,8},{16,20},{20,16},{24,28},{28,24},{1,5},{5... | collective-permute-start | bytes 172040 | tf_op jit(solution)/shard_map/ppermute | solution.py:336
  19.4 19.9 %collective-permute-start.10 = (bf16[64,2048]{1,0:T(8,128)(2,1)S(1)}, bf16[64,2048]{1,0:T(8,128)(2,1)S(1)}, u32[]{:S(2)}, u32[]{:S(2)}) collective-permute-start(bf16[64,2048]{1,0:T(8,128)(2,1)S(1)} %collective-permute-done.9.refs_2_), channel_id=1, source_target_pairs={{0,1},{1,0},{2,3},{3,2},{4,5},{5,4},{6,7},{7,6},{8,9},{9,8},{10,11... | collective-permute-start | bytes 786440 | tf_op jit(solution)/shard_map/ppermute | solution.py:339
  21.0 18.3 %collective-permute-start.8 = (bf16[64,2048]{1,0:T(8,128)(2,1)S(1)}, bf16[64,2048]{1,0:T(8,128)(2,1)S(1)}, u32[]{:S(2)}, u32[]{:S(2)}) collective-permute-start(bf16[64,2048]{1,0:T(8,128)(2,1)S(1)} %collective-permute-done.7.refs_0_), channel_id=1, source_target_pairs={{0,1},{1,0},{2,3},{3,2},{4,5},{5,4},{6,7},{7,6},{8,9},{9,8},{10,11... | collective-permute-start | bytes 786440 | tf_op jit(solution)/shard_map/ppermute | solution.py:339
  30.4 8.9 %collective-permute-start.11 = (f32[24,256]{1,0:T(8,128)S(1)}, f32[24,256]{1,0:T(8,128)S(1)}, u32[]{:S(2)}, u32[]{:S(2)}) collective-permute-start(f32[24,256]{1,0:T(8,128)S(1)} %get-tuple-element.27.pack.refs_4_), channel_id=1, source_target_pairs={{0,1},{1,0},{2,3},{3,2},{4,5},{5,4},{6,7},{7,6},{8,9},{9,8},{10,11... | collective-permute-start | bytes 73736 | tf_op jit(solution)/shard_map/ppermute | solution.py:339
  32.1 7.2 %collective-permute-start.12 = (f32[24,256]{1,0:T(8,128)S(1)}, f32[24,256]{1,0:T(8,128)S(1)}, u32[]{:S(2)}, u32[]{:S(2)}) collective-permute-start(f32[24,256]{1,0:T(8,128)S(1)} %get-tuple-element.27.pack.refs_4_), channel_id=1, source_target_pairs={{0,2},{1,3},{2,0},{3,1},{4,6},{5,7},{6,4},{7,5},{8,10},{9,11},{10,... | collective-permute-start | bytes 73736 | tf_op jit(solution)/shard_map/ppermute | solution.py:339
  34.6 5.6 %collective-permute-start.13 = (f32[24,256]{1,0:T(8,128)S(1)}, f32[24,256]{1,0:T(8,128)S(1)}, u32[]{:S(2)}, u32[]{:S(2)}) collective-permute-start(f32[24,256]{1,0:T(8,128)S(1)} %get-tuple-element.27.pack.refs_4_), channel_id=1, source_target_pairs={{0,3},{1,2},{2,1},{3,0},{4,7},{5,6},{6,5},{7,4},{8,11},{9,10},{10,... | collective-permute-start | bytes 73736 | tf_op jit(solution)/shard_map/ppermute | solution.py:339
  34.9 5.3 %copy-start.1 = (f32[1,2048]{1,0:T(1,128)S(1)}, f32[1,2048]{1,0:T(1,128)}, u32[]{:S(2)}) copy-start(f32[1,2048]{1,0:T(1,128)} %refs_8_.1) | copy-start | bytes 24580
  40.2 6.5 %copy-start.2 = (bf16[1,64,2048]{2,1,0:T(8,128)(2,1)S(1)}, bf16[1,64,2048]{2,1,0:T(8,128)(2,1)}, u32[]{:S(2)}) copy-start(bf16[1,64,2048]{2,1,0:T(8,128)(2,1)} %param.15) | copy-start | bytes 786436
  40.2 35.0 %copy-start = (bf16[64,4096]{1,0:T(8,128)(2,1)S(1)}, bf16[64,4096]{1,0:T(8,128)(2,1)}, u32[]{:S(2)}) copy-start(bf16[64,4096]{1,0:T(8,128)(2,1)} %refs_5_.1) | copy-start | bytes 1572868
  46.7 31.5 %collective-permute-start.14 = (bf16[128,3584]{1,0:T(8,128)(2,1)S(1)}, bf16[128,3584]{1,0:T(8,128)(2,1)S(1)}, u32[]{:S(2)}, u32[]{:S(2)}) collective-permute-start(bf16[128,3584]{1,0:T(8,128)(2,1)S(1)} %get-tuple-element.34), channel_id=1, source_target_pairs={{0,4},{4,0},{8,12},{12,8},{16,20},{20,16},{24,28},{28,24},{1,5},{5... | collective-permute-start | bytes 2752520 | tf_op jit(solution)/shard_map/ppermute | solution.py:336
  46.7 10.4 %collective-permute-start.6 = (bf16[64,2048]{1,0:T(8,128)(2,1)S(1)}, bf16[64,2048]{1,0:T(8,128)(2,1)S(1)}, u32[]{:S(2)}, u32[]{:S(2)}) collective-permute-start(bf16[64,2048]{1,0:T(8,128)(2,1)S(1)} %bitcast.22), channel_id=1, source_target_pairs={{0,8},{4,12},{8,16},{12,20},{16,24},{20,28},{1,9},{5,13},{9,17},{1... | collective-permute-start | bytes 786440 | tf_op jit(solution)/shard_map/ppermute | solution.py:355
  50.9 13.6 %collective-permute-start.3 = (bf16[64,2048]{1,0:T(8,128)(2,1)S(1)}, bf16[64,2048]{1,0:T(8,128)(2,1)S(1)}, u32[]{:S(2)}, u32[]{:S(2)}) collective-permute-start(bf16[64,2048]{1,0:T(8,128)(2,1)S(1)} %get-tuple-element.24), channel_id=1, source_target_pairs={{0,1},{1,0},{2,3},{3,2},{4,5},{5,4},{6,7},{7,6},{8,9},{9,8},{10,11... | collective-permute-start | bytes 786440 | tf_op jit(solution)/shard_map/ppermute | solution.py:339
  51.0 21.7 %collective-permute-start.4 = (bf16[64,2048]{1,0:T(8,128)(2,1)S(1)}, bf16[64,2048]{1,0:T(8,128)(2,1)S(1)}, u32[]{:S(2)}, u32[]{:S(2)}) collective-permute-start(bf16[64,2048]{1,0:T(8,128)(2,1)S(1)} %get-tuple-element.25), channel_id=1, source_target_pairs={{0,2},{1,3},{2,0},{3,1},{4,6},{5,7},{6,4},{7,5},{8,10},{9,11},{10,... | collective-permute-start | bytes 786440 | tf_op jit(solution)/shard_map/ppermute | solution.py:339
  54.2 18.5 %collective-permute-start.5 = (bf16[64,2048]{1,0:T(8,128)(2,1)S(1)}, bf16[64,2048]{1,0:T(8,128)(2,1)S(1)}, u32[]{:S(2)}, u32[]{:S(2)}) collective-permute-start(bf16[64,2048]{1,0:T(8,128)(2,1)S(1)} %get-tuple-element.26), channel_id=1, source_target_pairs={{0,3},{1,2},{2,1},{3,0},{4,7},{5,6},{6,5},{7,4},{8,11},{9,10},{10,... | collective-permute-start | bytes 786440 | tf_op jit(solution)/shard_map/ppermute | solution.py:339
  57.1 21.0 %collective-permute-start.15 = (f32[256,16]{1,0:T(8,128)S(1)}, f32[256,16]{1,0:T(8,128)S(1)}, u32[]{:S(2)}, u32[]{:S(2)}) collective-permute-start(f32[256,16]{1,0:T(8,128)S(1)} %get-tuple-element.35.refs_2_), channel_id=1, source_target_pairs={{0,4},{4,0},{8,12},{12,8},{16,20},{20,16},{24,28},{28,24},{1,5},{5... | collective-permute-start | bytes 49160 | tf_op jit(solution)/shard_map/ppermute | solution.py:336
  64.5 11.6 %collective-permute-start.16 = (f32[8,256]{1,0:T(8,128)S(1)}, f32[8,256]{1,0:T(8,128)S(1)}, u32[]{:S(2)}, u32[]{:S(2)}) collective-permute-start(f32[8,256]{1,0:T(8,128)S(1)} %get-tuple-element.36.refs_5_), channel_id=1, source_target_pairs={{0,1},{1,0},{2,3},{3,2},{4,5},{5,4},{6,7},{7,6},{8,9},{9,8},{10,11... | collective-permute-start | bytes 24584 | tf_op jit(solution)/shard_map/ppermute | solution.py:339
  72.7 5.3 %collective-permute-start.17 = (f32[8,256]{1,0:T(8,128)S(1)}, f32[8,256]{1,0:T(8,128)S(1)}, u32[]{:S(2)}, u32[]{:S(2)}) collective-permute-start(f32[8,256]{1,0:T(8,128)S(1)} %get-tuple-element.36.refs_5_), channel_id=1, source_target_pairs={{0,2},{1,3},{2,0},{3,1},{4,6},{5,7},{6,4},{7,5},{8,10},{9,11},{10,... | collective-permute-start | bytes 24584 | tf_op jit(solution)/shard_map/ppermute | solution.py:339
  72.7 5.5 %collective-permute-start.18 = (f32[8,256]{1,0:T(8,128)S(1)}, f32[8,256]{1,0:T(8,128)S(1)}, u32[]{:S(2)}, u32[]{:S(2)}) collective-permute-start(f32[8,256]{1,0:T(8,128)S(1)} %get-tuple-element.36.refs_5_), channel_id=1, source_target_pairs={{0,3},{1,2},{2,1},{3,0},{4,7},{5,6},{6,5},{7,4},{8,11},{9,10},{10,... | collective-permute-start | bytes 24584 | tf_op jit(solution)/shard_map/ppermute | solution.py:339

commit v3 on v2

v3 whole, which is shorter than its diff:
```python
import functools

import jax
import jax.numpy as jnp
from jax import lax
from jax.experimental import pallas as pl
from jax.experimental.pallas import tpu as pltpu
from jax.sharding import PartitionSpec as P

epsilon = 1e-06
f32 = jnp.float32
bf16 = jnp.bfloat16
NT = (((1,), (1,)), ((), ()))
TN = (((0,), (0,)), ((), ()))


def block_of(size, most):
    return max(b for b in range(128, most + 1, 128) if size % b == 0)


def dot(a, b, dims=(((1,), (0,)), ((), ()))):
    return lax.dot_general(a, b, dims, preferred_element_type=f32)


def two_parts(value):
    high = value.astype(bf16)
    low = (value - high.astype(f32)).astype(bf16)
    return jnp.concatenate([high, low], axis=1)


def halves(own, other, half):
    own, other = own.astype(f32), other.astype(f32)
    first = jnp.where(half == 0, own, other)
    second = jnp.where(half == 0, other, own)
    return jnp.concatenate([first, second], axis=0).astype(bf16)


def place_of(shard, half, count):
    return jnp.bitwise_xor(shard, half * (count // 2))


def whole_call(body, args, shapes, scratch=(), flops=0, moved=0, limit=12 << 20):
    one = pl.BlockSpec(memory_space=pltpu.VMEM)
    return pl.pallas_call(
        body,
        in_specs=[one] * len(args),
        out_specs=[one] * len(shapes),
        out_shape=shapes,
        scratch_shapes=scratch,
        compiler_params=pltpu.CompilerParams(vmem_limit_bytes=limit),
        cost_estimate=pl.CostEstimate(flops=flops, bytes_accessed=moved, transcendentals=0),
    )(*args)


def in_hbm(array):
    return pltpu.with_memory_space_constraint(array, pltpu.HBM)


def shaped(shape, dtype):
    return jax.ShapeDtypeStruct(shape, dtype)


def choose_kernel(returned, head, out):
    slot = lax.axis_index("section")
    width = out.shape[1]
    spot = pl.ds(pl.multiple_of((slot % 2) * width, width), width)

    @pl.when(slot < 2)
    def _():
        pltpu.sync_copy(head.at[:, spot], out)

    @pl.when(slot >= 2)
    def _():
        pltpu.sync_copy(returned, out)


def choose(returned, head, hidden):
    return pl.pallas_call(
        choose_kernel,
        in_specs=[pl.BlockSpec(memory_space=pltpu.HBM)] * 2,
        out_specs=pl.BlockSpec(memory_space=pltpu.VMEM),
        out_shape=shaped(returned.shape, bf16),
        name="choose",
        compiler_params=pltpu.CompilerParams(vmem_limit_bytes=4 << 20),
        cost_estimate=pl.CostEstimate(
            flops=hidden, bytes_accessed=2 * returned.size, transcendentals=0
        ),
    )(in_hbm(returned), in_hbm(head))


def forward_kernel(count, rows, nb, xo, xt, yo, yt, ao, at, b, w, *refs):
    outs, (pack, ys, fac) = refs[:count], refs[count : count + 3]
    xs, res = refs[count + 3 :]
    half = lax.axis_index("section") % 2
    me = lax.axis_index("tensor")
    ht = xo.shape[0]
    tokens = 2 * ht
    rank, width = b.shape
    lines, across = pack.shape[0] - rank, pack.shape[1]
    fac[...] = halves(ao[...], at[...], half)
    xs[:ht, :] = xo[...]
    xs[ht:tokens, :] = xt[...]
    xs[tokens:, :] = fac[...]
    ys[:ht, :] = yo[...]
    ys[ht:, :] = yt[...]
    lx = two_parts(dot(xs[:tokens, :], fac[...], NT))
    gram = two_parts(dot(fac[...], fac[...], NT))
    pack[lines:, :] = dot(ys[...], fac[...], NT).T
    for j in range(0, width, nb):
        cut = slice(j, j + nb)
        wv, bv = w[:, cut], b[:, cut]
        both_b = jnp.concatenate([bv, bv], axis=0)
        total = dot(xs[...], wv)
        res[...] = total[:tokens] + dot(lx, both_b)
        wf = wv.astype(f32)
        squares = jnp.sum((wf * wf).reshape(wf.shape[0] // 8, 8, nb), axis=0)
        cross = 2.0 * total[tokens:] + dot(gram, both_b)
        cross = bv.astype(f32) * cross
        for r in range(0, rank, 8):
            squares = squares + cross[r : r + 8]
        squares = jnp.sum(squares, axis=0, keepdims=True)
        for i in range(0, nb, across):
            at_line = (j + i) // across
            pack[at_line : at_line + 1, :] = squares[:, i : i + across]
        for k in range(count):
            at_row = place_of(jnp.bitwise_xor(me, k), half, count) * rows
            piece = res[pl.ds(pl.multiple_of(at_row, rows), rows), :]
            outs[k][:, cut] = piece.astype(outs[k].dtype)


def forward(count, rows, xo, xt, yo, yt, ao, at, b, w):
    ff, width = w.shape
    tokens = 2 * xo.shape[0]
    rank = b.shape[0]
    nb = block_of(width, 512)
    return whole_call(
        functools.partial(forward_kernel, count, rows, nb),
        (xo, xt, yo, yt, ao, at, b, w),
        [shaped((rows, width), f32 if k == 0 else bf16) for k in range(count)]
        + [
            shaped((width // tokens + rank, tokens), f32),
            shaped((tokens, ff), bf16),
            shaped((rank, ff), bf16),
        ],
        [pltpu.VMEM((tokens + rank, ff), bf16), pltpu.VMEM((tokens, nb), f32)],
        2 * tokens * ff * width,
        2 * ff * width,
    )


def again_kernel(nb, ys, pack, b, w, out):
    rank, width = b.shape
    ly = two_parts(pack[pack.shape[0] - rank :, :].T)
    for j in range(0, width, nb):
        cut = slice(j, j + nb)
        both_b = jnp.concatenate([b[:, cut], b[:, cut]], axis=0)
        out[:, cut] = dot(ys[...], w[:, cut]) + dot(ly, both_b)


def again(ys, pack, b, w):
    ff, width = w.shape
    tokens = ys.shape[0]
    return whole_call(
        functools.partial(again_kernel, block_of(width, 512)),
        (ys, pack, b, w),
        [shaped((tokens, width), f32)],
        (),
        2 * tokens * ff * width,
        2 * ff * width,
    )[0]


def join_kernel(one, two, out):
    out[...] = one[...] + two[...]


def join(one, two):
    return whole_call(join_kernel, (one, two), [shaped(one.shape, f32)])[0]


def prepare_kernel(count, rows, *refs):
    cots = refs[:count]
    packs, mag, r, b = refs[count : count + 2], *refs[count + 2 : count + 5]
    sc, ad, adapt, gb, magpack, norms = refs[count + 5 :]
    half = lax.axis_index("section") % 2
    me = lax.axis_index("tensor")
    rank = b.shape[0]
    _, width = sc.shape
    total = packs[0][...] + packs[1][...]
    lines = total.shape[0] - rank
    across = total.shape[1]
    sqr = jnp.sqrt(jnp.maximum(total[:lines], 0.0) + epsilon)
    for i in range(lines):
        norms[0:1, i * across : (i + 1) * across] = sqr[i : i + 1, :]
    scale = mag[...] / norms[0:1, :]
    norms[1:2, :] = scale
    mags = jnp.zeros((8, width), f32)
    for k in range(count):
        at_row = place_of(jnp.bitwise_xor(me, k), half, count) * rows
        spot = pl.ds(pl.multiple_of(at_row, rows), rows)
        cot = cots[k][...].astype(f32)
        sc[spot, :] = (cot * scale).astype(bf16)
        mags = mags + jnp.sum((cot * r[spot, :]).reshape(rows // 8, 8, width), axis=0)
    mags = jnp.sum(mags, axis=0, keepdims=True)
    for i in range(lines):
        magpack[i : i + 1, :] = mags[:, i * across : (i + 1) * across]
    part = dot(sc[...], b[...], NT)
    adapt[...] = part
    ad[...] = two_parts(part)
    gb[...] = dot(total[lines:].astype(bf16), sc[...])


def prepare(count, rows, cots, packs, mag, r, b):
    width = b.shape[1]
    tokens = rows * count
    rank = b.shape[0]
    return whole_call(
        functools.partial(prepare_kernel, count, rows),
        (*cots, *packs, mag, r, b),
        [
            shaped((tokens, width), bf16),
            shaped((tokens, 2 * rank), bf16),
            shaped((tokens, rank), f32),
            shaped((rank, width), f32),
            shaped((width // tokens, tokens), f32),
            shaped((2, width), f32),
        ],
        moved=8 * tokens * width,
    )


def backward_kernel(rb, sc, ad, fac, w, own, send):
    half_tokens = own.shape[0]
    for j in range(0, w.shape[0], rb):
        cut = slice(j, j + rb)
        both_a = jnp.concatenate([fac[:, cut], fac[:, cut]], axis=0)
        out = dot(sc[...], w[cut, :], NT) + dot(ad[...], both_a)
        own[:, cut] = out[:half_tokens]
        send[:, cut] = out[half_tokens:].astype(bf16)


def backward(sc, ad, fac, w):
    ff, width = w.shape
    tokens = sc.shape[0]
    return whole_call(
        functools.partial(backward_kernel, block_of(ff, 512)),
        (sc, ad, fac, w),
        [shaped((tokens // 2, ff), f32), shaped((tokens // 2, ff), bf16)],
        (),
        2 * tokens * ff * width,
        2 * ff * width,
    )


def emit_kernel(count, *refs):
    parts = refs[:count]
    carried, embedded, norms, adapt, got_adapt, ys, out, ga = refs[count:]
    slot = lax.axis_index("section")
    half = slot % 2
    width = out.shape[1]
    here = embedded[:, pl.ds(pl.multiple_of(half * width, width), width)].astype(f32)
    inflow = jnp.where(slot < 2, here, carried[...].astype(f32))
    total = parts[0][...]
    for k in range(1, count):
        total = total + parts[k][...].astype(f32)
    out[...] = (inflow + total * norms[1:2, :]).astype(bf16)
    tokens, rank = adapt.shape
    ht, hr = tokens // 2, rank // 2
    first = adapt[:ht, :] + got_adapt[ht:, :]
    second = adapt[ht:, :] + got_adapt[:ht, :]
    cot = jnp.concatenate([first, second], axis=0)
    cot = jnp.where(half == 0, cot[:, :hr], cot[:, hr:]).astype(bf16)
    ga[...] = dot(cot, ys[...], TN)


def emit(count, parts, carried, embedded, norms, adapt, got_adapt, ys):
    return whole_call(
        functools.partial(emit_kernel, count),
        (*parts, carried, embedded, norms, adapt, got_adapt, ys),
        [shaped(carried.shape, bf16), shaped((adapt.shape[1] // 2, ys.shape[1]), f32)],
        moved=8 * carried.size * 2,
    )


def finish_kernel(count, *refs):
    own, got = refs[:2]
    mags = refs[2 : 2 + count]
    norms = refs[2 + count]
    hidden, gm = refs[3 + count :]
    hidden[...] = (own[...] + got[...].astype(f32)).astype(bf16)
    total = mags[0][...]
    for k in range(1, count):
        total = total + mags[k][...]
    across = total.shape[1]
    for i in range(total.shape[0]):
        cut = slice(i * across, (i + 1) * across)
        gm[:, cut] = total[i : i + 1, :] / norms[0:1, cut]


def finish(count, own, got, mags, norms):
    return whole_call(
        functools.partial(finish_kernel, count),
        (own, got, *mags, norms),
        [shaped(own.shape, bf16), shaped((1, norms.shape[1]), f32)],
        moved=12 * own.size,
    )


def local(
    frozen,
    adapter_a,
    adapter_b,
    magnitude,
    hidden_fwd,
    carried,
    embedded,
    hidden_bwd,
    returned,
    head_grad,
):
    w, ao, b, xo, yo = frozen[0], adapter_a[0], adapter_b[0], hidden_fwd[0], hidden_bwd[0]
    slots = lax.axis_size("section")
    count = lax.axis_size("tensor")
    rows = carried.shape[1]

    def swap(array):
        return lax.ppermute(array, "section", [(i, i ^ 1) for i in range(slots)])

    def across(array, k):
        return lax.ppermute(array, "tensor", [(i, i ^ k) for i in range(count)])

    def shift(array, k):
        pairs = [
            (((s + 2) % slots) * count + t, s * count + (t ^ k))
            for s in range(slots)
            for t in range(count)
        ]
        return lax.ppermute(array, ("section", "tensor"), pairs)

    leaving = choose(returned[0], head_grad, 4 * rows * count * w.size)
    xt, at, yt = swap(xo), swap(ao), swap(yo)
    cots = [None] * count
    for k in range(count):
        direct = k < 2 or k % 2 == 0
        cots[k] = shift(leaving, k) if direct else across(cots[k - 1], 1)
    arriving = lax.ppermute(carried[0], "section", [(i, (i + 2) % slots) for i in range(slots)])
    *parts, pack, ys, fac = forward(count, rows, xo, xt, yo, yt, ao, at, b, w)
    for k in range(1, count):
        parts[k] = across(parts[k], k)
    got = across(pack, 1)
    r = again(ys, pack, b, w)
    for k in (2**n for n in range(1, count.bit_length() - 1)):
        pack = join(pack, got)
        got = across(pack, k)
    sc, ad, adapt, gb, magpack, norms = prepare(
        count, rows, cots, (pack, got), magnitude, r, b
    )
    got_adapt = swap(adapt)
    mags = [magpack]
    for k in range(1, count):
        mags.append(across(magpack, k))
    own, send = backward(sc, ad, fac, w)
    got = swap(send)
    out, ga = emit(count, parts, arriving, embedded, norms, adapt, got_adapt, ys)
    hidden, gm = finish(count, own, got, mags, norms)
    return (out[None], gm, ga[None], gb[None], hidden[None])


def solution(mesh):
    placed = (
        P("section", "tensor", None),
        P("section", None, "tensor"),
        P("section", None, None),
        P("section", None),
        P("section", None, "tensor"),
        P("section", "tensor", None),
        P("tensor", None),
        P("section", None, "tensor"),
        P("section", "tensor", None),
        P("tensor", None),
    )

    return jax.shard_map(
        local,
        mesh=mesh,
        in_specs=placed,
        out_specs=(
            P("section", "tensor", None),
            P("section", None),
            P("section", None, "tensor"),
            P("section", None, None),
            P("section", None, "tensor"),
        ),
        check_vma=False,
    )
```

time: 80.9 us -> 71.2 us (0.88); the launches traced: 79.8 us -> 71 us
  waiting for transfers between devices: 31 us -> 24.9 us
  Pallas kernels: 23.3 us -> 19.9 us
    pallas_call x1 -> x0, Pallas kernels: 8.98 us -> none  [forward(): pl.pallas_call(functools.partial(forward_kernel, count, rows, nb), in_spe...]
    ppermute x2 -> x3, waiting for transfers between devices: 10.8 us -> 4.08 us  [shift(): return lax.ppermute(array, ('section', 'tensor'), pairs)]
    pallas_call x4 -> x7, Pallas kernels: 13.4 us -> 18.8 us  [whole_call(): pl.pallas_call(body, in_specs=[one] * len(args), out_specs=[one] * len(sh...]
    ppermute x1, starting transfers between devices: 4.2 us -> 0.82 us  [local(): lax.ppermute(carried[0], 'section', [(i, (i + 2) % slots) for i in range(...]
    ppermute x11 -> x9, waiting for transfers between devices: 18.5 us -> 15.6 us  [across(): return lax.ppermute(array, 'tensor', [(i, i ^ k) for i in range(count)])]
    ppermute x1, waiting for transfers between devices: 1.75 us -> 3.84 us  [local(): lax.ppermute(carried[0], 'section', [(i, (i + 2) % slots) for i in range(...]
    ppermute x2 -> x3, starting transfers between devices: 6.42 us -> 8.41 us  [shift(): return lax.ppermute(array, ('section', 'tensor'), pairs)]
    ppermute x11 -> x9, starting transfers between devices: 13.5 us -> 15 us  [across(): return lax.ppermute(array, 'tensor', [(i, i ^ k) for i in range(count)])]
  transfers between devices with their start and end apart: 19 -> 18, of which waited for: 7 -> 9; matrix products, arithmetic and copies ran while one was open for 0% -> 0% of each run, Pallas kernels for 19% -> 18%
where the time goes in v3:
time: 71.2 us; the launch traced here: 71 us
  starting transfers between devices  25.4 us (36%)
  waiting for transfers between devices  24.9 us (35%)
  Pallas kernels  19.9 us (28%)
  between operations  0.81 us (1%)
    pallas_call x7, Pallas kernels, whole_call(): pl.pallas_call(body, in_specs=[one] * len(args), out_specs=[one] * len(sh...  18.8 us
    ppermute x9, waiting for transfers between devices, across(): return lax.ppermute(array, 'tensor', [(i, i ^ k) for i in range(count)])  15.6 us
    ppermute x9, starting transfers between devices, across(): return lax.ppermute(array, 'tensor', [(i, i ^ k) for i in range(count)])  15 us
    ppermute x3, starting transfers between devices, shift(): return lax.ppermute(array, ('section', 'tensor'), pairs)  8.41 us
    ppermute x3, waiting for transfers between devices, shift(): return lax.ppermute(array, ('section', 'tensor'), pairs)  4.08 us
    ppermute x1, waiting for transfers between devices, local(): lax.ppermute(carried[0], 'section', [(i, (i + 2) % slots) for i in range(...  3.84 us
  transfers between devices with their start and end apart: 18, of which 9 were waited for; matrix products, arithmetic and copies ran while one was open for 0% of the time, Pallas kernels for 18%

profile of v3, /device:TPU:0, one launch (start us, length us, event | category | flops | bytes accessed | tf_op | source)
XLA Modules:
  0.0 71.0 jit_solution(15522083969129332592)
XLA Ops:
  0.6 0.6 collective-permute-start
  1.2 0.1 collective-permute-start.1
  1.3 0.4 collective-permute-start.2
  1.7 0.0 slice-start
  1.7 0.0 slice-start.1
  1.7 0.0 slice-start.2
  1.7 0.0 slice-start.3
  1.7 0.0 copy-start
  1.7 0.0 copy-start.1
  1.7 0.0 copy-start.2
  1.7 0.0 copy-start.4
  1.8 1.1 %choose.1 = bf16[64,2048]{1,0:T(8,128)(2,1)S(1)} custom-call(bf16[64,2048]{1,0:T(8,128)(2,1)} %bitcast.26, bf16[64,4096]{1,0:T(8,128)(2,1)} %head.1), custom_call_target="tpu_custom_call" | custom-call | flops 7516192768 | bytes 262144 | tf_op jit(solution)/shard_map/choose/pallas_call | solution.py:78
  2.9 5.5 %collective-permute-start.9 = (bf16[64,2048]{1,0:T(8,128)(2,1)S(1)}, bf16[64,2048]{1,0:T(8,128)(2,1)S(1)}, u32[]{:S(2)}, u32[]{:S(2)}) collective-permute-start(bf16[64,2048]{1,0:T(8,128)(2,1)S(1)} %choose.1), channel_id=1, source_target_pairs={{8,2},{9,3},{10,0},{11,1},{12,6},{13,7},{14,4},{15,5},{16,10},{17,... | collective-permute-start | bytes 786440 | tf_op jit(solution)/shard_map/ppermute | solution.py:338
  8.4 0.0 collective-permute-done.2.at
  8.4 0.0 collective-permute-done.xt
  8.4 0.0 collective-permute-done.1.yt
  8.4 0.0 slice-done
  8.4 0.0 slice-done.1
  8.4 0.0 slice-done.2
  8.4 0.0 slice-done.3
  8.5 0.0 copy-done
  8.5 0.0 copy-done.1
  8.5 0.0 copy-done.2
  8.5 0.0 copy-done.4
  8.5 5.7 %shard_map.137 = (f32[64,2048]{1,0:T(8,128)S(1)}, bf16[64,2048]{1,0:T(8,128)(2,1)S(1)}, bf16[64,2048]{1,0:T(8,128)(2,1)S(1)}, bf16[64,2048]{1,0:T(8,128)(2,1)S(1...) custom-call(bf16[128,3584]{1,0:T(8,128)(2,1)S(1)} %bitcast.17, ...), custom_call_target="tpu_custom_call" | custom-call | flops 3758096384 | bytes 14680064 | tf_op jit(solution)/shard_map/pallas_call | solution.py:44
  14.2 1.7 %collective-permute-start.11 = (f32[24,256]{1,0:T(8,128)S(1)}, f32[24,256]{1,0:T(8,128)S(1)}, u32[]{:S(2)}, u32[]{:S(2)}) collective-permute-start(f32[24,256]{1,0:T(8,128)S(1)} %get-tuple-element.28.one.pack), channel_id=1, source_target_pairs={{0,1},{1,0},{2,3},{3,2},{4,5},{5,4},{6,7},{7,6},{8,9},{9,8},{10,11... | collective-permute-start | bytes 73736 | tf_op jit(solution)/shard_map/ppermute | solution.py:330
  15.8 2.5 %collective-permute-start.7 = (bf16[64,2048]{1,0:T(8,128)(2,1)S(1)}, bf16[64,2048]{1,0:T(8,128)(2,1)S(1)}, u32[]{:S(2)}, u32[]{:S(2)}) collective-permute-start(bf16[64,2048]{1,0:T(8,128)(2,1)S(1)} %choose.1), channel_id=1, source_target_pairs={{8,0},{9,1},{10,2},{11,3},{12,4},{13,5},{14,6},{15,7},{16,8},{17,9... | collective-permute-start | bytes 786440 | tf_op jit(solution)/shard_map/ppermute | solution.py:338
  18.3 0.4 collective-permute-start.8
  18.7 1.4 %collective-permute-done.9.refs_2_ = bf16[64,2048]{1,0:T(8,128)(2,1)S(1)} collective-permute-done((bf16[64,2048]{1,0:T(8,128)(2,1)S(1)}, bf16[64,2048]{1,0:T(8,128)(2,1)S(1)}, u32[]{:S(2)}, u32[]{:S(2)}) %collective-permute-start.9) | collective-permute-done | bytes 262176 | tf_op jit(solution)/shard_map/ppermute | solution.py:338
  20.1 1.6 %collective-permute-start.10 = (bf16[64,2048]{1,0:T(8,128)(2,1)S(1)}, bf16[64,2048]{1,0:T(8,128)(2,1)S(1)}, u32[]{:S(2)}, u32[]{:S(2)}) collective-permute-start(bf16[64,2048]{1,0:T(8,128)(2,1)S(1)} %collective-permute-done.9.refs_2_), channel_id=1, source_target_pairs={{0,1},{1,0},{2,3},{3,2},{4,5},{5,4},{6,7},{7,6},{8,9},{9,8},{10,11... | collective-permute-start | bytes 786440 | tf_op jit(solution)/shard_map/ppermute | solution.py:330
  21.7 0.0 collective-permute-done.11.two
  21.7 2.5 %collective-permute-start.12 = (f32[24,256]{1,0:T(8,128)S(1)}, f32[24,256]{1,0:T(8,128)S(1)}, u32[]{:S(2)}, u32[]{:S(2)}) collective-permute-start(f32[24,256]{1,0:T(8,128)S(1)} %shard_map.138.refs_4_), channel_id=1, source_target_pairs={{0,2},{1,3},{2,0},{3,1},{4,6},{5,7},{6,4},{7,5},{8,10},{9,11},{10,... | collective-permute-start | bytes 73736 | tf_op jit(solution)/shard_map/ppermute | solution.py:330
  24.2 0.0 copy-start.5
  24.2 4.4 %shard_map.139.refs_7_ = f32[256,2048]{1,0:T(8,128)S(1)} custom-call(bf16[256,3584]{1,0:T(8,128)(2,1)S(1)} %get-tuple-element.29.ys.refs_9_, f32[24,256]{1,0:T(8,128)S(1)} %get-tuple-element.28.one.pack, bf16[16,2048]{1,0:T(8,128)(2,1)S(1)} %bitcast.21, bf16[3584,2048]{1,0:T(8,128)(2,1)S(1)} %bitcast.14), custom_call_target="tpu_custom_call" | custom-call | flops 3758096384 | bytes 14680064 | tf_op jit(solution)/shard_map/pallas_call | solution.py:44
  28.6 2.7 %collective-permute-done.7.refs_0_ = bf16[64,2048]{1,0:T(8,128)(2,1)S(1)} collective-permute-done((bf16[64,2048]{1,0:T(8,128)(2,1)S(1)}, bf16[64,2048]{1,0:T(8,128)(2,1)S(1)}, u32[]{:S(2)}, u32[]{:S(2)}) %collective-permute-start.7) | collective-permute-done | bytes 262176 | tf_op jit(solution)/shard_map/ppermute | solution.py:338
  31.3 0.0 collective-permute-done.8.refs_1_
  31.3 2.0 %collective-permute-done.10.refs_3_ = bf16[64,2048]{1,0:T(8,128)(2,1)S(1)} collective-permute-done((bf16[64,2048]{1,0:T(8,128)(2,1)S(1)}, bf16[64,2048]{1,0:T(8,128)(2,1)S(1)}, u32[]{:S(2)}, u32[]{:S(2)}) %collective-permute-start.10) | collective-permute-done | bytes 262176 | tf_op jit(solution)/shard_map/ppermute | solution.py:330
  33.3 0.0 collective-permute-done.12.refs_5_
  33.3 0.0 copy-done.5
  33.3 1.9 %shard_map.140 = (bf16[256,2048]{1,0:T(8,128)(2,1)S(1)}, bf16[256,32]{1,0:T(8,128)(2,1)S(1)}, f32[256,16]{1,0:T(8,128)S(1)}, f32[16,2048]{1,0:T(8,128)}, f32[8,256]{1,0:T(8,128)S(1)}, /*index=5*/f32[2,2048]{1,0:T(2,128)S(1)}) custom-call(bf16[64,2048]{1,0:T(8,128)(2,1)S(1)} %collective-permute-done.7.refs_0_, ...), custom_call_target="tpu_custom_call" | custom-call | bytes 4194304 | tf_op jit(solution)/shard_map/pallas_call | solution.py:44
  35.1 0.0 copy-start.6
  35.1 4.4 %shard_map.142 = (f32[128,3584]{1,0:T(8,128)S(1)}, bf16[128,3584]{1,0:T(8,128)(2,1)S(1)}) custom-call(bf16[256,2048]{1,0:T(8,128)(2,1)S(1)} %get-tuple-element.33.sc, bf16[256,32]{1,0:T(8,128)(2,1)S(1)} %get-tuple-element.34.ad, bf16[16,3584]{1,0:T(8,128)(2,1)S(1)} %get-tuple-element.35.fac, bf16[3584,2048]{1,0:T(8,128)(2,1)S(1)} %bitcast.15), custom_call_target="tpu_custom_call" | custom-call | flops 3758096384 | bytes 14680064 | tf_op jit(solution)/shard_map/pallas_call | solution.py:44
  39.5 0.1 collective-permute-start.14
  39.6 0.0 copy-done.6
  39.6 0.8 %collective-permute-start.6 = (bf16[64,2048]{1,0:T(8,128)(2,1)S(1)}, bf16[64,2048]{1,0:T(8,128)(2,1)S(1)}, u32[]{:S(2)}, u32[]{:S(2)}) collective-permute-start(bf16[64,2048]{1,0:T(8,128)(2,1)S(1)} %bitcast.27), channel_id=1, source_target_pairs={{0,8},{4,12},{8,16},{12,20},{16,24},{20,28},{24,0},{28,4},{1,9},{5... | collective-permute-start | bytes 786440 | tf_op jit(solution)/shard_map/ppermute | solution.py:346
  40.4 2.6 %collective-permute-start.3 = (bf16[64,2048]{1,0:T(8,128)(2,1)S(1)}, bf16[64,2048]{1,0:T(8,128)(2,1)S(1)}, u32[]{:S(2)}, u32[]{:S(2)}) collective-permute-start(bf16[64,2048]{1,0:T(8,128)(2,1)S(1)} %get-tuple-element.25), channel_id=1, source_target_pairs={{0,1},{1,0},{2,3},{3,2},{4,5},{5,4},{6,7},{7,6},{8,9},{9,8},{10,11... | collective-permute-start | bytes 786440 | tf_op jit(solution)/shard_map/ppermute | solution.py:330
  43.0 1.1 %collective-permute-start.4 = (bf16[64,2048]{1,0:T(8,128)(2,1)S(1)}, bf16[64,2048]{1,0:T(8,128)(2,1)S(1)}, u32[]{:S(2)}, u32[]{:S(2)}) collective-permute-start(bf16[64,2048]{1,0:T(8,128)(2,1)S(1)} %get-tuple-element.26), channel_id=1, source_target_pairs={{0,2},{1,3},{2,0},{3,1},{4,6},{5,7},{6,4},{7,5},{8,10},{9,11},{10,... | collective-permute-start | bytes 786440 | tf_op jit(solution)/shard_map/ppermute | solution.py:330
  44.1 1.3 %collective-permute-start.5 = (bf16[64,2048]{1,0:T(8,128)(2,1)S(1)}, bf16[64,2048]{1,0:T(8,128)(2,1)S(1)}, u32[]{:S(2)}, u32[]{:S(2)}) collective-permute-start(bf16[64,2048]{1,0:T(8,128)(2,1)S(1)} %get-tuple-element.27), channel_id=1, source_target_pairs={{0,3},{1,2},{2,1},{3,0},{4,7},{5,6},{6,5},{7,4},{8,11},{9,10},{10,... | collective-permute-start | bytes 786440 | tf_op jit(solution)/shard_map/ppermute | solution.py:330
  45.4 3.8 %collective-permute-done.6.refs_4_ = bf16[64,2048]{1,0:T(8,128)(2,1)S(1)} collective-permute-done((bf16[64,2048]{1,0:T(8,128)(2,1)S(1)}, bf16[64,2048]{1,0:T(8,128)(2,1)S(1)}, u32[]{:S(2)}, u32[]{:S(2)}) %collective-permute-start.6) | collective-permute-done | bytes 262176 | tf_op jit(solution)/shard_map/ppermute | solution.py:346
  49.2 0.0 collective-permute-start.13
  49.2 1.3 %collective-permute-done.13.refs_8_ = f32[256,16]{1,0:T(8,128)S(1)} collective-permute-done((f32[256,16]{1,0:T(8,128)S(1)}, f32[256,16]{1,0:T(8,128)S(1)}, u32[]{:S(2)}, u32[]{:S(2)}) %collective-permute-start.13) | collective-permute-done | bytes 16416 | tf_op jit(solution)/shard_map/ppermute | solution.py:327
  50.6 1.9 %collective-permute-start.15 = (f32[8,256]{1,0:T(8,128)S(1)}, f32[8,256]{1,0:T(8,128)S(1)}, u32[]{:S(2)}, u32[]{:S(2)}) collective-permute-start(f32[8,256]{1,0:T(8,128)S(1)} %get-tuple-element.38.refs_2_), channel_id=1, source_target_pairs={{0,1},{1,0},{2,3},{3,2},{4,5},{5,4},{6,7},{7,6},{8,9},{9,8},{10,11... | collective-permute-start | bytes 24584 | tf_op jit(solution)/shard_map/ppermute | solution.py:330
  52.4 1.5 %collective-permute-done.3.refs_1_ = bf16[64,2048]{1,0:T(8,128)(2,1)S(1)} collective-permute-done((bf16[64,2048]{1,0:T(8,128)(2,1)S(1)}, bf16[64,2048]{1,0:T(8,128)(2,1)S(1)}, u32[]{:S(2)}, u32[]{:S(2)}) %collective-permute-start.3) | collective-permute-done | bytes 262176 | tf_op jit(solution)/shard_map/ppermute | solution.py:330
  54.0 1.2 %collective-permute-start.16 = (f32[8,256]{1,0:T(8,128)S(1)}, f32[8,256]{1,0:T(8,128)S(1)}, u32[]{:S(2)}, u32[]{:S(2)}) collective-permute-start(f32[8,256]{1,0:T(8,128)S(1)} %get-tuple-element.38.refs_2_), channel_id=1, source_target_pairs={{0,2},{1,3},{2,0},{3,1},{4,6},{5,7},{6,4},{7,5},{8,10},{9,11},{10,... | collective-permute-start | bytes 24584 | tf_op jit(solution)/shard_map/ppermute | solution.py:330
  55.2 9.3 %collective-permute-done.4.refs_2_ = bf16[64,2048]{1,0:T(8,128)(2,1)S(1)} collective-permute-done((bf16[64,2048]{1,0:T(8,128)(2,1)S(1)}, bf16[64,2048]{1,0:T(8,128)(2,1)S(1)}, u32[]{:S(2)}, u32[]{:S(2)}) %collective-permute-start.4) | collective-permute-done | bytes 262176 | tf_op jit(solution)/shard_map/ppermute | solution.py:330
  64.5 1.2 %collective-permute-start.17 = (f32[8,256]{1,0:T(8,128)S(1)}, f32[8,256]{1,0:T(8,128)S(1)}, u32[]{:S(2)}, u32[]{:S(2)}) collective-permute-start(f32[8,256]{1,0:T(8,128)S(1)} %get-tuple-element.38.refs_2_), channel_id=1, source_target_pairs={{0,3},{1,2},{2,1},{3,0},{4,7},{5,6},{6,5},{7,4},{8,11},{9,10},{10,... | collective-permute-start | bytes 24584 | tf_op jit(solution)/shard_map/ppermute | solution.py:330
  65.7 0.0 collective-permute-done.5.refs_3_
  65.7 0.0 copy-done.3
  65.7 1.4 %shard_map.141 = (bf16[64,2048]{1,0:T(8,128)(2,1)}, f32[8,3584]{1,0:T(8,128)}) custom-call(f32[64,2048]{1,0:T(8,128)S(1)} %get-tuple-element.24.refs_0_, bf16[64,2048]{1,0:T(8,128)(2,1)S(1)} %collective-permute-done.3.refs_1_, bf16[64,2048]{1,0:T(8,128)(2,1)S(1)} %collective-permute-done.4.refs_2_, bf16[64,2048]{1,0:T(8,128)(2,1)S(1)} %collective-permute-done.5.refs_3_, ...), custom_call_target="tpu_custom_call" | custom-call | bytes 2097152 | tf_op jit(solution)/shard_map/pallas_call | solution.py:44
  67.1 0.0 collective-permute-done.15.refs_3_
  67.1 2.3 %collective-permute-done.16.refs_4_ = f32[8,256]{1,0:T(8,128)S(1)} collective-permute-done((f32[8,256]{1,0:T(8,128)S(1)}, f32[8,256]{1,0:T(8,128)S(1)}, u32[]{:S(2)}, u32[]{:S(2)}) %collective-permute-start.16) | collective-permute-done | bytes 8224 | tf_op jit(solution)/shard_map/ppermute | solution.py:330
  69.4 0.5 collective-permute-done.17.refs_5_
  70.0 0.0 collective-permute-done.14.refs_1_
  70.0 1.1 %shard_map.143 = (bf16[128,3584]{1,0:T(8,128)(2,1)}, f32[1,2048]{1,0:T(1,128)}) custom-call(f32[128,3584]{1,0:T(8,128)S(1)} %get-tuple-element.36.refs_0_, bf16[128,3584]{1,0:T(8,128)(2,1)S(1)} %collective-permute-done.14.refs_1_, f32[8,256]{1,0:T(8,128)S(1)} %get-tuple-element.38.refs_2_, f32[8,256]{1,0:T(8,128)S(1)} %collective-permute-done.15.refs_3_, ...), custom_call_target="tpu_custom_call" | custom-call | bytes 5505024 | tf_op jit(solution)/shard_map/pallas_call | solution.py:44
  (3 shorter events, 0.0 us)
Async XLA Ops:
  0.6 7.8 %collective-permute-start = (bf16[128,3584]{1,0:T(8,128)(2,1)}, bf16[128,3584]{1,0:T(8,128)(2,1)S(1)}, u32[]{:S(2)}, u32[]{:S(2)}) collective-permute-start(bf16[128,3584]{1,0:T(8,128)(2,1)} %bitcast.16), channel_id=1, source_target_pairs={{0,4},{4,0},{8,12},{12,8},{16,20},{20,16},{24,28},{28,24},{1,5},{5... | collective-permute-start | bytes 2752520 | tf_op jit(solution)/shard_map/ppermute | solution.py:327
  1.2 7.2 %collective-permute-start.1 = (bf16[128,3584]{1,0:T(8,128)(2,1)}, bf16[128,3584]{1,0:T(8,128)(2,1)S(1)}, u32[]{:S(2)}, u32[]{:S(2)}) collective-permute-start(bf16[128,3584]{1,0:T(8,128)(2,1)} %bitcast.18), channel_id=1, source_target_pairs={{0,4},{4,0},{8,12},{12,8},{16,20},{20,16},{24,28},{28,24},{1,5},{5... | collective-permute-start | bytes 2752520 | tf_op jit(solution)/shard_map/ppermute | solution.py:327
  1.3 7.1 %collective-permute-start.2 = (bf16[8,3584]{1,0:T(8,128)(2,1)}, bf16[8,3584]{1,0:T(8,128)(2,1)S(1)}, u32[]{:S(2)}, u32[]{:S(2)}) collective-permute-start(bf16[8,3584]{1,0:T(8,128)(2,1)} %bitcast.23), channel_id=1, source_target_pairs={{0,4},{4,0},{8,12},{12,8},{16,20},{20,16},{24,28},{28,24},{1,5},{5... | collective-permute-start | bytes 172040 | tf_op jit(solution)/shard_map/ppermute | solution.py:327
  1.7 6.7 %slice-start = ((s8[14680064]{0:T(1024)(128)(4,1)}), s8[4194304]{0:T(1024)(128)(4,1)S(1)}, s32[]{:S(2)}) async-start(s8[14680064]{0:T(1024)(128)(4,1)} %bitcast.11), calls=%async_computation | async-start | bytes 8388608
  1.7 6.7 %slice-start.1 = ((s8[14680064]{0:T(1024)(128)(4,1)}), s8[4194304]{0:T(1024)(128)(4,1)S(1)}, s32[]{:S(2)}) async-start(s8[14680064]{0:T(1024)(128)(4,1)} %bitcast.11), calls=%async_computation.1 | async-start | bytes 8388608
  1.7 6.7 %slice-start.2 = ((s8[14680064]{0:T(1024)(128)(4,1)}), s8[4194304]{0:T(1024)(128)(4,1)S(1)}, s32[]{:S(2)}) async-start(s8[14680064]{0:T(1024)(128)(4,1)} %bitcast.11), calls=%async_computation.2 | async-start | bytes 8388608
  1.7 6.7 %slice-start.3 = ((s8[14680064]{0:T(1024)(128)(4,1)}), s8[2097152]{0:T(1024)(128)(4,1)S(1)}, s32[]{:S(2)}) async-start(s8[14680064]{0:T(1024)(128)(4,1)} %bitcast.11), calls=%async_computation.3 | async-start | bytes 4194304
  1.7 6.7 %copy-start = (bf16[1,128,3584]{2,1,0:T(8,128)(2,1)S(1)}, bf16[1,128,3584]{2,1,0:T(8,128)(2,1)}, u32[]{:S(2)}) copy-start(bf16[1,128,3584]{2,1,0:T(8,128)(2,1)} %param.14) | copy-start | bytes 2752516
  1.7 6.7 %copy-start.1 = (bf16[1,128,3584]{2,1,0:T(8,128)(2,1)S(1)}, bf16[1,128,3584]{2,1,0:T(8,128)(2,1)}, u32[]{:S(2)}) copy-start(bf16[1,128,3584]{2,1,0:T(8,128)(2,1)} %param.17) | copy-start | bytes 2752516
  1.7 6.7 %copy-start.2 = (bf16[1,16,2048]{2,1,0:T(8,128)(2,1)S(1)}, bf16[1,16,2048]{2,1,0:T(8,128)(2,1)}, u32[]{:S(2)}) copy-start(bf16[1,16,2048]{2,1,0:T(8,128)(2,1)} %param.12) | copy-start | bytes 196612
  1.7 6.7 %copy-start.4 = (bf16[1,8,3584]{2,1,0:T(8,128)(2,1)S(1)}, bf16[1,8,3584]{2,1,0:T(8,128)(2,1)}, u32[]{:S(2)}) copy-start(bf16[1,8,3584]{2,1,0:T(8,128)(2,1)} %param.11) | copy-start | bytes 172036
  2.9 17.2 %collective-permute-start.9 = (bf16[64,2048]{1,0:T(8,128)(2,1)S(1)}, bf16[64,2048]{1,0:T(8,128)(2,1)S(1)}, u32[]{:S(2)}, u32[]{:S(2)}) collective-permute-start(bf16[64,2048]{1,0:T(8,128)(2,1)S(1)} %choose.1), channel_id=1, source_target_pairs={{8,2},{9,3},{10,0},{11,1},{12,6},{13,7},{14,4},{15,5},{16,10},{17,... | collective-permute-start | bytes 786440 | tf_op jit(solution)/shard_map/ppermute | solution.py:338
  14.2 7.5 %collective-permute-start.11 = (f32[24,256]{1,0:T(8,128)S(1)}, f32[24,256]{1,0:T(8,128)S(1)}, u32[]{:S(2)}, u32[]{:S(2)}) collective-permute-start(f32[24,256]{1,0:T(8,128)S(1)} %get-tuple-element.28.one.pack), channel_id=1, source_target_pairs={{0,1},{1,0},{2,3},{3,2},{4,5},{5,4},{6,7},{7,6},{8,9},{9,8},{10,11... | collective-permute-start | bytes 73736 | tf_op jit(solution)/shard_map/ppermute | solution.py:330
  15.8 15.5 %collective-permute-start.7 = (bf16[64,2048]{1,0:T(8,128)(2,1)S(1)}, bf16[64,2048]{1,0:T(8,128)(2,1)S(1)}, u32[]{:S(2)}, u32[]{:S(2)}) collective-permute-start(bf16[64,2048]{1,0:T(8,128)(2,1)S(1)} %choose.1), channel_id=1, source_target_pairs={{8,0},{9,1},{10,2},{11,3},{12,4},{13,5},{14,6},{15,7},{16,8},{17,9... | collective-permute-start | bytes 786440 | tf_op jit(solution)/shard_map/ppermute | solution.py:338
  18.3 13.0 %collective-permute-start.8 = (bf16[64,2048]{1,0:T(8,128)(2,1)S(1)}, bf16[64,2048]{1,0:T(8,128)(2,1)S(1)}, u32[]{:S(2)}, u32[]{:S(2)}) collective-permute-start(bf16[64,2048]{1,0:T(8,128)(2,1)S(1)} %choose.1), channel_id=1, source_target_pairs={{8,1},{9,0},{10,3},{11,2},{12,5},{13,4},{14,7},{15,6},{16,9},{17,8... | collective-permute-start | bytes 786440 | tf_op jit(solution)/shard_map/ppermute | solution.py:338
  20.1 13.2 %collective-permute-start.10 = (bf16[64,2048]{1,0:T(8,128)(2,1)S(1)}, bf16[64,2048]{1,0:T(8,128)(2,1)S(1)}, u32[]{:S(2)}, u32[]{:S(2)}) collective-permute-start(bf16[64,2048]{1,0:T(8,128)(2,1)S(1)} %collective-permute-done.9.refs_2_), channel_id=1, source_target_pairs={{0,1},{1,0},{2,3},{3,2},{4,5},{5,4},{6,7},{7,6},{8,9},{9,8},{10,11... | collective-permute-start | bytes 786440 | tf_op jit(solution)/shard_map/ppermute | solution.py:330
  21.7 11.5 %collective-permute-start.12 = (f32[24,256]{1,0:T(8,128)S(1)}, f32[24,256]{1,0:T(8,128)S(1)}, u32[]{:S(2)}, u32[]{:S(2)}) collective-permute-start(f32[24,256]{1,0:T(8,128)S(1)} %shard_map.138.refs_4_), channel_id=1, source_target_pairs={{0,2},{1,3},{2,0},{3,1},{4,6},{5,7},{6,4},{7,5},{8,10},{9,11},{10,... | collective-permute-start | bytes 73736 | tf_op jit(solution)/shard_map/ppermute | solution.py:330
  24.2 9.1 %copy-start.5 = (f32[1,2048]{1,0:T(1,128)S(1)}, f32[1,2048]{1,0:T(1,128)}, u32[]{:S(2)}) copy-start(f32[1,2048]{1,0:T(1,128)} %refs_6_.1) | copy-start | bytes 24580
  35.1 4.5 %copy-start.6 = (bf16[1,64,2048]{2,1,0:T(8,128)(2,1)S(1)}, bf16[1,64,2048]{2,1,0:T(8,128)(2,1)}, u32[]{:S(2)}) copy-start(bf16[1,64,2048]{2,1,0:T(8,128)(2,1)} %param.15) | copy-start | bytes 786436
  35.1 30.6 %copy-start.3 = (bf16[64,4096]{1,0:T(8,128)(2,1)S(1)}, bf16[64,4096]{1,0:T(8,128)(2,1)}, u32[]{:S(2)}) copy-start(bf16[64,4096]{1,0:T(8,128)(2,1)} %refs_5_.1) | copy-start | bytes 1572868
  39.5 30.4 %collective-permute-start.14 = (bf16[128,3584]{1,0:T(8,128)(2,1)S(1)}, bf16[128,3584]{1,0:T(8,128)(2,1)S(1)}, u32[]{:S(2)}, u32[]{:S(2)}) collective-permute-start(bf16[128,3584]{1,0:T(8,128)(2,1)S(1)} %get-tuple-element.37), channel_id=1, source_target_pairs={{0,4},{4,0},{8,12},{12,8},{16,20},{20,16},{24,28},{28,24},{1,5},{5... | collective-permute-start | bytes 2752520 | tf_op jit(solution)/shard_map/ppermute | solution.py:327
  39.6 9.6 %collective-permute-start.6 = (bf16[64,2048]{1,0:T(8,128)(2,1)S(1)}, bf16[64,2048]{1,0:T(8,128)(2,1)S(1)}, u32[]{:S(2)}, u32[]{:S(2)}) collective-permute-start(bf16[64,2048]{1,0:T(8,128)(2,1)S(1)} %bitcast.27), channel_id=1, source_target_pairs={{0,8},{4,12},{8,16},{12,20},{16,24},{20,28},{24,0},{28,4},{1,9},{5... | collective-permute-start | bytes 786440 | tf_op jit(solution)/shard_map/ppermute | solution.py:346
  40.4 13.5 %collective-permute-start.3 = (bf16[64,2048]{1,0:T(8,128)(2,1)S(1)}, bf16[64,2048]{1,0:T(8,128)(2,1)S(1)}, u32[]{:S(2)}, u32[]{:S(2)}) collective-permute-start(bf16[64,2048]{1,0:T(8,128)(2,1)S(1)} %get-tuple-element.25), channel_id=1, source_target_pairs={{0,1},{1,0},{2,3},{3,2},{4,5},{5,4},{6,7},{7,6},{8,9},{9,8},{10,11... | collective-permute-start | bytes 786440 | tf_op jit(solution)/shard_map/ppermute | solution.py:330
  43.0 21.5 %collective-permute-start.4 = (bf16[64,2048]{1,0:T(8,128)(2,1)S(1)}, bf16[64,2048]{1,0:T(8,128)(2,1)S(1)}, u32[]{:S(2)}, u32[]{:S(2)}) collective-permute-start(bf16[64,2048]{1,0:T(8,128)(2,1)S(1)} %get-tuple-element.26), channel_id=1, source_target_pairs={{0,2},{1,3},{2,0},{3,1},{4,6},{5,7},{6,4},{7,5},{8,10},{9,11},{10,... | collective-permute-start | bytes 786440 | tf_op jit(solution)/shard_map/ppermute | solution.py:330
  44.1 21.6 %collective-permute-start.5 = (bf16[64,2048]{1,0:T(8,128)(2,1)S(1)}, bf16[64,2048]{1,0:T(8,128)(2,1)S(1)}, u32[]{:S(2)}, u32[]{:S(2)}) collective-permute-start(bf16[64,2048]{1,0:T(8,128)(2,1)S(1)} %get-tuple-element.27), channel_id=1, source_target_pairs={{0,3},{1,2},{2,1},{3,0},{4,7},{5,6},{6,5},{7,4},{8,11},{9,10},{10,... | collective-permute-start | bytes 786440 | tf_op jit(solution)/shard_map/ppermute | solution.py:330
  49.2 1.3 %collective-permute-start.13 = (f32[256,16]{1,0:T(8,128)S(1)}, f32[256,16]{1,0:T(8,128)S(1)}, u32[]{:S(2)}, u32[]{:S(2)}) collective-permute-start(f32[256,16]{1,0:T(8,128)S(1)} %get-tuple-element.31.refs_7_), channel_id=1, source_target_pairs={{0,4},{4,0},{8,12},{12,8},{16,20},{20,16},{24,28},{28,24},{1,5},{5... | collective-permute-start | bytes 49160 | tf_op jit(solution)/shard_map/ppermute | solution.py:327
  50.6 16.6 %collective-permute-start.15 = (f32[8,256]{1,0:T(8,128)S(1)}, f32[8,256]{1,0:T(8,128)S(1)}, u32[]{:S(2)}, u32[]{:S(2)}) collective-permute-start(f32[8,256]{1,0:T(8,128)S(1)} %get-tuple-element.38.refs_2_), channel_id=1, source_target_pairs={{0,1},{1,0},{2,3},{3,2},{4,5},{5,4},{6,7},{7,6},{8,9},{9,8},{10,11... | collective-permute-start | bytes 24584 | tf_op jit(solution)/shard_map/ppermute | solution.py:330
  54.0 15.5 %collective-permute-start.16 = (f32[8,256]{1,0:T(8,128)S(1)}, f32[8,256]{1,0:T(8,128)S(1)}, u32[]{:S(2)}, u32[]{:S(2)}) collective-permute-start(f32[8,256]{1,0:T(8,128)S(1)} %get-tuple-element.38.refs_2_), channel_id=1, source_target_pairs={{0,2},{1,3},{2,0},{3,1},{4,6},{5,7},{6,4},{7,5},{8,10},{9,11},{10,... | collective-permute-start | bytes 24584 | tf_op jit(solution)/shard_map/ppermute | solution.py:330
  64.5 5.4 %collective-permute-start.17 = (f32[8,256]{1,0:T(8,128)S(1)}, f32[8,256]{1,0:T(8,128)S(1)}, u32[]{:S(2)}, u32[]{:S(2)}) collective-permute-start(f32[8,256]{1,0:T(8,128)S(1)} %get-tuple-element.38.refs_2_), channel_id=1, source_target_pairs={{0,3},{1,2},{2,1},{3,0},{4,7},{5,6},{6,5},{7,4},{8,11},{9,10},{10,... | collective-permute-start | bytes 24584 | tf_op jit(solution)/shard_map/ppermute | solution.py:330

commit v4 on v3

--- a/solution.py
+++ b/solution.py
@@ -181,7 +181,7 @@
 def prepare_kernel(count, rows, *refs):
     cots = refs[:count]
     packs, mag, r, b = refs[count : count + 2], *refs[count + 2 : count + 5]
-    sc, ad, adapt, gb, magpack, norms = refs[count + 5 :]
+    sc, ad, adapt, low, magpack, norms = refs[count + 5 :]
     half = lax.axis_index("section") % 2
     me = lax.axis_index("tensor")
     rank = b.shape[0]
@@ -207,7 +207,7 @@
     part = dot(sc[...], b[...], NT)
     adapt[...] = part
     ad[...] = two_parts(part)
-    gb[...] = dot(total[lines:].astype(bf16), sc[...])
+    low[...] = total[lines:].astype(bf16)
 
 
 def prepare(count, rows, cots, packs, mag, r, b):
@@ -221,7 +221,7 @@
             shaped((tokens, width), bf16),
             shaped((tokens, 2 * rank), bf16),
             shaped((tokens, rank), f32),
-            shaped((rank, width), f32),
+            shaped((rank, tokens), bf16),
             shaped((width // tokens, tokens), f32),
             shaped((2, width), f32),
         ],
@@ -254,7 +254,7 @@
 
 def emit_kernel(count, *refs):
     parts = refs[:count]
-    carried, embedded, norms, adapt, got_adapt, ys, out, ga = refs[count:]
+    carried, embedded, norms, adapt, got_adapt, ys, low, sc, out, ga, gb = refs[count:]
     slot = lax.axis_index("section")
     half = slot % 2
     width = out.shape[1]
@@ -271,13 +271,18 @@
     cot = jnp.concatenate([first, second], axis=0)
     cot = jnp.where(half == 0, cot[:, :hr], cot[:, hr:]).astype(bf16)
     ga[...] = dot(cot, ys[...], TN)
-
-
-def emit(count, parts, carried, embedded, norms, adapt, got_adapt, ys):
+    gb[...] = dot(low[...], sc[...])
+
+
+def emit(count, parts, carried, embedded, norms, adapt, got_adapt, ys, low, sc):
     return whole_call(
         functools.partial(emit_kernel, count),
-        (*parts, carried, embedded, norms, adapt, got_adapt, ys),
-        [shaped(carried.shape, bf16), shaped((adapt.shape[1] // 2, ys.shape[1]), f32)],
+        (*parts, carried, embedded, norms, adapt, got_adapt, ys, low, sc),
+        [
+            shaped(carried.shape, bf16),
+            shaped((adapt.shape[1] // 2, ys.shape[1]), f32),
+            shaped((adapt.shape[1], sc.shape[1]), f32),
+        ],
         moved=8 * carried.size * 2,
     )
 
@@ -352,7 +357,7 @@
     for k in (2**n for n in range(1, count.bit_length() - 1)):
         pack = join(pack, got)
         got = across(pack, k)
-    sc, ad, adapt, gb, magpack, norms = prepare(
+    sc, ad, adapt, low, magpack, norms = prepare(
         count, rows, cots, (pack, got), magnitude, r, b
     )
     got_adapt = swap(adapt)
@@ -361,7 +366,9 @@
         mags.append(across(magpack, k))
     own, send = backward(sc, ad, fac, w)
     got = swap(send)
-    out, ga = emit(count, parts, arriving, embedded, norms, adapt, got_adapt, ys)
+    out, ga, gb = emit(
+        count, parts, arriving, embedded, norms, adapt, got_adapt, ys, low, sc
+    )
     hidden, gm = finish(count, own, got, mags, norms)
     return (out[None], gm, ga[None], gb[None], hidden[None])
 

time: 71.2 us -> 68.7 us (0.965)
  starting transfers between devices: 25.4 us -> 24.3 us
  waiting for transfers between devices: 24.9 us -> 24.1 us
    ppermute x9, waiting for transfers between devices: 15.6 us -> 13.6 us  [across(): return lax.ppermute(array, 'tensor', [(i, i ^ k) for i in range(count)])]
    ppermute x1, waiting for transfers between devices: 3.84 us -> 4.7 us  [local(): lax.ppermute(carried[0], 'section', [(i, (i + 2) % slots) for i in range(...]
    ppermute x9, starting transfers between devices: 15 us -> 14.2 us  [across(): return lax.ppermute(array, 'tensor', [(i, i ^ k) for i in range(count)])]
  transfers between devices with their start and end apart: 18 -> 18, of which waited for: 9 -> 7; matrix products, arithmetic and copies ran while one was open for 0% -> 0% of each run, Pallas kernels for 18% -> 19%
where the time goes in v4:
time: 68.7 us; the launch traced here: 68.6 us
  starting transfers between devices  24.3 us (35%)
  waiting for transfers between devices  24.1 us (35%)
  Pallas kernels  19.4 us (28%)
  between operations  0.82 us (1%)
    pallas_call x7, Pallas kernels, whole_call(): pl.pallas_call(body, in_specs=[one] * len(args), out_specs=[one] * len(sh...  18.2 us
    ppermute x9, starting transfers between devices, across(): return lax.ppermute(array, 'tensor', [(i, i ^ k) for i in range(count)])  14.2 us
    ppermute x9, waiting for transfers between devices, across(): return lax.ppermute(array, 'tensor', [(i, i ^ k) for i in range(count)])  13.6 us
    ppermute x3, starting transfers between devices, shift(): return lax.ppermute(array, ('section', 'tensor'), pairs)  8.4 us
    ppermute x1, waiting for transfers between devices, local(): lax.ppermute(carried[0], 'section', [(i, (i + 2) % slots) for i in range(...  4.7 us
    ppermute x3, waiting for transfers between devices, shift(): return lax.ppermute(array, ('section', 'tensor'), pairs)  4.46 us
  transfers between devices with their start and end apart: 18, of which 7 were waited for; matrix products, arithmetic and copies ran while one was open for 0% of the time, Pallas kernels for 19%

profile of v4, /device:TPU:0, one launch (start us, length us, event | category | flops | bytes accessed | tf_op | source)
XLA Modules:
  0.0 68.6 jit_solution(12227641714020895228)
XLA Ops:
  0.6 0.6 collective-permute-start
  1.2 0.1 collective-permute-start.1
  1.3 0.4 collective-permute-start.2
  1.7 0.0 slice-start
  1.7 0.0 slice-start.1
  1.7 0.0 slice-start.2
  1.7 0.0 slice-start.3
  1.7 0.0 copy-start
  1.7 0.0 copy-start.1
  1.7 0.0 copy-start.2
  1.7 0.0 copy-start.4
  1.8 1.1 %choose.1 = bf16[64,2048]{1,0:T(8,128)(2,1)S(1)} custom-call(bf16[64,2048]{1,0:T(8,128)(2,1)} %bitcast.26, bf16[64,4096]{1,0:T(8,128)(2,1)} %head.1), custom_call_target="tpu_custom_call" | custom-call | flops 7516192768 | bytes 262144 | tf_op jit(solution)/shard_map/choose/pallas_call | solution.py:78
  2.9 5.5 %collective-permute-start.9 = (bf16[64,2048]{1,0:T(8,128)(2,1)S(1)}, bf16[64,2048]{1,0:T(8,128)(2,1)S(1)}, u32[]{:S(2)}, u32[]{:S(2)}) collective-permute-start(bf16[64,2048]{1,0:T(8,128)(2,1)S(1)} %choose.1), channel_id=1, source_target_pairs={{8,2},{9,3},{10,0},{11,1},{12,6},{13,7},{14,4},{15,5},{16,10},{17,... | collective-permute-start | bytes 786440 | tf_op jit(solution)/shard_map/ppermute | solution.py:343
  8.4 0.0 collective-permute-done.2.at
  8.4 0.0 collective-permute-done.xt
  8.4 0.0 collective-permute-done.1.yt
  8.4 0.0 slice-done
  8.4 0.0 slice-done.1
  8.4 0.0 slice-done.2
  8.4 0.0 slice-done.3
  8.5 0.0 copy-done
  8.5 0.0 copy-done.1
  8.5 0.0 copy-done.2
  8.5 0.0 copy-done.4
  8.5 5.7 %shard_map.137 = (f32[64,2048]{1,0:T(8,128)S(1)}, bf16[64,2048]{1,0:T(8,128)(2,1)S(1)}, bf16[64,2048]{1,0:T(8,128)(2,1)S(1)}, bf16[64,2048]{1,0:T(8,128)(2,1)S(1...) custom-call(bf16[128,3584]{1,0:T(8,128)(2,1)S(1)} %bitcast.17, ...), custom_call_target="tpu_custom_call" | custom-call | flops 3758096384 | bytes 14680064 | tf_op jit(solution)/shard_map/pallas_call | solution.py:44
  14.2 1.7 %collective-permute-start.11 = (f32[24,256]{1,0:T(8,128)S(1)}, f32[24,256]{1,0:T(8,128)S(1)}, u32[]{:S(2)}, u32[]{:S(2)}) collective-permute-start(f32[24,256]{1,0:T(8,128)S(1)} %get-tuple-element.29.one.pack), channel_id=1, source_target_pairs={{0,1},{1,0},{2,3},{3,2},{4,5},{5,4},{6,7},{7,6},{8,9},{9,8},{10,11... | collective-permute-start | bytes 73736 | tf_op jit(solution)/shard_map/ppermute | solution.py:335
  15.8 2.3 %collective-permute-start.8 = (bf16[64,2048]{1,0:T(8,128)(2,1)S(1)}, bf16[64,2048]{1,0:T(8,128)(2,1)S(1)}, u32[]{:S(2)}, u32[]{:S(2)}) collective-permute-start(bf16[64,2048]{1,0:T(8,128)(2,1)S(1)} %choose.1), channel_id=1, source_target_pairs={{8,1},{9,0},{10,3},{11,2},{12,5},{13,4},{14,7},{15,6},{16,9},{17,8... | collective-permute-start | bytes 786440 | tf_op jit(solution)/shard_map/ppermute | solution.py:343
  18.2 0.5 collective-permute-start.7
  18.7 1.4 %collective-permute-done.9.refs_2_ = bf16[64,2048]{1,0:T(8,128)(2,1)S(1)} collective-permute-done((bf16[64,2048]{1,0:T(8,128)(2,1)S(1)}, bf16[64,2048]{1,0:T(8,128)(2,1)S(1)}, u32[]{:S(2)}, u32[]{:S(2)}) %collective-permute-start.9) | collective-permute-done | bytes 262176 | tf_op jit(solution)/shard_map/ppermute | solution.py:343
  20.1 1.6 %collective-permute-start.10 = (bf16[64,2048]{1,0:T(8,128)(2,1)S(1)}, bf16[64,2048]{1,0:T(8,128)(2,1)S(1)}, u32[]{:S(2)}, u32[]{:S(2)}) collective-permute-start(bf16[64,2048]{1,0:T(8,128)(2,1)S(1)} %collective-permute-done.9.refs_2_), channel_id=1, source_target_pairs={{0,1},{1,0},{2,3},{3,2},{4,5},{5,4},{6,7},{7,6},{8,9},{9,8},{10,11... | collective-permute-start | bytes 786440 | tf_op jit(solution)/shard_map/ppermute | solution.py:335
  21.7 0.0 collective-permute-done.11.two
  21.7 2.5 %collective-permute-start.12 = (f32[24,256]{1,0:T(8,128)S(1)}, f32[24,256]{1,0:T(8,128)S(1)}, u32[]{:S(2)}, u32[]{:S(2)}) collective-permute-start(f32[24,256]{1,0:T(8,128)S(1)} %shard_map.138.refs_4_), channel_id=1, source_target_pairs={{0,2},{1,3},{2,0},{3,1},{4,6},{5,7},{6,4},{7,5},{8,10},{9,11},{10,... | collective-permute-start | bytes 73736 | tf_op jit(solution)/shard_map/ppermute | solution.py:335
  24.2 4.4 %shard_map.139.refs_7_ = f32[256,2048]{1,0:T(8,128)S(1)} custom-call(bf16[256,3584]{1,0:T(8,128)(2,1)S(1)} %get-tuple-element.30.ys.refs_9_, f32[24,256]{1,0:T(8,128)S(1)} %get-tuple-element.29.one.pack, bf16[16,2048]{1,0:T(8,128)(2,1)S(1)} %bitcast.21, bf16[3584,2048]{1,0:T(8,128)(2,1)S(1)} %bitcast.14), custom_call_target="tpu_custom_call" | custom-call | flops 3758096384 | bytes 14680064 | tf_op jit(solution)/shard_map/pallas_call | solution.py:44
  28.6 0.0 collective-permute-done.8.refs_1_
  28.6 3.1 %collective-permute-done.7.refs_0_ = bf16[64,2048]{1,0:T(8,128)(2,1)S(1)} collective-permute-done((bf16[64,2048]{1,0:T(8,128)(2,1)S(1)}, bf16[64,2048]{1,0:T(8,128)(2,1)S(1)}, u32[]{:S(2)}, u32[]{:S(2)}) %collective-permute-start.7) | collective-permute-done | bytes 262176 | tf_op jit(solution)/shard_map/ppermute | solution.py:343
  31.7 1.5 %collective-permute-done.10.refs_3_ = bf16[64,2048]{1,0:T(8,128)(2,1)S(1)} collective-permute-done((bf16[64,2048]{1,0:T(8,128)(2,1)S(1)}, bf16[64,2048]{1,0:T(8,128)(2,1)S(1)}, u32[]{:S(2)}, u32[]{:S(2)}) %collective-permute-start.10) | collective-permute-done | bytes 262176 | tf_op jit(solution)/shard_map/ppermute | solution.py:335
  33.3 0.0 collective-permute-done.12.refs_5_
  33.3 0.0 copy-done.5
  33.3 1.1 %shard_map.140 = (bf16[256,2048]{1,0:T(8,128)(2,1)S(1)}, bf16[256,32]{1,0:T(8,128)(2,1)S(1)}, f32[256,16]{1,0:T(8,128)S(1)}, bf16[16,256]{1,0:T(8,128)(2,1)S(1)}...) custom-call(bf16[64,2048]{1,0:T(8,128)(2,1)S(1)} %collective-permute-done.7.refs_0_, ...), custom_call_target="tpu_custom_call" | custom-call | bytes 4194304 | tf_op jit(solution)/shard_map/pallas_call | solution.py:44
  34.4 0.0 copy-start.6
  34.4 0.0 copy-start.3
  34.4 4.4 %shard_map.142 = (f32[128,3584]{1,0:T(8,128)S(1)}, bf16[128,3584]{1,0:T(8,128)(2,1)S(1)}) custom-call(bf16[256,2048]{1,0:T(8,128)(2,1)S(1)} %get-tuple-element.34.refs_11_.sc, bf16[256,32]{1,0:T(8,128)(2,1)S(1)} %get-tuple-element.36.ad, bf16[16,3584]{1,0:T(8,128)(2,1)S(1)} %get-tuple-element.37.fac, bf16[3584,2048]{1,0:T(8,128)(2,1)S(1)} %bitcast.15), custom_call_target="tpu_custom_call" | custom-call | flops 3758096384 | bytes 14680064 | tf_op jit(solution)/shard_map/pallas_call | solution.py:44
  38.8 0.1 collective-permute-start.14
  39.0 0.0 copy-done.6
  39.0 0.5 collective-permute-start.6
  39.4 1.2 %collective-permute-start.3 = (bf16[64,2048]{1,0:T(8,128)(2,1)S(1)}, bf16[64,2048]{1,0:T(8,128)(2,1)S(1)}, u32[]{:S(2)}, u32[]{:S(2)}) collective-permute-start(bf16[64,2048]{1,0:T(8,128)(2,1)S(1)} %get-tuple-element.26), channel_id=1, source_target_pairs={{0,1},{1,0},{2,3},{3,2},{4,5},{5,4},{6,7},{7,6},{8,9},{9,8},{10,11... | collective-permute-start | bytes 786440 | tf_op jit(solution)/shard_map/ppermute | solution.py:335
  40.7 2.8 %collective-permute-start.4 = (bf16[64,2048]{1,0:T(8,128)(2,1)S(1)}, bf16[64,2048]{1,0:T(8,128)(2,1)S(1)}, u32[]{:S(2)}, u32[]{:S(2)}) collective-permute-start(bf16[64,2048]{1,0:T(8,128)(2,1)S(1)} %get-tuple-element.27), channel_id=1, source_target_pairs={{0,2},{1,3},{2,0},{3,1},{4,6},{5,7},{6,4},{7,5},{8,10},{9,11},{10,... | collective-permute-start | bytes 786440 | tf_op jit(solution)/shard_map/ppermute | solution.py:335
  43.5 0.3 collective-permute-start.5
  43.8 4.7 %collective-permute-done.6.refs_4_ = bf16[64,2048]{1,0:T(8,128)(2,1)S(1)} collective-permute-done((bf16[64,2048]{1,0:T(8,128)(2,1)S(1)}, bf16[64,2048]{1,0:T(8,128)(2,1)S(1)}, u32[]{:S(2)}, u32[]{:S(2)}) %collective-permute-start.6) | collective-permute-done | bytes 262176 | tf_op jit(solution)/shard_map/ppermute | solution.py:351
  48.5 0.0 collective-permute-start.13
  48.5 1.3 %collective-permute-done.13.refs_8_ = f32[256,16]{1,0:T(8,128)S(1)} collective-permute-done((f32[256,16]{1,0:T(8,128)S(1)}, f32[256,16]{1,0:T(8,128)S(1)}, u32[]{:S(2)}, u32[]{:S(2)}) %collective-permute-start.13) | collective-permute-done | bytes 16416 | tf_op jit(solution)/shard_map/ppermute | solution.py:332
  49.9 3.5 %collective-permute-start.17 = (f32[8,256]{1,0:T(8,128)S(1)}, f32[8,256]{1,0:T(8,128)S(1)}, u32[]{:S(2)}, u32[]{:S(2)}) collective-permute-start(f32[8,256]{1,0:T(8,128)S(1)} %get-tuple-element.40.refs_2_), channel_id=1, source_target_pairs={{0,3},{1,2},{2,1},{3,0},{4,7},{5,6},{6,5},{7,4},{8,11},{9,10},{10,... | collective-permute-start | bytes 24584 | tf_op jit(solution)/shard_map/ppermute | solution.py:335
  53.4 0.0 collective-permute-done.3.refs_1_
  53.4 0.5 collective-permute-start.16
  53.9 8.5 %collective-permute-done.4.refs_2_ = bf16[64,2048]{1,0:T(8,128)(2,1)S(1)} collective-permute-done((bf16[64,2048]{1,0:T(8,128)(2,1)S(1)}, bf16[64,2048]{1,0:T(8,128)(2,1)S(1)}, u32[]{:S(2)}, u32[]{:S(2)}) %collective-permute-start.4) | collective-permute-done | bytes 262176 | tf_op jit(solution)/shard_map/ppermute | solution.py:335
  62.4 0.0 collective-permute-start.15
  62.4 0.0 collective-permute-done.5.refs_3_
  62.4 0.0 copy-done.3
  62.4 1.6 %shard_map.141 = (bf16[64,2048]{1,0:T(8,128)(2,1)}, f32[8,3584]{1,0:T(8,128)}, f32[16,2048]{1,0:T(8,128)}) custom-call(f32[64,2048]{1,0:T(8,128)S(1)} %get-tuple-element.25.refs_0_, bf16[64,2048]{1,0:T(8,128)(2,1)S(1)} %collective-permute-done.3.refs_1_, bf16[64,2048]{1,0:T(8,128)(2,1)S(1)} %collective-permute-done.4.refs_2_, ...), custom_call_target="tpu_custom_call" | custom-call | bytes 2097152 | tf_op jit(solution)/shard_map/pallas_call | solution.py:44
  64.0 0.0 collective-permute-done.17.refs_5_
  64.0 3.5 %collective-permute-done.16.refs_4_ = f32[8,256]{1,0:T(8,128)S(1)} collective-permute-done((f32[8,256]{1,0:T(8,128)S(1)}, f32[8,256]{1,0:T(8,128)S(1)}, u32[]{:S(2)}, u32[]{:S(2)}) %collective-permute-start.16) | collective-permute-done | bytes 8224 | tf_op jit(solution)/shard_map/ppermute | solution.py:335
  67.5 0.0 collective-permute-done.15.refs_3_
  67.5 0.0 collective-permute-done.14.refs_1_
  67.5 1.1 %shard_map.143 = (bf16[128,3584]{1,0:T(8,128)(2,1)}, f32[1,2048]{1,0:T(1,128)}) custom-call(f32[128,3584]{1,0:T(8,128)S(1)} %get-tuple-element.38.refs_0_, bf16[128,3584]{1,0:T(8,128)(2,1)S(1)} %collective-permute-done.14.refs_1_, f32[8,256]{1,0:T(8,128)S(1)} %get-tuple-element.40.refs_2_, f32[8,256]{1,0:T(8,128)S(1)} %collective-permute-done.15.refs_3_, ...), custom_call_target="tpu_custom_call" | custom-call | bytes 5505024 | tf_op jit(solution)/shard_map/pallas_call | solution.py:44
  (3 shorter events, 0.0 us)
Async XLA Ops:
  0.6 7.8 %collective-permute-start = (bf16[128,3584]{1,0:T(8,128)(2,1)}, bf16[128,3584]{1,0:T(8,128)(2,1)S(1)}, u32[]{:S(2)}, u32[]{:S(2)}) collective-permute-start(bf16[128,3584]{1,0:T(8,128)(2,1)} %bitcast.16), channel_id=1, source_target_pairs={{0,4},{4,0},{8,12},{12,8},{16,20},{20,16},{24,28},{28,24},{1,5},{5... | collective-permute-start | bytes 2752520 | tf_op jit(solution)/shard_map/ppermute | solution.py:332
  1.2 7.2 %collective-permute-start.1 = (bf16[128,3584]{1,0:T(8,128)(2,1)}, bf16[128,3584]{1,0:T(8,128)(2,1)S(1)}, u32[]{:S(2)}, u32[]{:S(2)}) collective-permute-start(bf16[128,3584]{1,0:T(8,128)(2,1)} %bitcast.18), channel_id=1, source_target_pairs={{0,4},{4,0},{8,12},{12,8},{16,20},{20,16},{24,28},{28,24},{1,5},{5... | collective-permute-start | bytes 2752520 | tf_op jit(solution)/shard_map/ppermute | solution.py:332
  1.3 7.1 %collective-permute-start.2 = (bf16[8,3584]{1,0:T(8,128)(2,1)}, bf16[8,3584]{1,0:T(8,128)(2,1)S(1)}, u32[]{:S(2)}, u32[]{:S(2)}) collective-permute-start(bf16[8,3584]{1,0:T(8,128)(2,1)} %bitcast.23), channel_id=1, source_target_pairs={{0,4},{4,0},{8,12},{12,8},{16,20},{20,16},{24,28},{28,24},{1,5},{5... | collective-permute-start | bytes 172040 | tf_op jit(solution)/shard_map/ppermute | solution.py:332
  1.7 6.7 %slice-start = ((s8[14680064]{0:T(1024)(128)(4,1)}), s8[4194304]{0:T(1024)(128)(4,1)S(1)}, s32[]{:S(2)}) async-start(s8[14680064]{0:T(1024)(128)(4,1)} %bitcast.11), calls=%async_computation | async-start | bytes 8388608
  1.7 6.7 %slice-start.1 = ((s8[14680064]{0:T(1024)(128)(4,1)}), s8[4194304]{0:T(1024)(128)(4,1)S(1)}, s32[]{:S(2)}) async-start(s8[14680064]{0:T(1024)(128)(4,1)} %bitcast.11), calls=%async_computation.1 | async-start | bytes 8388608
  1.7 6.7 %slice-start.2 = ((s8[14680064]{0:T(1024)(128)(4,1)}), s8[4194304]{0:T(1024)(128)(4,1)S(1)}, s32[]{:S(2)}) async-start(s8[14680064]{0:T(1024)(128)(4,1)} %bitcast.11), calls=%async_computation.2 | async-start | bytes 8388608
  1.7 6.7 %slice-start.3 = ((s8[14680064]{0:T(1024)(128)(4,1)}), s8[2097152]{0:T(1024)(128)(4,1)S(1)}, s32[]{:S(2)}) async-start(s8[14680064]{0:T(1024)(128)(4,1)} %bitcast.11), calls=%async_computation.3 | async-start | bytes 4194304
  1.7 6.7 %copy-start = (bf16[1,128,3584]{2,1,0:T(8,128)(2,1)S(1)}, bf16[1,128,3584]{2,1,0:T(8,128)(2,1)}, u32[]{:S(2)}) copy-start(bf16[1,128,3584]{2,1,0:T(8,128)(2,1)} %param.14) | copy-start | bytes 2752516
  1.7 6.7 %copy-start.1 = (bf16[1,128,3584]{2,1,0:T(8,128)(2,1)S(1)}, bf16[1,128,3584]{2,1,0:T(8,128)(2,1)}, u32[]{:S(2)}) copy-start(bf16[1,128,3584]{2,1,0:T(8,128)(2,1)} %param.17) | copy-start | bytes 2752516
  1.7 6.7 %copy-start.2 = (bf16[1,16,2048]{2,1,0:T(8,128)(2,1)S(1)}, bf16[1,16,2048]{2,1,0:T(8,128)(2,1)}, u32[]{:S(2)}) copy-start(bf16[1,16,2048]{2,1,0:T(8,128)(2,1)} %param.12) | copy-start | bytes 196612
  1.7 6.7 %copy-start.4 = (bf16[1,8,3584]{2,1,0:T(8,128)(2,1)S(1)}, bf16[1,8,3584]{2,1,0:T(8,128)(2,1)}, u32[]{:S(2)}) copy-start(bf16[1,8,3584]{2,1,0:T(8,128)(2,1)} %param.11) | copy-start | bytes 172036
  2.9 17.2 %collective-permute-start.9 = (bf16[64,2048]{1,0:T(8,128)(2,1)S(1)}, bf16[64,2048]{1,0:T(8,128)(2,1)S(1)}, u32[]{:S(2)}, u32[]{:S(2)}) collective-permute-start(bf16[64,2048]{1,0:T(8,128)(2,1)S(1)} %choose.1), channel_id=1, source_target_pairs={{8,2},{9,3},{10,0},{11,1},{12,6},{13,7},{14,4},{15,5},{16,10},{17,... | collective-permute-start | bytes 786440 | tf_op jit(solution)/shard_map/ppermute | solution.py:343
  14.2 7.5 %collective-permute-start.11 = (f32[24,256]{1,0:T(8,128)S(1)}, f32[24,256]{1,0:T(8,128)S(1)}, u32[]{:S(2)}, u32[]{:S(2)}) collective-permute-start(f32[24,256]{1,0:T(8,128)S(1)} %get-tuple-element.29.one.pack), channel_id=1, source_target_pairs={{0,1},{1,0},{2,3},{3,2},{4,5},{5,4},{6,7},{7,6},{8,9},{9,8},{10,11... | collective-permute-start | bytes 73736 | tf_op jit(solution)/shard_map/ppermute | solution.py:335
  15.8 12.8 %collective-permute-start.8 = (bf16[64,2048]{1,0:T(8,128)(2,1)S(1)}, bf16[64,2048]{1,0:T(8,128)(2,1)S(1)}, u32[]{:S(2)}, u32[]{:S(2)}) collective-permute-start(bf16[64,2048]{1,0:T(8,128)(2,1)S(1)} %choose.1), channel_id=1, source_target_pairs={{8,1},{9,0},{10,3},{11,2},{12,5},{13,4},{14,7},{15,6},{16,9},{17,8... | collective-permute-start | bytes 786440 | tf_op jit(solution)/shard_map/ppermute | solution.py:343
  18.2 13.6 %collective-permute-start.7 = (bf16[64,2048]{1,0:T(8,128)(2,1)S(1)}, bf16[64,2048]{1,0:T(8,128)(2,1)S(1)}, u32[]{:S(2)}, u32[]{:S(2)}) collective-permute-start(bf16[64,2048]{1,0:T(8,128)(2,1)S(1)} %choose.1), channel_id=1, source_target_pairs={{8,0},{9,1},{10,2},{11,3},{12,4},{13,5},{14,6},{15,7},{16,8},{17,9... | collective-permute-start | bytes 786440 | tf_op jit(solution)/shard_map/ppermute | solution.py:343
  20.1 13.2 %collective-permute-start.10 = (bf16[64,2048]{1,0:T(8,128)(2,1)S(1)}, bf16[64,2048]{1,0:T(8,128)(2,1)S(1)}, u32[]{:S(2)}, u32[]{:S(2)}) collective-permute-start(bf16[64,2048]{1,0:T(8,128)(2,1)S(1)} %collective-permute-done.9.refs_2_), channel_id=1, source_target_pairs={{0,1},{1,0},{2,3},{3,2},{4,5},{5,4},{6,7},{7,6},{8,9},{9,8},{10,11... | collective-permute-start | bytes 786440 | tf_op jit(solution)/shard_map/ppermute | solution.py:335
  21.7 11.5 %collective-permute-start.12 = (f32[24,256]{1,0:T(8,128)S(1)}, f32[24,256]{1,0:T(8,128)S(1)}, u32[]{:S(2)}, u32[]{:S(2)}) collective-permute-start(f32[24,256]{1,0:T(8,128)S(1)} %shard_map.138.refs_4_), channel_id=1, source_target_pairs={{0,2},{1,3},{2,0},{3,1},{4,6},{5,7},{6,4},{7,5},{8,10},{9,11},{10,... | collective-permute-start | bytes 73736 | tf_op jit(solution)/shard_map/ppermute | solution.py:335
  24.2 9.1 %copy-start.5 = (f32[1,2048]{1,0:T(1,128)S(1)}, f32[1,2048]{1,0:T(1,128)}, u32[]{:S(2)}) copy-start(f32[1,2048]{1,0:T(1,128)} %refs_6_.1) | copy-start | bytes 24580
  34.4 4.5 %copy-start.6 = (bf16[1,64,2048]{2,1,0:T(8,128)(2,1)S(1)}, bf16[1,64,2048]{2,1,0:T(8,128)(2,1)}, u32[]{:S(2)}) copy-start(bf16[1,64,2048]{2,1,0:T(8,128)(2,1)} %param.15) | copy-start | bytes 786436
  34.4 28.0 %copy-start.3 = (bf16[64,4096]{1,0:T(8,128)(2,1)S(1)}, bf16[64,4096]{1,0:T(8,128)(2,1)}, u32[]{:S(2)}) copy-start(bf16[64,4096]{1,0:T(8,128)(2,1)} %refs_5_.1) | copy-start | bytes 1572868
  38.8 28.7 %collective-permute-start.14 = (bf16[128,3584]{1,0:T(8,128)(2,1)S(1)}, bf16[128,3584]{1,0:T(8,128)(2,1)S(1)}, u32[]{:S(2)}, u32[]{:S(2)}) collective-permute-start(bf16[128,3584]{1,0:T(8,128)(2,1)S(1)} %get-tuple-element.39), channel_id=1, source_target_pairs={{0,4},{4,0},{8,12},{12,8},{16,20},{20,16},{24,28},{28,24},{1,5},{5... | collective-permute-start | bytes 2752520 | tf_op jit(solution)/shard_map/ppermute | solution.py:332
  39.0 9.6 %collective-permute-start.6 = (bf16[64,2048]{1,0:T(8,128)(2,1)S(1)}, bf16[64,2048]{1,0:T(8,128)(2,1)S(1)}, u32[]{:S(2)}, u32[]{:S(2)}) collective-permute-start(bf16[64,2048]{1,0:T(8,128)(2,1)S(1)} %bitcast.27), channel_id=1, source_target_pairs={{0,8},{4,12},{8,16},{12,20},{16,24},{20,28},{24,0},{28,4},{1,9},{5... | collective-permute-start | bytes 786440 | tf_op jit(solution)/shard_map/ppermute | solution.py:351
  39.4 13.9 %collective-permute-start.3 = (bf16[64,2048]{1,0:T(8,128)(2,1)S(1)}, bf16[64,2048]{1,0:T(8,128)(2,1)S(1)}, u32[]{:S(2)}, u32[]{:S(2)}) collective-permute-start(bf16[64,2048]{1,0:T(8,128)(2,1)S(1)} %get-tuple-element.26), channel_id=1, source_target_pairs={{0,1},{1,0},{2,3},{3,2},{4,5},{5,4},{6,7},{7,6},{8,9},{9,8},{10,11... | collective-permute-start | bytes 786440 | tf_op jit(solution)/shard_map/ppermute | solution.py:335
  40.7 21.7 %collective-permute-start.4 = (bf16[64,2048]{1,0:T(8,128)(2,1)S(1)}, bf16[64,2048]{1,0:T(8,128)(2,1)S(1)}, u32[]{:S(2)}, u32[]{:S(2)}) collective-permute-start(bf16[64,2048]{1,0:T(8,128)(2,1)S(1)} %get-tuple-element.27), channel_id=1, source_target_pairs={{0,2},{1,3},{2,0},{3,1},{4,6},{5,7},{6,4},{7,5},{8,10},{9,11},{10,... | collective-permute-start | bytes 786440 | tf_op jit(solution)/shard_map/ppermute | solution.py:335
  43.5 18.9 %collective-permute-start.5 = (bf16[64,2048]{1,0:T(8,128)(2,1)S(1)}, bf16[64,2048]{1,0:T(8,128)(2,1)S(1)}, u32[]{:S(2)}, u32[]{:S(2)}) collective-permute-start(bf16[64,2048]{1,0:T(8,128)(2,1)S(1)} %get-tuple-element.28), channel_id=1, source_target_pairs={{0,3},{1,2},{2,1},{3,0},{4,7},{5,6},{6,5},{7,4},{8,11},{9,10},{10,... | collective-permute-start | bytes 786440 | tf_op jit(solution)/shard_map/ppermute | solution.py:335
  48.5 1.3 %collective-permute-start.13 = (f32[256,16]{1,0:T(8,128)S(1)}, f32[256,16]{1,0:T(8,128)S(1)}, u32[]{:S(2)}, u32[]{:S(2)}) collective-permute-start(f32[256,16]{1,0:T(8,128)S(1)} %get-tuple-element.32.refs_7_), channel_id=1, source_target_pairs={{0,4},{4,0},{8,12},{12,8},{16,20},{20,16},{24,28},{28,24},{1,5},{5... | collective-permute-start | bytes 49160 | tf_op jit(solution)/shard_map/ppermute | solution.py:332
  49.9 14.1 %collective-permute-start.17 = (f32[8,256]{1,0:T(8,128)S(1)}, f32[8,256]{1,0:T(8,128)S(1)}, u32[]{:S(2)}, u32[]{:S(2)}) collective-permute-start(f32[8,256]{1,0:T(8,128)S(1)} %get-tuple-element.40.refs_2_), channel_id=1, source_target_pairs={{0,3},{1,2},{2,1},{3,0},{4,7},{5,6},{6,5},{7,4},{8,11},{9,10},{10,... | collective-permute-start | bytes 24584 | tf_op jit(solution)/shard_map/ppermute | solution.py:335
  53.4 14.1 %collective-permute-start.16 = (f32[8,256]{1,0:T(8,128)S(1)}, f32[8,256]{1,0:T(8,128)S(1)}, u32[]{:S(2)}, u32[]{:S(2)}) collective-permute-start(f32[8,256]{1,0:T(8,128)S(1)} %get-tuple-element.40.refs_2_), channel_id=1, source_target_pairs={{0,2},{1,3},{2,0},{3,1},{4,6},{5,7},{6,4},{7,5},{8,10},{9,11},{10,... | collective-permute-start | bytes 24584 | tf_op jit(solution)/shard_map/ppermute | solution.py:335
  62.4 5.1 %collective-permute-start.15 = (f32[8,256]{1,0:T(8,128)S(1)}, f32[8,256]{1,0:T(8,128)S(1)}, u32[]{:S(2)}, u32[]{:S(2)}) collective-permute-start(f32[8,256]{1,0:T(8,128)S(1)} %get-tuple-element.40.refs_2_), channel_id=1, source_target_pairs={{0,1},{1,0},{2,3},{3,2},{4,5},{5,4},{6,7},{7,6},{8,9},{9,8},{10,11... | collective-permute-start | bytes 24584 | tf_op jit(solution)/shard_map/ppermute | solution.py:335

commit v5 on v3

--- a/solution.py
+++ b/solution.py
@@ -181,7 +181,7 @@
 def prepare_kernel(count, rows, *refs):
     cots = refs[:count]
     packs, mag, r, b = refs[count : count + 2], *refs[count + 2 : count + 5]
-    sc, ad, adapt, gb, magpack, norms = refs[count + 5 :]
+    sc, ad, adapt, low, magpack, norms = refs[count + 5 :]
     half = lax.axis_index("section") % 2
     me = lax.axis_index("tensor")
     rank = b.shape[0]
@@ -207,7 +207,7 @@
     part = dot(sc[...], b[...], NT)
     adapt[...] = part
     ad[...] = two_parts(part)
-    gb[...] = dot(total[lines:].astype(bf16), sc[...])
+    low[...] = total[lines:].astype(bf16)
 
 
 def prepare(count, rows, cots, packs, mag, r, b):
@@ -221,7 +221,7 @@
             shaped((tokens, width), bf16),
             shaped((tokens, 2 * rank), bf16),
             shaped((tokens, rank), f32),
-            shaped((rank, width), f32),
+            shaped((rank, tokens), bf16),
             shaped((width // tokens, tokens), f32),
             shaped((2, width), f32),
         ],
@@ -252,9 +252,31 @@
     )
 
 
+def adapters_kernel(adapt, got_adapt, ys, low, sc, ga, gb):
+    half = lax.axis_index("section") % 2
+    tokens, rank = adapt.shape
+    ht, hr = tokens // 2, rank // 2
+    first = adapt[:ht, :] + got_adapt[ht:, :]
+    second = adapt[ht:, :] + got_adapt[:ht, :]
+    cot = jnp.concatenate([first, second], axis=0)
+    cot = jnp.where(half == 0, cot[:, :hr], cot[:, hr:]).astype(bf16)
+    ga[...] = dot(cot, ys[...], TN)
+    gb[...] = dot(low[...], sc[...])
+
+
+def adapters(adapt, got_adapt, ys, low, sc):
+    rank = adapt.shape[1]
+    return whole_call(
+        adapters_kernel,
+        (adapt, got_adapt, ys, low, sc),
+        [shaped((rank // 2, ys.shape[1]), f32), shaped((rank, sc.shape[1]), f32)],
+        moved=2 * ys.size,
+    )
+
+
 def emit_kernel(count, *refs):
     parts = refs[:count]
-    carried, embedded, norms, adapt, got_adapt, ys, out, ga = refs[count:]
+    carried, embedded, norms, out = refs[count:]
     slot = lax.axis_index("section")
     half = slot % 2
     width = out.shape[1]
@@ -264,22 +286,15 @@
     for k in range(1, count):
         total = total + parts[k][...].astype(f32)
     out[...] = (inflow + total * norms[1:2, :]).astype(bf16)
-    tokens, rank = adapt.shape
-    ht, hr = tokens // 2, rank // 2
-    first = adapt[:ht, :] + got_adapt[ht:, :]
-    second = adapt[ht:, :] + got_adapt[:ht, :]
-    cot = jnp.concatenate([first, second], axis=0)
-    cot = jnp.where(half == 0, cot[:, :hr], cot[:, hr:]).astype(bf16)
-    ga[...] = dot(cot, ys[...], TN)
-
-
-def emit(count, parts, carried, embedded, norms, adapt, got_adapt, ys):
+
+
+def emit(count, parts, carried, embedded, norms):
     return whole_call(
         functools.partial(emit_kernel, count),
-        (*parts, carried, embedded, norms, adapt, got_adapt, ys),
-        [shaped(carried.shape, bf16), shaped((adapt.shape[1] // 2, ys.shape[1]), f32)],
+        (*parts, carried, embedded, norms),
+        [shaped(carried.shape, bf16)],
         moved=8 * carried.size * 2,
-    )
+    )[0]
 
 
 def finish_kernel(count, *refs):
@@ -352,7 +367,7 @@
     for k in (2**n for n in range(1, count.bit_length() - 1)):
         pack = join(pack, got)
         got = across(pack, k)
-    sc, ad, adapt, gb, magpack, norms = prepare(
+    sc, ad, adapt, low, magpack, norms = prepare(
         count, rows, cots, (pack, got), magnitude, r, b
     )
     got_adapt = swap(adapt)
@@ -361,7 +376,8 @@
         mags.append(across(magpack, k))
     own, send = backward(sc, ad, fac, w)
     got = swap(send)
-    out, ga = emit(count, parts, arriving, embedded, norms, adapt, got_adapt, ys)
+    ga, gb = adapters(adapt, got_adapt, ys, low, sc)
+    out = emit(count, parts, arriving, embedded, norms)
     hidden, gm = finish(count, own, got, mags, norms)
     return (out[None], gm, ga[None], gb[None], hidden[None])
 

time: 71.2 us -> 70.5 us (level)
    ppermute x9, waiting for transfers between devices: 15.6 us -> 14.9 us  [across(): return lax.ppermute(array, 'tensor', [(i, i ^ k) for i in range(count)])]
    pallas_call x7 -> x8, Pallas kernels: 18.8 us -> 18.8 us  [whole_call(): pl.pallas_call(body, in_specs=[one] * len(args), out_specs=[one] * len(sh...]
  transfers between devices with their start and end apart: 18 -> 18, of which waited for: 9 -> 9; matrix products, arithmetic and copies ran while one was open for 0% -> 0% of each run, Pallas kernels for 18% -> 19%
where the time goes in v5:
time: 70.5 us; the launch traced here: 70.4 us
  starting transfers between devices  25.4 us (36%)
  waiting for transfers between devices  24.2 us (34%)
  Pallas kernels  20 us (28%)
  between operations  0.82 us (1%)
    pallas_call x8, Pallas kernels, whole_call(): pl.pallas_call(body, in_specs=[one] * len(args), out_specs=[one] * len(sh...  18.8 us
    ppermute x9, starting transfers between devices, across(): return lax.ppermute(array, 'tensor', [(i, i ^ k) for i in range(count)])  15 us
    ppermute x9, waiting for transfers between devices, across(): return lax.ppermute(array, 'tensor', [(i, i ^ k) for i in range(count)])  14.9 us
    ppermute x3, starting transfers between devices, shift(): return lax.ppermute(array, ('section', 'tensor'), pairs)  8.41 us
    ppermute x3, waiting for transfers between devices, shift(): return lax.ppermute(array, ('section', 'tensor'), pairs)  4.08 us
    ppermute x1, waiting for transfers between devices, local(): lax.ppermute(carried[0], 'section', [(i, (i + 2) % slots) for i in range(...  3.83 us
  transfers between devices with their start and end apart: 18, of which 9 were waited for; matrix products, arithmetic and copies ran while one was open for 0% of the time, Pallas kernels for 19%

profile of v5, /device:TPU:0, one launch (start us, length us, event | category | flops | bytes accessed | tf_op | source)
XLA Modules:
  0.0 70.4 jit_solution(17103396250370087692)
XLA Ops:
  0.6 0.6 collective-permute-start
  1.2 0.1 collective-permute-start.1
  1.3 0.4 collective-permute-start.2
  1.7 0.0 slice-start
  1.7 0.0 slice-start.1
  1.7 0.0 slice-start.2
  1.7 0.0 copy-start
  1.7 0.0 copy-start.1
  1.7 0.0 copy-start.2
  1.7 0.0 copy-start.4
  1.8 1.1 %choose.1 = bf16[64,2048]{1,0:T(8,128)(2,1)S(1)} custom-call(bf16[64,2048]{1,0:T(8,128)(2,1)} %bitcast.27, bf16[64,4096]{1,0:T(8,128)(2,1)} %head.1), custom_call_target="tpu_custom_call" | custom-call | flops 7516192768 | bytes 262144 | tf_op jit(solution)/shard_map/choose/pallas_call | solution.py:78
  2.9 5.5 %collective-permute-start.9 = (bf16[64,2048]{1,0:T(8,128)(2,1)S(1)}, bf16[64,2048]{1,0:T(8,128)(2,1)S(1)}, u32[]{:S(2)}, u32[]{:S(2)}) collective-permute-start(bf16[64,2048]{1,0:T(8,128)(2,1)S(1)} %choose.1), channel_id=1, source_target_pairs={{8,2},{9,3},{10,0},{11,1},{12,6},{13,7},{14,4},{15,5},{16,10},{17,... | collective-permute-start | bytes 786440 | tf_op jit(solution)/shard_map/ppermute | solution.py:353
  8.4 0.0 collective-permute-done.2.at
  8.4 0.0 collective-permute-done.xt
  8.4 0.0 collective-permute-done.1.yt
  8.4 0.0 slice-done
  8.4 0.0 slice-done.1
  8.4 0.0 slice-done.2
  8.4 0.0 slice-done.3
  8.5 0.0 copy-done
  8.5 0.0 copy-done.1
  8.5 0.0 copy-done.2
  8.5 0.0 copy-done.4
  8.5 5.7 %shard_map.137 = (f32[64,2048]{1,0:T(8,128)S(1)}, bf16[64,2048]{1,0:T(8,128)(2,1)S(1)}, bf16[64,2048]{1,0:T(8,128)(2,1)S(1)}, bf16[64,2048]{1,0:T(8,128)(2,1)S(1...) custom-call(bf16[128,3584]{1,0:T(8,128)(2,1)S(1)} %bitcast.17, ...), custom_call_target="tpu_custom_call" | custom-call | flops 3758096384 | bytes 14680064 | tf_op jit(solution)/shard_map/pallas_call | solution.py:44
  14.2 1.7 %collective-permute-start.11 = (f32[24,256]{1,0:T(8,128)S(1)}, f32[24,256]{1,0:T(8,128)S(1)}, u32[]{:S(2)}, u32[]{:S(2)}) collective-permute-start(f32[24,256]{1,0:T(8,128)S(1)} %get-tuple-element.28.one.pack), channel_id=1, source_target_pairs={{0,1},{1,0},{2,3},{3,2},{4,5},{5,4},{6,7},{7,6},{8,9},{9,8},{10,11... | collective-permute-start | bytes 73736 | tf_op jit(solution)/shard_map/ppermute | solution.py:345
  15.8 2.5 %collective-permute-start.7 = (bf16[64,2048]{1,0:T(8,128)(2,1)S(1)}, bf16[64,2048]{1,0:T(8,128)(2,1)S(1)}, u32[]{:S(2)}, u32[]{:S(2)}) collective-permute-start(bf16[64,2048]{1,0:T(8,128)(2,1)S(1)} %choose.1), channel_id=1, source_target_pairs={{8,0},{9,1},{10,2},{11,3},{12,4},{13,5},{14,6},{15,7},{16,8},{17,9... | collective-permute-start | bytes 786440 | tf_op jit(solution)/shard_map/ppermute | solution.py:353
  18.3 0.4 collective-permute-start.8
  18.7 1.4 %collective-permute-done.9.refs_2_ = bf16[64,2048]{1,0:T(8,128)(2,1)S(1)} collective-permute-done((bf16[64,2048]{1,0:T(8,128)(2,1)S(1)}, bf16[64,2048]{1,0:T(8,128)(2,1)S(1)}, u32[]{:S(2)}, u32[]{:S(2)}) %collective-permute-start.9) | collective-permute-done | bytes 262176 | tf_op jit(solution)/shard_map/ppermute | solution.py:353
  20.1 1.6 %collective-permute-start.10 = (bf16[64,2048]{1,0:T(8,128)(2,1)S(1)}, bf16[64,2048]{1,0:T(8,128)(2,1)S(1)}, u32[]{:S(2)}, u32[]{:S(2)}) collective-permute-start(bf16[64,2048]{1,0:T(8,128)(2,1)S(1)} %collective-permute-done.9.refs_2_), channel_id=1, source_target_pairs={{0,1},{1,0},{2,3},{3,2},{4,5},{5,4},{6,7},{7,6},{8,9},{9,8},{10,11... | collective-permute-start | bytes 786440 | tf_op jit(solution)/shard_map/ppermute | solution.py:345
  21.7 0.0 collective-permute-done.11.two
  21.7 2.5 %collective-permute-start.12 = (f32[24,256]{1,0:T(8,128)S(1)}, f32[24,256]{1,0:T(8,128)S(1)}, u32[]{:S(2)}, u32[]{:S(2)}) collective-permute-start(f32[24,256]{1,0:T(8,128)S(1)} %shard_map.138.refs_4_), channel_id=1, source_target_pairs={{0,2},{1,3},{2,0},{3,1},{4,6},{5,7},{6,4},{7,5},{8,10},{9,11},{10,... | collective-permute-start | bytes 73736 | tf_op jit(solution)/shard_map/ppermute | solution.py:345
  24.2 4.4 %shard_map.139.refs_7_ = f32[256,2048]{1,0:T(8,128)S(1)} custom-call(bf16[256,3584]{1,0:T(8,128)(2,1)S(1)} %get-tuple-element.29.ys, f32[24,256]{1,0:T(8,128)S(1)} %get-tuple-element.28.one.pack, bf16[16,2048]{1,0:T(8,128)(2,1)S(1)} %bitcast.21, bf16[3584,2048]{1,0:T(8,128)(2,1)S(1)} %bitcast.14), custom_call_target="tpu_custom_call" | custom-call | flops 3758096384 | bytes 14680064 | tf_op jit(solution)/shard_map/pallas_call | solution.py:44
  28.6 2.7 %collective-permute-done.7.refs_0_ = bf16[64,2048]{1,0:T(8,128)(2,1)S(1)} collective-permute-done((bf16[64,2048]{1,0:T(8,128)(2,1)S(1)}, bf16[64,2048]{1,0:T(8,128)(2,1)S(1)}, u32[]{:S(2)}, u32[]{:S(2)}) %collective-permute-start.7) | collective-permute-done | bytes 262176 | tf_op jit(solution)/shard_map/ppermute | solution.py:353
  31.3 0.0 collective-permute-done.8.refs_1_
  31.3 2.0 %collective-permute-done.10.refs_3_ = bf16[64,2048]{1,0:T(8,128)(2,1)S(1)} collective-permute-done((bf16[64,2048]{1,0:T(8,128)(2,1)S(1)}, bf16[64,2048]{1,0:T(8,128)(2,1)S(1)}, u32[]{:S(2)}, u32[]{:S(2)}) %collective-permute-start.10) | collective-permute-done | bytes 262176 | tf_op jit(solution)/shard_map/ppermute | solution.py:345
  33.3 0.0 collective-permute-done.12.refs_5_
  33.3 0.0 copy-done.5
  33.3 1.1 %shard_map.140 = (bf16[256,2048]{1,0:T(8,128)(2,1)S(1)}, bf16[256,32]{1,0:T(8,128)(2,1)S(1)}, f32[256,16]{1,0:T(8,128)S(1)}, bf16[16,256]{1,0:T(8,128)(2,1)S(1)}...) custom-call(bf16[64,2048]{1,0:T(8,128)(2,1)S(1)} %collective-permute-done.7.refs_0_, ...), custom_call_target="tpu_custom_call" | custom-call | bytes 4194304 | tf_op jit(solution)/shard_map/pallas_call | solution.py:44
  34.4 0.0 copy-start.6
  34.4 4.4 %shard_map.142 = (f32[128,3584]{1,0:T(8,128)S(1)}, bf16[128,3584]{1,0:T(8,128)(2,1)S(1)}) custom-call(bf16[256,2048]{1,0:T(8,128)(2,1)S(1)} %get-tuple-element.31.sc, bf16[256,32]{1,0:T(8,128)(2,1)S(1)} %get-tuple-element.32.ad, bf16[16,3584]{1,0:T(8,128)(2,1)S(1)} %get-tuple-element.33.fac, bf16[3584,2048]{1,0:T(8,128)(2,1)S(1)} %bitcast.15), custom_call_target="tpu_custom_call" | custom-call | flops 3758096384 | bytes 14680064 | tf_op jit(solution)/shard_map/pallas_call | solution.py:44
  38.8 0.0 copy-start.3
  38.8 0.1 collective-permute-start.13
  38.9 0.0 copy-done.6
  38.9 0.8 %collective-permute-start.6 = (bf16[64,2048]{1,0:T(8,128)(2,1)S(1)}, bf16[64,2048]{1,0:T(8,128)(2,1)S(1)}, u32[]{:S(2)}, u32[]{:S(2)}) collective-permute-start(bf16[64,2048]{1,0:T(8,128)(2,1)S(1)} %bitcast.28), channel_id=1, source_target_pairs={{0,8},{4,12},{8,16},{12,20},{16,24},{20,28},{24,0},{28,4},{1,9},{5... | collective-permute-start | bytes 786440 | tf_op jit(solution)/shard_map/ppermute | solution.py:361
  39.8 2.6 %collective-permute-start.3 = (bf16[64,2048]{1,0:T(8,128)(2,1)S(1)}, bf16[64,2048]{1,0:T(8,128)(2,1)S(1)}, u32[]{:S(2)}, u32[]{:S(2)}) collective-permute-start(bf16[64,2048]{1,0:T(8,128)(2,1)S(1)} %get-tuple-element.25), channel_id=1, source_target_pairs={{0,1},{1,0},{2,3},{3,2},{4,5},{5,4},{6,7},{7,6},{8,9},{9,8},{10,11... | collective-permute-start | bytes 786440 | tf_op jit(solution)/shard_map/ppermute | solution.py:345
  42.3 1.1 %collective-permute-start.4 = (bf16[64,2048]{1,0:T(8,128)(2,1)S(1)}, bf16[64,2048]{1,0:T(8,128)(2,1)S(1)}, u32[]{:S(2)}, u32[]{:S(2)}) collective-permute-start(bf16[64,2048]{1,0:T(8,128)(2,1)S(1)} %get-tuple-element.26), channel_id=1, source_target_pairs={{0,2},{1,3},{2,0},{3,1},{4,6},{5,7},{6,4},{7,5},{8,10},{9,11},{10,... | collective-permute-start | bytes 786440 | tf_op jit(solution)/shard_map/ppermute | solution.py:345
  43.4 1.3 %collective-permute-start.5 = (bf16[64,2048]{1,0:T(8,128)(2,1)S(1)}, bf16[64,2048]{1,0:T(8,128)(2,1)S(1)}, u32[]{:S(2)}, u32[]{:S(2)}) collective-permute-start(bf16[64,2048]{1,0:T(8,128)(2,1)S(1)} %get-tuple-element.27), channel_id=1, source_target_pairs={{0,3},{1,2},{2,1},{3,0},{4,7},{5,6},{6,5},{7,4},{8,11},{9,10},{10,... | collective-permute-start | bytes 786440 | tf_op jit(solution)/shard_map/ppermute | solution.py:345
  44.7 3.8 %collective-permute-done.6.refs_4_ = bf16[64,2048]{1,0:T(8,128)(2,1)S(1)} collective-permute-done((bf16[64,2048]{1,0:T(8,128)(2,1)S(1)}, bf16[64,2048]{1,0:T(8,128)(2,1)S(1)}, u32[]{:S(2)}, u32[]{:S(2)}) %collective-permute-start.6) | collective-permute-done | bytes 262176 | tf_op jit(solution)/shard_map/ppermute | solution.py:361
  48.5 0.0 collective-permute-start.17
  48.5 1.3 %collective-permute-done.17.got_adapt = f32[256,16]{1,0:T(8,128)S(1)} collective-permute-done((f32[256,16]{1,0:T(8,128)S(1)}, f32[256,16]{1,0:T(8,128)S(1)}, u32[]{:S(2)}, u32[]{:S(2)}) %collective-permute-start.17) | collective-permute-done | bytes 16416 | tf_op jit(solution)/shard_map/ppermute | solution.py:342
  49.9 1.9 %collective-permute-start.14 = (f32[8,256]{1,0:T(8,128)S(1)}, f32[8,256]{1,0:T(8,128)S(1)}, u32[]{:S(2)}, u32[]{:S(2)}) collective-permute-start(f32[8,256]{1,0:T(8,128)S(1)} %get-tuple-element.36.refs_2_), channel_id=1, source_target_pairs={{0,1},{1,0},{2,3},{3,2},{4,5},{5,4},{6,7},{7,6},{8,9},{9,8},{10,11... | collective-permute-start | bytes 24584 | tf_op jit(solution)/shard_map/ppermute | solution.py:345
  51.7 1.5 %collective-permute-done.3.refs_1_ = bf16[64,2048]{1,0:T(8,128)(2,1)S(1)} collective-permute-done((bf16[64,2048]{1,0:T(8,128)(2,1)S(1)}, bf16[64,2048]{1,0:T(8,128)(2,1)S(1)}, u32[]{:S(2)}, u32[]{:S(2)}) %collective-permute-start.3) | collective-permute-done | bytes 262176 | tf_op jit(solution)/shard_map/ppermute | solution.py:345
  53.3 1.2 %collective-permute-start.15 = (f32[8,256]{1,0:T(8,128)S(1)}, f32[8,256]{1,0:T(8,128)S(1)}, u32[]{:S(2)}, u32[]{:S(2)}) collective-permute-start(f32[8,256]{1,0:T(8,128)S(1)} %get-tuple-element.36.refs_2_), channel_id=1, source_target_pairs={{0,2},{1,3},{2,0},{3,1},{4,6},{5,7},{6,4},{7,5},{8,10},{9,11},{10,... | collective-permute-start | bytes 24584 | tf_op jit(solution)/shard_map/ppermute | solution.py:345
  54.5 9.3 %collective-permute-done.4.refs_2_ = bf16[64,2048]{1,0:T(8,128)(2,1)S(1)} collective-permute-done((bf16[64,2048]{1,0:T(8,128)(2,1)S(1)}, bf16[64,2048]{1,0:T(8,128)(2,1)S(1)}, u32[]{:S(2)}, u32[]{:S(2)}) %collective-permute-start.4) | collective-permute-done | bytes 262176 | tf_op jit(solution)/shard_map/ppermute | solution.py:345
  63.8 1.2 %collective-permute-start.16 = (f32[8,256]{1,0:T(8,128)S(1)}, f32[8,256]{1,0:T(8,128)S(1)}, u32[]{:S(2)}, u32[]{:S(2)}) collective-permute-start(f32[8,256]{1,0:T(8,128)S(1)} %get-tuple-element.36.refs_2_), channel_id=1, source_target_pairs={{0,3},{1,2},{2,1},{3,0},{4,7},{5,6},{6,5},{7,4},{8,11},{9,10},{10,... | collective-permute-start | bytes 24584 | tf_op jit(solution)/shard_map/ppermute | solution.py:345
  65.0 1.2 %shard_map.144 = (f32[8,3584]{1,0:T(8,128)}, f32[16,2048]{1,0:T(8,128)}) custom-call(f32[256,16]{1,0:T(8,128)S(1)} %get-tuple-element.38.adapt, f32[256,16]{1,0:T(8,128)S(1)} %collective-permute-done.17.got_adapt, bf16[256,3584]{1,0:T(8,128)(2,1)S(1)} %get-tuple-element.29.ys, bf16[16,256]{1,0:T(8,128)(2,1)S(1)} %get-tuple-element.39.low, ...), custom_call_target="tpu_custom_call" | custom-call | bytes 1835008 | tf_op jit(solution)/shard_map/pallas_call | solution.py:44
  66.3 0.0 collective-permute-done.5.refs_3_
  66.3 0.0 copy-done.3
  66.3 0.9 %shard_map.141 = bf16[64,2048]{1,0:T(8,128)(2,1)} custom-call(f32[64,2048]{1,0:T(8,128)S(1)} %get-tuple-element.24.refs_0_, bf16[64,2048]{1,0:T(8,128)(2,1)S(1)} %collective-permute-done.3.refs_1_, bf16[64,2048]{1,0:T(8,128)(2,1)S(1)} %collective-permute-done.4.refs_2_, bf16[64,2048]{1,0:T(8,128)(2,1)S(1)} %collective-permute-done.5.refs_3_, ...), custom_call_target="tpu_custom_call" | custom-call | bytes 2097152 | tf_op jit(solution)/shard_map/pallas_call | solution.py:44
  67.2 0.0 collective-permute-done.14.refs_3_
  67.2 1.5 %collective-permute-done.15.refs_4_ = f32[8,256]{1,0:T(8,128)S(1)} collective-permute-done((f32[8,256]{1,0:T(8,128)S(1)}, f32[8,256]{1,0:T(8,128)S(1)}, u32[]{:S(2)}, u32[]{:S(2)}) %collective-permute-start.15) | collective-permute-done | bytes 8224 | tf_op jit(solution)/shard_map/ppermute | solution.py:345
  68.7 0.5 collective-permute-done.16.refs_5_
  69.3 0.0 collective-permute-done.13.refs_1_
  69.3 1.1 %shard_map.143 = (bf16[128,3584]{1,0:T(8,128)(2,1)}, f32[1,2048]{1,0:T(1,128)}) custom-call(f32[128,3584]{1,0:T(8,128)S(1)} %get-tuple-element.34.refs_0_, bf16[128,3584]{1,0:T(8,128)(2,1)S(1)} %collective-permute-done.13.refs_1_, f32[8,256]{1,0:T(8,128)S(1)} %get-tuple-element.36.refs_2_, f32[8,256]{1,0:T(8,128)S(1)} %collective-permute-done.14.refs_3_, ...), custom_call_target="tpu_custom_call" | custom-call | bytes 5505024 | tf_op jit(solution)/shard_map/pallas_call | solution.py:44
  (4 shorter events, 0.0 us)
Async XLA Ops:
  0.6 7.8 %collective-permute-start = (bf16[128,3584]{1,0:T(8,128)(2,1)}, bf16[128,3584]{1,0:T(8,128)(2,1)S(1)}, u32[]{:S(2)}, u32[]{:S(2)}) collective-permute-start(bf16[128,3584]{1,0:T(8,128)(2,1)} %bitcast.16), channel_id=1, source_target_pairs={{0,4},{4,0},{8,12},{12,8},{16,20},{20,16},{24,28},{28,24},{1,5},{5... | collective-permute-start | bytes 2752520 | tf_op jit(solution)/shard_map/ppermute | solution.py:342
  1.2 7.2 %collective-permute-start.1 = (bf16[128,3584]{1,0:T(8,128)(2,1)}, bf16[128,3584]{1,0:T(8,128)(2,1)S(1)}, u32[]{:S(2)}, u32[]{:S(2)}) collective-permute-start(bf16[128,3584]{1,0:T(8,128)(2,1)} %bitcast.18), channel_id=1, source_target_pairs={{0,4},{4,0},{8,12},{12,8},{16,20},{20,16},{24,28},{28,24},{1,5},{5... | collective-permute-start | bytes 2752520 | tf_op jit(solution)/shard_map/ppermute | solution.py:342
  1.3 7.1 %collective-permute-start.2 = (bf16[8,3584]{1,0:T(8,128)(2,1)}, bf16[8,3584]{1,0:T(8,128)(2,1)S(1)}, u32[]{:S(2)}, u32[]{:S(2)}) collective-permute-start(bf16[8,3584]{1,0:T(8,128)(2,1)} %bitcast.23), channel_id=1, source_target_pairs={{0,4},{4,0},{8,12},{12,8},{16,20},{20,16},{24,28},{28,24},{1,5},{5... | collective-permute-start | bytes 172040 | tf_op jit(solution)/shard_map/ppermute | solution.py:342
  1.7 6.7 %slice-start = ((s8[14680064]{0:T(1024)(128)(4,1)}), s8[4194304]{0:T(1024)(128)(4,1)S(1)}, s32[]{:S(2)}) async-start(s8[14680064]{0:T(1024)(128)(4,1)} %bitcast.11), calls=%async_computation | async-start | bytes 8388608
  1.7 6.7 %slice-start.1 = ((s8[14680064]{0:T(1024)(128)(4,1)}), s8[4194304]{0:T(1024)(128)(4,1)S(1)}, s32[]{:S(2)}) async-start(s8[14680064]{0:T(1024)(128)(4,1)} %bitcast.11), calls=%async_computation.1 | async-start | bytes 8388608
  1.7 6.7 %slice-start.2 = ((s8[14680064]{0:T(1024)(128)(4,1)}), s8[4194304]{0:T(1024)(128)(4,1)S(1)}, s32[]{:S(2)}) async-start(s8[14680064]{0:T(1024)(128)(4,1)} %bitcast.11), calls=%async_computation.2 | async-start | bytes 8388608
  1.7 6.7 %slice-start.3 = ((s8[14680064]{0:T(1024)(128)(4,1)}), s8[2097152]{0:T(1024)(128)(4,1)S(1)}, s32[]{:S(2)}) async-start(s8[14680064]{0:T(1024)(128)(4,1)} %bitcast.11), calls=%async_computation.3 | async-start | bytes 4194304
  1.7 6.7 %copy-start = (bf16[1,128,3584]{2,1,0:T(8,128)(2,1)S(1)}, bf16[1,128,3584]{2,1,0:T(8,128)(2,1)}, u32[]{:S(2)}) copy-start(bf16[1,128,3584]{2,1,0:T(8,128)(2,1)} %param.14) | copy-start | bytes 2752516
  1.7 6.7 %copy-start.1 = (bf16[1,128,3584]{2,1,0:T(8,128)(2,1)S(1)}, bf16[1,128,3584]{2,1,0:T(8,128)(2,1)}, u32[]{:S(2)}) copy-start(bf16[1,128,3584]{2,1,0:T(8,128)(2,1)} %param.17) | copy-start | bytes 2752516
  1.7 6.7 %copy-start.2 = (bf16[1,16,2048]{2,1,0:T(8,128)(2,1)S(1)}, bf16[1,16,2048]{2,1,0:T(8,128)(2,1)}, u32[]{:S(2)}) copy-start(bf16[1,16,2048]{2,1,0:T(8,128)(2,1)} %param.12) | copy-start | bytes 196612
  1.7 6.7 %copy-start.4 = (bf16[1,8,3584]{2,1,0:T(8,128)(2,1)S(1)}, bf16[1,8,3584]{2,1,0:T(8,128)(2,1)}, u32[]{:S(2)}) copy-start(bf16[1,8,3584]{2,1,0:T(8,128)(2,1)} %param.11) | copy-start | bytes 172036
  2.9 17.2 %collective-permute-start.9 = (bf16[64,2048]{1,0:T(8,128)(2,1)S(1)}, bf16[64,2048]{1,0:T(8,128)(2,1)S(1)}, u32[]{:S(2)}, u32[]{:S(2)}) collective-permute-start(bf16[64,2048]{1,0:T(8,128)(2,1)S(1)} %choose.1), channel_id=1, source_target_pairs={{8,2},{9,3},{10,0},{11,1},{12,6},{13,7},{14,4},{15,5},{16,10},{17,... | collective-permute-start | bytes 786440 | tf_op jit(solution)/shard_map/ppermute | solution.py:353
  14.2 7.5 %collective-permute-start.11 = (f32[24,256]{1,0:T(8,128)S(1)}, f32[24,256]{1,0:T(8,128)S(1)}, u32[]{:S(2)}, u32[]{:S(2)}) collective-permute-start(f32[24,256]{1,0:T(8,128)S(1)} %get-tuple-element.28.one.pack), channel_id=1, source_target_pairs={{0,1},{1,0},{2,3},{3,2},{4,5},{5,4},{6,7},{7,6},{8,9},{9,8},{10,11... | collective-permute-start | bytes 73736 | tf_op jit(solution)/shard_map/ppermute | solution.py:345
  15.8 15.5 %collective-permute-start.7 = (bf16[64,2048]{1,0:T(8,128)(2,1)S(1)}, bf16[64,2048]{1,0:T(8,128)(2,1)S(1)}, u32[]{:S(2)}, u32[]{:S(2)}) collective-permute-start(bf16[64,2048]{1,0:T(8,128)(2,1)S(1)} %choose.1), channel_id=1, source_target_pairs={{8,0},{9,1},{10,2},{11,3},{12,4},{13,5},{14,6},{15,7},{16,8},{17,9... | collective-permute-start | bytes 786440 | tf_op jit(solution)/shard_map/ppermute | solution.py:353
  18.3 13.0 %collective-permute-start.8 = (bf16[64,2048]{1,0:T(8,128)(2,1)S(1)}, bf16[64,2048]{1,0:T(8,128)(2,1)S(1)}, u32[]{:S(2)}, u32[]{:S(2)}) collective-permute-start(bf16[64,2048]{1,0:T(8,128)(2,1)S(1)} %choose.1), channel_id=1, source_target_pairs={{8,1},{9,0},{10,3},{11,2},{12,5},{13,4},{14,7},{15,6},{16,9},{17,8... | collective-permute-start | bytes 786440 | tf_op jit(solution)/shard_map/ppermute | solution.py:353
  20.1 13.2 %collective-permute-start.10 = (bf16[64,2048]{1,0:T(8,128)(2,1)S(1)}, bf16[64,2048]{1,0:T(8,128)(2,1)S(1)}, u32[]{:S(2)}, u32[]{:S(2)}) collective-permute-start(bf16[64,2048]{1,0:T(8,128)(2,1)S(1)} %collective-permute-done.9.refs_2_), channel_id=1, source_target_pairs={{0,1},{1,0},{2,3},{3,2},{4,5},{5,4},{6,7},{7,6},{8,9},{9,8},{10,11... | collective-permute-start | bytes 786440 | tf_op jit(solution)/shard_map/ppermute | solution.py:345
  21.7 11.5 %collective-permute-start.12 = (f32[24,256]{1,0:T(8,128)S(1)}, f32[24,256]{1,0:T(8,128)S(1)}, u32[]{:S(2)}, u32[]{:S(2)}) collective-permute-start(f32[24,256]{1,0:T(8,128)S(1)} %shard_map.138.refs_4_), channel_id=1, source_target_pairs={{0,2},{1,3},{2,0},{3,1},{4,6},{5,7},{6,4},{7,5},{8,10},{9,11},{10,... | collective-permute-start | bytes 73736 | tf_op jit(solution)/shard_map/ppermute | solution.py:345
  24.2 9.1 %copy-start.5 = (f32[1,2048]{1,0:T(1,128)S(1)}, f32[1,2048]{1,0:T(1,128)}, u32[]{:S(2)}) copy-start(f32[1,2048]{1,0:T(1,128)} %refs_6_.1) | copy-start | bytes 24580
  34.4 4.5 %copy-start.6 = (bf16[1,64,2048]{2,1,0:T(8,128)(2,1)S(1)}, bf16[1,64,2048]{2,1,0:T(8,128)(2,1)}, u32[]{:S(2)}) copy-start(bf16[1,64,2048]{2,1,0:T(8,128)(2,1)} %param.15) | copy-start | bytes 786436
  38.8 27.4 %copy-start.3 = (bf16[64,4096]{1,0:T(8,128)(2,1)S(1)}, bf16[64,4096]{1,0:T(8,128)(2,1)}, u32[]{:S(2)}) copy-start(bf16[64,4096]{1,0:T(8,128)(2,1)} %refs_5_.1) | copy-start | bytes 1572868
  38.8 30.4 %collective-permute-start.13 = (bf16[128,3584]{1,0:T(8,128)(2,1)S(1)}, bf16[128,3584]{1,0:T(8,128)(2,1)S(1)}, u32[]{:S(2)}, u32[]{:S(2)}) collective-permute-start(bf16[128,3584]{1,0:T(8,128)(2,1)S(1)} %get-tuple-element.35), channel_id=1, source_target_pairs={{0,4},{4,0},{8,12},{12,8},{16,20},{20,16},{24,28},{28,24},{1,5},{5... | collective-permute-start | bytes 2752520 | tf_op jit(solution)/shard_map/ppermute | solution.py:342
  38.9 9.6 %collective-permute-start.6 = (bf16[64,2048]{1,0:T(8,128)(2,1)S(1)}, bf16[64,2048]{1,0:T(8,128)(2,1)S(1)}, u32[]{:S(2)}, u32[]{:S(2)}) collective-permute-start(bf16[64,2048]{1,0:T(8,128)(2,1)S(1)} %bitcast.28), channel_id=1, source_target_pairs={{0,8},{4,12},{8,16},{12,20},{16,24},{20,28},{24,0},{28,4},{1,9},{5... | collective-permute-start | bytes 786440 | tf_op jit(solution)/shard_map/ppermute | solution.py:361
  39.8 13.5 %collective-permute-start.3 = (bf16[64,2048]{1,0:T(8,128)(2,1)S(1)}, bf16[64,2048]{1,0:T(8,128)(2,1)S(1)}, u32[]{:S(2)}, u32[]{:S(2)}) collective-permute-start(bf16[64,2048]{1,0:T(8,128)(2,1)S(1)} %get-tuple-element.25), channel_id=1, source_target_pairs={{0,1},{1,0},{2,3},{3,2},{4,5},{5,4},{6,7},{7,6},{8,9},{9,8},{10,11... | collective-permute-start | bytes 786440 | tf_op jit(solution)/shard_map/ppermute | solution.py:345
  42.3 21.5 %collective-permute-start.4 = (bf16[64,2048]{1,0:T(8,128)(2,1)S(1)}, bf16[64,2048]{1,0:T(8,128)(2,1)S(1)}, u32[]{:S(2)}, u32[]{:S(2)}) collective-permute-start(bf16[64,2048]{1,0:T(8,128)(2,1)S(1)} %get-tuple-element.26), channel_id=1, source_target_pairs={{0,2},{1,3},{2,0},{3,1},{4,6},{5,7},{6,4},{7,5},{8,10},{9,11},{10,... | collective-permute-start | bytes 786440 | tf_op jit(solution)/shard_map/ppermute | solution.py:345
  43.4 22.8 %collective-permute-start.5 = (bf16[64,2048]{1,0:T(8,128)(2,1)S(1)}, bf16[64,2048]{1,0:T(8,128)(2,1)S(1)}, u32[]{:S(2)}, u32[]{:S(2)}) collective-permute-start(bf16[64,2048]{1,0:T(8,128)(2,1)S(1)} %get-tuple-element.27), channel_id=1, source_target_pairs={{0,3},{1,2},{2,1},{3,0},{4,7},{5,6},{6,5},{7,4},{8,11},{9,10},{10,... | collective-permute-start | bytes 786440 | tf_op jit(solution)/shard_map/ppermute | solution.py:345
  48.5 1.3 %collective-permute-start.17 = (f32[256,16]{1,0:T(8,128)S(1)}, f32[256,16]{1,0:T(8,128)S(1)}, u32[]{:S(2)}, u32[]{:S(2)}) collective-permute-start(f32[256,16]{1,0:T(8,128)S(1)} %get-tuple-element.38.adapt), channel_id=1, source_target_pairs={{0,4},{4,0},{8,12},{12,8},{16,20},{20,16},{24,28},{28,24},{1,5},{5... | collective-permute-start | bytes 49160 | tf_op jit(solution)/shard_map/ppermute | solution.py:342
  49.9 17.3 %collective-permute-start.14 = (f32[8,256]{1,0:T(8,128)S(1)}, f32[8,256]{1,0:T(8,128)S(1)}, u32[]{:S(2)}, u32[]{:S(2)}) collective-permute-start(f32[8,256]{1,0:T(8,128)S(1)} %get-tuple-element.36.refs_2_), channel_id=1, source_target_pairs={{0,1},{1,0},{2,3},{3,2},{4,5},{5,4},{6,7},{7,6},{8,9},{9,8},{10,11... | collective-permute-start | bytes 24584 | tf_op jit(solution)/shard_map/ppermute | solution.py:345
  53.3 15.5 %collective-permute-start.15 = (f32[8,256]{1,0:T(8,128)S(1)}, f32[8,256]{1,0:T(8,128)S(1)}, u32[]{:S(2)}, u32[]{:S(2)}) collective-permute-start(f32[8,256]{1,0:T(8,128)S(1)} %get-tuple-element.36.refs_2_), channel_id=1, source_target_pairs={{0,2},{1,3},{2,0},{3,1},{4,6},{5,7},{6,4},{7,5},{8,10},{9,11},{10,... | collective-permute-start | bytes 24584 | tf_op jit(solution)/shard_map/ppermute | solution.py:345
  63.8 5.4 %collective-permute-start.16 = (f32[8,256]{1,0:T(8,128)S(1)}, f32[8,256]{1,0:T(8,128)S(1)}, u32[]{:S(2)}, u32[]{:S(2)}) collective-permute-start(f32[8,256]{1,0:T(8,128)S(1)} %get-tuple-element.36.refs_2_), channel_id=1, source_target_pairs={{0,3},{1,2},{2,1},{3,0},{4,7},{5,6},{6,5},{7,4},{8,11},{9,10},{10,... | collective-permute-start | bytes 24584 | tf_op jit(solution)/shard_map/ppermute | solution.py:345
